TPU v7x, 128 devices: a whole 4x4x4 slice. The times are simulated.
128 devices in a mesh: row: 8 (over x, z_hi), col: 16 (over y, z_lo, core).
Axes of the slice: x: 4, y: 4, z: 4 (z_hi: 2, z_lo: 2; z = z_hi * 2 + z_lo), core: 2. Of those that a mesh axis runs over, the one named last changes fastest.
Arguments:
- grad_out: bfloat16 [16, 256, 8192], P('col', 'row'), may hold values from -0.25 to 0.25
- pre_act: bfloat16 [4096, 14336], P('col', 'row'), may hold values from -6 to 6
- down_weight: bfloat16 [8192, 14336], P('col', 'row'), may hold values from -3 to 3
Outputs:
- grad_pre: bfloat16 [4096, 14336], P('col', 'row')
- grad_weight: bfloat16 [8192, 14336], P('col', 'row')
All inputs are finite; a program needn't handle non-finite values.
Results may differ from a plain program's by a relative error of at most 0.0048.
Values may be sent and summed in bfloat16 or wider, within the bound.
No kernel may reach another device: no remote copies, remote signals or barrier semaphores. Data moves between devices by JAX's collectives and lax.ppermute only.
A program may use at most 128 MiB of HBM per device.

v0:
```python
import math

import jax
import jax.numpy as jnp
from jax import lax
from jax.sharding import PartitionSpec as P


def gelu_parts(pre_float):
    cumulative = 0.5 * (1.0 + jax.scipy.special.erf(pre_float / math.sqrt(2.0)))
    density = jnp.exp(-0.5 * pre_float * pre_float) / math.sqrt(2.0 * math.pi)
    return (pre_float * cumulative, cumulative + pre_float * density)


def shards(grad_out, pre_act, down_weight):
    shard_rows = grad_out[0]
    token_block = lax.all_gather(shard_rows, "row", axis=0, tiled=True)
    column_block = lax.all_to_all(token_block, "col", split_axis=1, concat_axis=0, tiled=True)
    activated, slope = gelu_parts(pre_act.astype(jnp.float32))
    hidden = activated.astype(jnp.bfloat16)
    row_slice = column_block
    grad_hidden = lax.psum_scatter(
        jnp.dot(row_slice, down_weight, preferred_element_type=jnp.float32),
        "col",
        scatter_dimension=0,
        tiled=True,
    )
    grad_pre = (grad_hidden * slope).astype(jnp.bfloat16)
    row_slice = column_block
    grad_weight = lax.dot_general(
        row_slice,
        lax.all_gather(hidden, "col", axis=0, tiled=True),
        (((0,), (0,)), ((), ())),
        preferred_element_type=jnp.float32,
    )
    return (grad_pre, grad_weight.astype(jnp.bfloat16))


def solution(mesh):
    in_specs = (P("col", "row", None), P("col", "row"), P("col", "row"))
    out_specs = (P("col", "row"), P("col", "row"))
    return jax.shard_map(shards, mesh=mesh, in_specs=in_specs, out_specs=out_specs, check_vma=False)
```

profile of v0, /device:TPU:0, one launch (start us, length us, event | category | flops | bytes accessed | tf_op | source)
XLA Modules:
  0.0 582.0 jit_solution(2370361156632593929)
XLA Ops:
  7.2 0.0 copy-start
  7.2 0.0 all-gather.6.cloned.1.call-start
  7.2 0.7 all-gather.6.cloned.1.call-update
  7.9 0.0 reduce-scatter.2.cloned.1.call-start
  8.0 76.5 %all-gather.6.cloned.1.call-done = bf16[1,256,8192]{2,1,0:T(8,128)(2,1)} async-done(((bf16[1,32,8192]{2,1,0:T(8,128)(2,1)}), bf16[1,256,8192]{2,1,0:T(8,128)(2,1)}) %all-gather.6.cloned.1.call-update) | async-done | bytes 4194320 | tf_op jit(solution)/shard_map/all_gather | solution.py:17
  84.4 6.4 %copy.10 = bf16[1,256,8192]{1,2,0:T(8,128)(2,1)} copy(bf16[1,256,8192]{2,1,0:T(8,128)(2,1)} %all-gather.6.cloned.1.call-done) | data formatting | bytes 8388608 | tf_op jit(solution)/shard_map/all_gather | solution.py:17
  90.8 54.8 %all_to_all.19 = bf16[256,16,512]{0,2,1:T(8,128)(2,1)} all-to-all(bf16[256,16,512]{0,2,1:T(8,128)(2,1)} %bitcast.9), channel_id=1, replica_groups=mesh['row'=8,'col'=16] {'col'}, dimensions={1} | all-to-all | bytes 8388608 | tf_op jit(solution)/shard_map/all_to_all | solution.py:18
  145.6 6.4 %copy.11 = bf16[16,256,512]{2,1,0:T(8,128)(2,1)} copy(bf16[16,256,512]{1,2,0:T(8,128)(2,1)} %bitcast.10) | data formatting | bytes 8388608 | tf_op jit(solution)/shard_map/all_to_all | solution.py:18
  151.9 0.0 copy-done
  151.9 16.4 %fusion.10 = f32[4096,1792]{1,0:T(8,128)} fusion(bf16[4096,512]{1,0:T(8,128)(2,1)} %bitcast.11, bf16[512,1792]{1,0:T(8,128)(2,1)S(1)} %copy-done), kind=kOutput, calls=%fused_computation.16 | convolution fusion | flops 7516192768 | bytes 35389440 | tf_op jit(solution)/shard_map/dot_general | solution.py:23
  168.3 0.0 copy-start.2
  168.3 0.0 reduce-scatter.2.cloned.1.call-update
  168.4 0.0 all-gather.4.cloned.1.call-start
  168.4 295.9 %reduce-scatter.2.cloned.1.call-done = f32[256,1792]{1,0:T(8,128)} async-done(((f32[4096,1792]{1,0:T(8,128)}), f32[256,1792]{1,0:T(8,128)}) %reduce-scatter.2.cloned.1.call-update) | async-done | bytes 1835024 | tf_op jit(solution)/shard_map/reduce_scatter | solution.py:22
  464.3 0.0 copy-done.2
  464.3 3.6 fusion.9
  467.9 0.0 all-gather.4.cloned.1.call-update
  467.9 90.4 %all-gather.4.cloned.1.call-done = bf16[4096,1792]{1,0:T(8,128)(2,1)} async-done(((bf16[256,1792]{1,0:T(8,128)(2,1)}), bf16[4096,1792]{1,0:T(8,128)(2,1)}) %all-gather.4.cloned.1.call-update) | async-done | bytes 14680080 | tf_op jit(solution)/shard_map/all_gather | solution.py:32
  558.4 0.0 copy-start.1
  558.4 13.3 %fusion = bf16[512,1792]{0,1:T(8,128)(2,1)} fusion(bf16[4096,1792]{1,0:T(8,128)(2,1)} %all-gather.4.cloned.1.call-done, bf16[4096,512]{1,0:T(8,128)(2,1)} %bitcast.12), kind=kOutput, calls=%fused_computation.6 | convolution fusion | flops 7517110272 | bytes 20709376 | tf_op jit(solution)/shard_map/dot_general | solution.py:30
  571.7 3.8 copy.12
  575.5 0.0 copy-done.1
Async XLA Ops:
  7.2 144.8 %copy-start = (bf16[512,1792]{1,0:T(8,128)(2,1)S(1)}, bf16[512,1792]{1,0:T(8,128)(2,1)}, u32[]{:S(2)}) copy-start(bf16[512,1792]{1,0:T(8,128)(2,1)} %param.5) | copy-start | bytes 5505028
  7.2 77.3 %all-gather.6.cloned.1.call-start = ((), (), s32[]{:S(2)}) async-start(), calls=%async_computation.4 | async-start | bytes 4718592 | tf_op jit(solution)/shard_map/all_gather | solution.py:17
  7.9 456.4 %reduce-scatter.2.cloned.1.call-start = ((), (), s32[]{:S(2)}) async-start(), calls=%async_computation.2 | async-start | bytes 31195136 | tf_op jit(solution)/shard_map/reduce_scatter | solution.py:22
  168.3 295.9 %copy-start.2 = (bf16[256,1792]{1,0:T(8,128)(2,1)S(1)}, bf16[256,1792]{1,0:T(8,128)(2,1)}, u32[]{:S(2)}) copy-start(bf16[256,1792]{1,0:T(8,128)(2,1)} %param.4) | copy-start | bytes 2752516
  168.4 390.0 %all-gather.4.cloned.1.call-start = ((), (), s32[]{:S(2)}) async-start(), calls=%async_computation.3 | async-start | bytes 15597568 | tf_op jit(solution)/shard_map/all_gather | solution.py:32
  558.4 17.1 %copy-start.1 = (bf16[512,1792]{1,0:T(8,128)(2,1)S(1)}, bf16[512,1792]{1,0:T(8,128)(2,1)}, u32[]{:S(2)}) copy-start(bf16[512,1792]{1,0:T(8,128)(2,1)} %param.5) | copy-start | bytes 5505028
Sparse Core Ops, SparseCore 0:
  10.4 74.0 all-gather.5
  168.5 295.7 reduce-scatter.1
  468.0 90.2 all-gather.3
where the time goes:
time: 584 us; the launch traced here: 582 us
  waiting for transfers between devices  463 us (79%)
  blocking collectives  54.8 us (9%)
  matrix products  29.8 us (5%)
  local copies, waits for them, and re-layouts  16.5 us (3%)
  between operations  13.8 us (2%)
    reduce_scatter x1, waiting for transfers between devices, shards(): lax.psum_scatter(jnp.dot(row_slice, down_weight, preferred_element_type=j...  296 us
    all_gather x1, waiting for transfers between devices, shards(): lax.all_gather(hidden, 'col', axis=0, tiled=True)  90.4 us
    all_gather x1, waiting for transfers between devices, shards(): token_block = lax.all_gather(shard_rows, 'row', axis=0, tiled=True)  76.5 us
    all_to_all x1, blocking collectives, shards(): lax.all_to_all(token_block, 'col', split_axis=1, concat_axis=0, tiled=True)  54.8 us
    dot_general x1, matrix products, shards(): jnp.dot(row_slice, down_weight, preferred_element_type=jnp.float32)  16.4 us
    dot_general x1, matrix products, shards(): lax.dot_general(row_slice, lax.all_gather(hidden, 'col', axis=0, tiled=Tr...  13.3 us
  transfers between devices with their start and end apart: 3, of which 3 were waited for; matrix products, arithmetic and copies ran while one was open for 0% of the time, Pallas kernels for 0%

commit v1 on v0

v1 whole, which is shorter than its diff:
```python
import math

import jax
import jax.numpy as jnp
from jax import lax
from jax.sharding import Mesh, PartitionSpec as P

NAMES = ("x", "zh", "y", "zl", "core")
SIZES = {"x": 4, "zh": 2, "y": 4, "zl": 2, "core": 2}


def shift(value, axis, by):
    size = SIZES[axis]
    return lax.ppermute(value, axis, [(i, (i + by) % size) for i in range(size)])


def rolled(value, dim, axis):
    size = SIZES[axis]
    at = lax.axis_index(axis)
    if size == 2:
        return jnp.where(at == 0, value, jnp.flip(value, dim))
    return lax.dynamic_slice_in_dim(jnp.concatenate([value, value], dim), at, size, dim)


def unrolled(value, dim, axis):
    size = SIZES[axis]
    at = lax.axis_index(axis)
    if size == 2:
        return jnp.where(at == 0, value, jnp.flip(value, dim))
    return lax.dynamic_slice_in_dim(jnp.concatenate([value, value], dim), (size - at) % size, size, dim)


def gelu_parts(pre_float):
    cumulative = 0.5 * (1.0 + jax.scipy.special.erf(pre_float / math.sqrt(2.0)))
    density = jnp.exp(-0.5 * pre_float * pre_float) / math.sqrt(2.0 * math.pi)
    return (pre_float * cumulative, cumulative + pre_float * density)


def shards(grad_out, pre_act, weight):
    bf16, f32 = jnp.bfloat16, jnp.float32
    rows, width = grad_out.shape[1:]
    tokens, hidden_units = pre_act.shape
    own_rows = weight.shape[0]

    weight_other = shift(weight, "zl", 1)

    pieces = grad_out[0].reshape(rows, 4, 2, 2, own_rows)
    pieces = rolled(rolled(rolled(pieces, 1, "y"), 2, "zl"), 3, "core")
    pieces = pieces.transpose(3, 1, 0, 2, 4).reshape(2, 4, rows, 2 * own_rows)
    pieces = jnp.stack([pieces[0], shift(pieces[1], "core", 1)])
    grad = jnp.stack([pieces[:, 0]] + [shift(pieces[:, -s % 4], "y", -s) for s in (1, 2, 3)], 1)
    grad = jnp.stack([grad, shift(grad, "zh", 1)], 2)
    grad = jnp.stack([grad] + [shift(grad, "x", -s) for s in (1, 2, 3)], 2)
    grad = grad.reshape(8 * tokens, 2 * own_rows)

    pre = pre_act.astype(f32)
    activated, slope = gelu_parts(pre)
    hidden = activated.astype(bf16).reshape(4, 2, rows, hidden_units)
    hidden = rolled(rolled(hidden, 0, "x"), 1, "zh").reshape(tokens, hidden_units)
    hidden = jnp.stack([hidden] + [shift(hidden, "y", -s) for s in (1, 2, 3)])
    hidden = jnp.stack([hidden, shift(hidden, "core", 1)]).reshape(8 * tokens, hidden_units)

    weights = jnp.concatenate([weight, weight_other], 0)
    half = 4 * tokens
    partial_away = jnp.dot(grad[half:], weights, preferred_element_type=f32).astype(bf16)
    partial_away = shift(partial_away, "core", 1)
    partial = jnp.dot(grad[:half], weights, preferred_element_type=f32)
    partial = (partial + partial_away.astype(f32)).reshape(4, tokens, hidden_units)
    total = partial[0]
    for s in (1, 2, 3):
        total = total + shift(partial[s].astype(bf16), "y", s).astype(f32)
    total = unrolled(unrolled(total.reshape(4, 2, rows, hidden_units), 0, "x"), 1, "zh")
    grad_pre = (total.reshape(tokens, hidden_units) * slope).astype(bf16)

    contract = (((0,), (0,)), ((), ()))
    away = lax.dot_general(grad[:, own_rows:], hidden, contract, preferred_element_type=f32).astype(bf16)
    away = shift(away, "zl", 1)
    own = lax.dot_general(grad[:, :own_rows], hidden, contract, preferred_element_type=f32)
    return (grad_pre, (own + away.astype(f32)).astype(bf16))


def solution(mesh):
    sizes = tuple(SIZES[name] for name in NAMES)
    inner = Mesh(mesh.devices.reshape(sizes), NAMES)
    col, row = ("y", "zl", "core"), ("x", "zh")
    in_specs = (P(col, row, None), P(col, row), P(col, row))
    out_specs = (P(col, row), P(col, row))
    return jax.shard_map(shards, mesh=inner, in_specs=in_specs, out_specs=out_specs, check_vma=False)
```

time: 584 us -> 300 us (0.51)
  waiting for transfers between devices: 463 us -> 222 us
  blocking collectives: 54.8 us -> 0 us
  starting transfers between devices: 0.12 us -> 25.4 us
  between operations: 13.8 us -> 0.91 us
  matrix products: 29.8 us -> 21.1 us
  other arithmetic: 3.62 us -> 12.1 us
    reduce_scatter x1 -> x0, waiting for transfers between devices: 296 us -> none  [shards(): lax.psum_scatter(jnp.dot(row_slice, down_weight, preferred_element_type=j...]
    ppermute x0 -> x18, waiting for transfers between devices: none -> 222 us  [shift(): lax.ppermute(value, axis, [(i, (i + by) % size) for i in range(size)])]
    all_gather x2 -> x0, waiting for transfers between devices: 167 us -> none  [the longest x1 90.4 us: shards(): lax.all_gather(hidden, 'col', axis=0, tiled=True)]
    all_to_all x1 -> x0, blocking collectives: 54.8 us -> none  [shards(): lax.all_to_all(token_block, 'col', split_axis=1, concat_axis=0, tiled=True)]
    ppermute x0 -> x18, starting transfers between devices: none -> 25.4 us  [shift(): lax.ppermute(value, axis, [(i, (i + by) % size) for i in range(size)])]
    dot_general x2 -> x4, matrix products: 29.8 us -> 21.1 us  [the longest x1 5.99 us: shards(): partial = jnp.dot(grad[:half], weights, preferred_element_type=f32)]
    all_to_all x1 -> x0, local copies, waits for them, and re-layouts: 6.37 us -> none  [shards(): lax.all_to_all(token_block, 'col', split_axis=1, concat_axis=0, tiled=True)]
    all_gather x1 -> x0, local copies, waits for them, and re-layouts: 6.36 us -> none  [shards(): token_block = lax.all_gather(shard_rows, 'row', axis=0, tiled=True)]
  transfers between devices with their start and end apart: 3 -> 18, of which waited for: 3 -> 13; matrix products, arithmetic and copies ran while one was open for 0% -> 2% of each run, Pallas kernels for 0% -> 0%
where the time goes in v1:
time: 300 us; the launch traced here: 299 us
  waiting for transfers between devices  222 us (74%)
  starting transfers between devices  25.4 us (8%)
  matrix products  21.1 us (7%)
  local copies, waits for them, and re-layouts  17.7 us (6%)
  other arithmetic  12.1 us (4%)
    ppermute x18, waiting for transfers between devices, shift(): lax.ppermute(value, axis, [(i, (i + by) % size) for i in range(size)])  222 us
    ppermute x18, starting transfers between devices, shift(): lax.ppermute(value, axis, [(i, (i + by) % size) for i in range(size)])  25.4 us
  transfers between devices with their start and end apart: 18, of which 13 were waited for; matrix products, arithmetic and copies ran while one was open for 2% of the time, Pallas kernels for 0%

profile of v1, /device:TPU:0, one launch (start us, length us, event | category | flops | bytes accessed | tf_op | source)
XLA Modules:
  0.0 299.1 jit_solution(8437777454186206261)
XLA Ops:
  0.6 1.4 reshape_squeeze.3
  2.5 1.3 fusion.15
  3.8 2.8 rev.16
  6.6 1.4 broadcast_select_fusion
  9.2 2.1 collective-permute-start.8
  11.5 3.1 %collective-permute-start.1 = (bf16[2,32,1024]{2,1,0:T(8,128)(2,1)S(1)}, bf16[2,32,1024]{2,1,0:T(8,128)(2,1)S(1)}, u32[]{:S(2)}, u32[]{:S(2)}) collective-permute-start(bf16[2,32,1024]{2,1,0:T(8,128)(2,1)S(1)} %get-tuple-element.16), channel_id=1, source_target_pairs={{0,12},{4,0},{8,4},{12,8},{1,13},{5,1},{9,5},{13,9},{2,14},{6,2},{... | collective-permute-start | bytes 393224 | tf_op jit(solution)/shard_map/ppermute | solution.py:14
  14.6 0.6 collective-permute-start.2
  15.2 1.0 collective-permute-start.3
  16.2 4.3 %collective-permute-done.1 = bf16[2,32,1024]{2,1,0:T(8,128)(2,1)S(1)} collective-permute-done((bf16[2,32,1024]{2,1,0:T(8,128)(2,1)S(1)}, bf16[2,32,1024]{2,1,0:T(8,128)(2,1)S(1)}, u32[]{:S(2)}, u32[]{:S(2)}) %collective-permute-start.1) | collective-permute-done | bytes 131104 | tf_op jit(solution)/shard_map/ppermute | solution.py:14
  20.4 2.0 collective-permute-done.2
  22.5 1.7 collective-permute-done.3
  24.2 3.7 %collective-permute-start.4 = (bf16[2,4,32,1024]{3,2,0,1:T(8,128)(2,1)S(1)}, bf16[2,4,32,1024]{3,2,0,1:T(8,128)(2,1)S(1)}, u32[]{:S(2)}, u32[]{:S(2)}) collective-permute-start(bf16[2,4,32,1024]{3,2,0,1:T(8,128)(2,1)S(1)} %get-tuple-element.14), channel_id=1, source_target_pairs={{0,16},{16,0},{1,17},{17,1},{2,18},{18,2},{3,19},{19,3},{4,20},{20... | collective-permute-start | bytes 1572872 | tf_op jit(solution)/shard_map/ppermute | solution.py:14
  27.9 38.5 %collective-permute-done.4 = bf16[2,4,32,1024]{3,2,0,1:T(8,128)(2,1)S(1)} collective-permute-done((bf16[2,4,32,1024]{3,2,0,1:T(8,128)(2,1)S(1)}, bf16[2,4,32,1024]{3,2,0,1:T(8,128)(2,1)S(1)}, u32[]{:S(2)}, u32[]{:S(2)}) %collective-permute-start.4) | collective-permute-done | bytes 524320 | tf_op jit(solution)/shard_map/ppermute | solution.py:14
  66.5 2.8 collective-permute-start.5
  69.3 0.8 collective-permute-start.6
  70.1 0.9 collective-permute-start.7
  71.2 1.6 constant_dynamic-update-slice_fusion
  72.8 41.3 %collective-permute-done.5 = bf16[2,4,2,32,1024]{4,3,0,1,2:T(8,128)(2,1)S(1)} collective-permute-done((bf16[2,4,2,32,1024]{4,3,0,1,2:T(8,128)(2,1)S(1)}, bf16[2,4,2,32,1024]{4,3,0,1,2:T(8,128)(2,1)S(1)}, u32[]{:S(2)}, u32[]{:S(2)}) %collective-permute-start.5) | collective-permute-done | bytes 1048608 | tf_op jit(solution)/shard_map/ppermute | solution.py:14
  114.1 3.7 %collective-permute-done.7 = bf16[2,4,2,32,1024]{4,3,0,1,2:T(8,128)(2,1)S(1)} collective-permute-done((bf16[2,4,2,32,1024]{4,3,0,1,2:T(8,128)(2,1)S(1)}, bf16[2,4,2,32,1024]{4,3,0,1,2:T(8,128)(2,1)S(1)}, u32[]{:S(2)}, u32[]{:S(2)}) %collective-permute-start.7) | collective-permute-done | bytes 1048608 | tf_op jit(solution)/shard_map/ppermute | solution.py:14
  117.7 0.5 pad_maximum_fusion.1
  118.3 0.8 fusion.27
  119.1 1.5 copy-done
  120.8 4.2 %convolution_convert_fusion = bf16[1024,1792]{1,0:T(8,128)(2,1)S(1)} fusion(bf16[1024,1024]{1,0:T(8,128)(2,1)S(1)} %bitcast.58, bf16[1024,1792]{1,0:T(8,128)(2,1)S(1)} %constant_dynamic-update-slice_fusion), kind=kOutput, calls=%fused_computation.3 | convolution fusion | flops 3759931392 | bytes 9437184 | tf_op jit(solution)/shard_map/dot_general | solution.py:65
  125.6 6.1 %collective-permute-done.9 = bf16[1024,1792]{1,0:T(8,128)(2,1)S(1)} collective-permute-done((bf16[1024,1792]{1,0:T(8,128)(2,1)S(1)}, bf16[1024,1792]{1,0:T(8,128)(2,1)S(1)}, u32[]{:S(2)}, u32[]{:S(2)}) %collective-permute-start.9) | collective-permute-done | bytes 3670048 | tf_op jit(solution)/shard_map/ppermute | solution.py:14
  131.7 6.0 %fusion.30 = (bf16[1024,1792]{1,0:T(8,128)(2,1)S(1)}, f32[1024,1792]{1,0:T(8,128)}) fusion(bf16[1024,1792]{1,0:T(8,128)(2,1)S(1)} %collective-permute-done.9, bf16[1024,1024]{1,0:T(8,128)(2,1)S(1)} %bitcast.57, bf16[1024,1792]{1,0:T(8,128)(2,1)S(1)} %constant_dynamic-update-slice_fusion), kind=kOutput, calls=%fused_computation.64 | convolution fusion | flops 3763601408 | bytes 20447232 | tf_op jit(solution)/shard_map/dot_general | solution.py:67
  137.7 1.6 fusion.28
  139.3 1.6 collective-permute-start.10
  140.9 2.9 collective-permute-start.11
  143.8 1.3 collective-permute-start.12
  145.1 18.0 %collective-permute-done.10 = bf16[256,1792]{1,0:T(8,128)(2,1)S(1)} collective-permute-done((bf16[256,1792]{1,0:T(8,128)(2,1)}, bf16[256,1792]{1,0:T(8,128)(2,1)S(1)}, u32[]{:S(2)}, u32[]{:S(2)}) %collective-permute-start.10) | collective-permute-done | bytes 917536 | tf_op jit(solution)/shard_map/ppermute | solution.py:14
  163.2 20.8 %collective-permute-done.11 = bf16[256,1792]{1,0:T(8,128)(2,1)S(1)} collective-permute-done((bf16[256,1792]{1,0:T(8,128)(2,1)}, bf16[256,1792]{1,0:T(8,128)(2,1)S(1)}, u32[]{:S(2)}, u32[]{:S(2)}) %collective-permute-start.11) | collective-permute-done | bytes 917536 | tf_op jit(solution)/shard_map/ppermute | solution.py:14
  184.0 1.9 fusion.13
  186.4 0.6 copy-done.5
  187.1 1.8 fusion.10
  189.4 2.1 collective-permute-start.13
  191.5 1.1 collective-permute-start.14
  192.7 0.8 collective-permute-start.15
  193.5 37.6 %collective-permute-done.13 = bf16[256,1792]{1,0:T(8,128)(2,1)S(1)} collective-permute-done((bf16[256,1792]{1,0:T(8,128)(2,1)S(1)}, bf16[256,1792]{1,0:T(8,128)(2,1)S(1)}, u32[]{:S(2)}, u32[]{:S(2)}) %collective-permute-start.13) | collective-permute-done | bytes 917536 | tf_op jit(solution)/shard_map/ppermute | solution.py:14
  231.0 3.4 %collective-permute-done.15 = bf16[256,1792]{1,0:T(8,128)(2,1)S(1)} collective-permute-done((bf16[256,1792]{1,0:T(8,128)(2,1)S(1)}, bf16[256,1792]{1,0:T(8,128)(2,1)S(1)}, u32[]{:S(2)}, u32[]{:S(2)}) %collective-permute-start.15) | collective-permute-done | bytes 917536 | tf_op jit(solution)/shard_map/ppermute | solution.py:14
  234.4 0.6 fusion.26
  235.1 1.5 copy-done.1
  236.6 2.4 copy.14
  239.0 2.5 collective-permute-done.16
  241.5 1.8 copy-done.3
  243.4 2.7 pad_maximum_fusion
  246.1 5.8 %convolution_convert_fusion.1 = bf16[512,1792]{1,0:T(8,128)(2,1)S(1)} fusion(bf16[2048,1792]{1,0:T(8,128)(2,1)S(1)} %bitcast.46, bf16[2048,1024]{1,0:T(8,128)(2,1)} %bitcast.49), kind=kOutput, calls=%fused_computation.13 | convolution fusion | flops 3759013888 | bytes 11272192 | tf_op jit(solution)/shard_map/dot_general | solution.py:76
  251.9 42.0 %collective-permute-done.17 = bf16[512,1792]{1,0:T(8,128)(2,1)S(1)} collective-permute-done((bf16[512,1792]{1,0:T(8,128)(2,1)S(1)}, bf16[512,1792]{1,0:T(8,128)(2,1)S(1)}, u32[]{:S(2)}, u32[]{:S(2)}) %collective-permute-start.17) | collective-permute-done | bytes 1835040 | tf_op jit(solution)/shard_map/ppermute | solution.py:14
  294.0 5.1 %add_convert_fusion = bf16[512,1792]{1,0:T(8,128)(2,1)} fusion(bf16[512,1792]{1,0:T(8,128)(2,1)S(1)} %collective-permute-done.17, bf16[2048,1792]{1,0:T(8,128)(2,1)S(1)} %bitcast.47, bf16[2048,1024]{1,0:T(8,128)(2,1)S(1)} %bitcast.50), kind=kOutput, calls=%fused_computation.7 | convolution fusion | flops 3760848896 | bytes 13107200 | tf_op jit(solution)/shard_map/dot_general | solution.py:78
  (32 shorter events, 4.1 us)
Async XLA Ops:
  2.1 7.1 %copy-start.4 = (bf16[512,1792]{1,0:T(8,128)(2,1)S(1)}, bf16[512,1792]{1,0:T(8,128)(2,1)}, u32[]{:S(2)}) copy-start(bf16[512,1792]{1,0:T(8,128)(2,1)} %param.5) | copy-start | bytes 5505028
  9.1 2.4 collective-permute-start
  9.2 62.0 %collective-permute-start.8 = (bf16[512,1792]{1,0:T(8,128)(2,1)S(1)}, bf16[512,1792]{1,0:T(8,128)(2,1)}, u32[]{:S(2)}, u32[]{:S(2)}) collective-permute-start(bf16[512,1792]{1,0:T(8,128)(2,1)S(1)} %copy-done.4), channel_id=1, source_target_pairs={{0,2},{2,0},{1,3},{3,1},{4,6},{6,4},{5,7},{7,5},{8,10},{10,8},{9,1... | collective-permute-start | bytes 5505032 | tf_op jit(solution)/shard_map/ppermute | solution.py:14
  11.5 9.0 %collective-permute-start.1 = (bf16[2,32,1024]{2,1,0:T(8,128)(2,1)S(1)}, bf16[2,32,1024]{2,1,0:T(8,128)(2,1)S(1)}, u32[]{:S(2)}, u32[]{:S(2)}) collective-permute-start(bf16[2,32,1024]{2,1,0:T(8,128)(2,1)S(1)} %get-tuple-element.16), channel_id=1, source_target_pairs={{0,12},{4,0},{8,4},{12,8},{1,13},{5,1},{9,5},{13,9},{2,14},{6,2},{... | collective-permute-start | bytes 393224 | tf_op jit(solution)/shard_map/ppermute | solution.py:14
  14.6 7.9 %collective-permute-start.2 = (bf16[2,32,1024]{2,1,0:T(8,128)(2,1)S(1)}, bf16[2,32,1024]{2,1,0:T(8,128)(2,1)S(1)}, u32[]{:S(2)}, u32[]{:S(2)}) collective-permute-start(bf16[2,32,1024]{2,1,0:T(8,128)(2,1)S(1)} %get-tuple-element.18), channel_id=1, source_target_pairs={{0,8},{4,12},{8,0},{12,4},{1,9},{5,13},{9,1},{13,5},{2,10},{6,14},... | collective-permute-start | bytes 393224 | tf_op jit(solution)/shard_map/ppermute | solution.py:14
  15.2 9.0 %collective-permute-start.3 = (bf16[2,32,1024]{2,1,0:T(8,128)(2,1)S(1)}, bf16[2,32,1024]{2,1,0:T(8,128)(2,1)S(1)}, u32[]{:S(2)}, u32[]{:S(2)}) collective-permute-start(bf16[2,32,1024]{2,1,0:T(8,128)(2,1)S(1)} %get-tuple-element.17), channel_id=1, source_target_pairs={{0,4},{4,8},{8,12},{12,0},{1,5},{5,9},{9,13},{13,1},{2,6},{6,10},{... | collective-permute-start | bytes 393224 | tf_op jit(solution)/shard_map/ppermute | solution.py:14
  24.2 42.1 %collective-permute-start.4 = (bf16[2,4,32,1024]{3,2,0,1:T(8,128)(2,1)S(1)}, bf16[2,4,32,1024]{3,2,0,1:T(8,128)(2,1)S(1)}, u32[]{:S(2)}, u32[]{:S(2)}) collective-permute-start(bf16[2,4,32,1024]{3,2,0,1:T(8,128)(2,1)S(1)} %get-tuple-element.14), channel_id=1, source_target_pairs={{0,16},{16,0},{1,17},{17,1},{2,18},{18,2},{3,19},{19,3},{4,20},{20... | collective-permute-start | bytes 1572872 | tf_op jit(solution)/shard_map/ppermute | solution.py:14
  66.5 47.6 %collective-permute-start.5 = (bf16[2,4,2,32,1024]{4,3,0,1,2:T(8,128)(2,1)S(1)}, bf16[2,4,2,32,1024]{4,3,0,1,2:T(8,128)(2,1)S(1)}, u32[]{:S(2)}, u32[]{:S(2)}) collective-permute-start(bf16[2,4,2,32,1024]{4,3,0,1,2:T(8,128)(2,1)S(1)} %get-tuple-element.10), channel_id=1, source_target_pairs={{0,96},{32,0},{64,32},{96,64},{1,97},{33,1},{65,33},{97,65},{2,98}... | collective-permute-start | bytes 3145736 | tf_op jit(solution)/shard_map/ppermute | solution.py:14
  69.3 44.7 %collective-permute-start.6 = (bf16[2,4,2,32,1024]{4,3,0,1,2:T(8,128)(2,1)S(1)}, bf16[2,4,2,32,1024]{4,3,0,1,2:T(8,128)(2,1)S(1)}, u32[]{:S(2)}, u32[]{:S(2)}) collective-permute-start(bf16[2,4,2,32,1024]{4,3,0,1,2:T(8,128)(2,1)S(1)} %get-tuple-element.10), channel_id=1, source_target_pairs={{0,64},{32,96},{64,0},{96,32},{1,65},{33,97},{65,1},{97,33},{2,66}... | collective-permute-start | bytes 3145736 | tf_op jit(solution)/shard_map/ppermute | solution.py:14
  70.1 47.6 %collective-permute-start.7 = (bf16[2,4,2,32,1024]{4,3,0,1,2:T(8,128)(2,1)S(1)}, bf16[2,4,2,32,1024]{4,3,0,1,2:T(8,128)(2,1)S(1)}, u32[]{:S(2)}, u32[]{:S(2)}) collective-permute-start(bf16[2,4,2,32,1024]{4,3,0,1,2:T(8,128)(2,1)S(1)} %get-tuple-element.10), channel_id=1, source_target_pairs={{0,32},{32,64},{64,96},{96,0},{1,33},{33,65},{65,97},{97,1},{2,34}... | collective-permute-start | bytes 3145736 | tf_op jit(solution)/shard_map/ppermute | solution.py:14
  118.3 2.3 copy-start
  125.0 6.7 %collective-permute-start.9 = (bf16[1024,1792]{1,0:T(8,128)(2,1)S(1)}, bf16[1024,1792]{1,0:T(8,128)(2,1)S(1)}, u32[]{:S(2)}, u32[]{:S(2)}) collective-permute-start(bf16[1024,1792]{1,0:T(8,128)(2,1)S(1)} %convolution_convert_fusion), channel_id=1, source_target_pairs={{0,1},{1,0},{2,3},{3,2},{4,5},{5,4},{6,7},{7,6},{8,9},{9,8},{10,11... | collective-permute-start | bytes 11010056 | tf_op jit(solution)/shard_map/ppermute | solution.py:14
  139.3 23.9 %collective-permute-start.10 = (bf16[256,1792]{1,0:T(8,128)(2,1)}, bf16[256,1792]{1,0:T(8,128)(2,1)S(1)}, u32[]{:S(2)}, u32[]{:S(2)}) collective-permute-start(bf16[256,1792]{1,0:T(8,128)(2,1)} %get-tuple-element.6), channel_id=1, source_target_pairs={{0,4},{4,8},{8,12},{12,0},{1,5},{5,9},{9,13},{13,1},{2,6},{6,10},{... | collective-permute-start | bytes 2752520 | tf_op jit(solution)/shard_map/ppermute | solution.py:14
  140.9 43.1 %collective-permute-start.11 = (bf16[256,1792]{1,0:T(8,128)(2,1)}, bf16[256,1792]{1,0:T(8,128)(2,1)S(1)}, u32[]{:S(2)}, u32[]{:S(2)}) collective-permute-start(bf16[256,1792]{1,0:T(8,128)(2,1)} %get-tuple-element.8), channel_id=1, source_target_pairs={{0,8},{4,12},{8,0},{12,4},{1,9},{5,13},{9,1},{13,5},{2,10},{6,14},... | collective-permute-start | bytes 2752520 | tf_op jit(solution)/shard_map/ppermute | solution.py:14
  143.8 40.2 %collective-permute-start.12 = (bf16[256,1792]{1,0:T(8,128)(2,1)}, bf16[256,1792]{1,0:T(8,128)(2,1)S(1)}, u32[]{:S(2)}, u32[]{:S(2)}) collective-permute-start(bf16[256,1792]{1,0:T(8,128)(2,1)} %get-tuple-element.7), channel_id=1, source_target_pairs={{0,12},{4,0},{8,4},{12,8},{1,13},{5,1},{9,5},{13,9},{2,14},{6,2},{... | collective-permute-start | bytes 2752520 | tf_op jit(solution)/shard_map/ppermute | solution.py:14
  185.9 1.2 copy-start.5
  189.4 41.6 %collective-permute-start.13 = (bf16[256,1792]{1,0:T(8,128)(2,1)S(1)}, bf16[256,1792]{1,0:T(8,128)(2,1)S(1)}, u32[]{:S(2)}, u32[]{:S(2)}) collective-permute-start(bf16[256,1792]{1,0:T(8,128)(2,1)S(1)} %bitcast.52), channel_id=1, source_target_pairs={{0,12},{4,0},{8,4},{12,8},{1,13},{5,1},{9,5},{13,9},{2,14},{6,2},{... | collective-permute-start | bytes 2752520 | tf_op jit(solution)/shard_map/ppermute | solution.py:14
  191.5 39.5 %collective-permute-start.14 = (bf16[256,1792]{1,0:T(8,128)(2,1)S(1)}, bf16[256,1792]{1,0:T(8,128)(2,1)S(1)}, u32[]{:S(2)}, u32[]{:S(2)}) collective-permute-start(bf16[256,1792]{1,0:T(8,128)(2,1)S(1)} %bitcast.53), channel_id=1, source_target_pairs={{0,8},{4,12},{8,0},{12,4},{1,9},{5,13},{9,1},{13,5},{2,10},{6,14},... | collective-permute-start | bytes 2752520 | tf_op jit(solution)/shard_map/ppermute | solution.py:14
  192.7 41.8 %collective-permute-start.15 = (bf16[256,1792]{1,0:T(8,128)(2,1)S(1)}, bf16[256,1792]{1,0:T(8,128)(2,1)S(1)}, u32[]{:S(2)}, u32[]{:S(2)}) collective-permute-start(bf16[256,1792]{1,0:T(8,128)(2,1)S(1)} %bitcast.54), channel_id=1, source_target_pairs={{0,4},{4,8},{8,12},{12,0},{1,5},{5,9},{9,13},{13,1},{2,6},{6,10},{... | collective-permute-start | bytes 2752520 | tf_op jit(solution)/shard_map/ppermute | solution.py:14
  234.4 2.2 copy-start.1
  235.1 6.5 %collective-permute-start.16 = (bf16[4,256,1792]{2,1,0:T(8,128)(2,1)S(1)}, bf16[4,256,1792]{2,1,0:T(8,128)(2,1)S(1)}, u32[]{:S(2)}, u32[]{:S(2)}) collective-permute-start(bf16[4,256,1792]{2,1,0:T(8,128)(2,1)S(1)} %get-tuple-element.5), channel_id=1, source_target_pairs={{0,1},{1,0},{2,3},{3,2},{4,5},{5,4},{6,7},{7,6},{8,9},{9,8},{10,11... | collective-permute-start | bytes 11010056 | tf_op jit(solution)/shard_map/ppermute | solution.py:14
  241.5 1.8 copy-start.3
  246.1 47.9 %copy-start.2 = (bf16[2,4,4,2,32,1024]{5,4,3,2,1,0:T(8,128)(2,1)S(1)}, bf16[2,4,4,2,32,1024]{5,4,3,2,1,0:T(8,128)(2,1)}, u32[]{:S(2)}) copy-start(bf16[2,4,4,2,32,1024]{5,4,3,2,1,0:T(8,128)(2,1)} %copy.14) | copy-start | bytes 12582916
  251.9 42.1 %collective-permute-start.17 = (bf16[512,1792]{1,0:T(8,128)(2,1)S(1)}, bf16[512,1792]{1,0:T(8,128)(2,1)S(1)}, u32[]{:S(2)}, u32[]{:S(2)}) collective-permute-start(bf16[512,1792]{1,0:T(8,128)(2,1)S(1)} %convolution_convert_fusion.1), channel_id=1, source_target_pairs={{0,2},{2,0},{1,3},{3,1},{4,6},{6,4},{5,7},{7,5},{8,10},{10,8},{9,1... | collective-permute-start | bytes 5505032 | tf_op jit(solution)/shard_map/ppermute | solution.py:14

commit v2 on v0

v2 whole, which is shorter than its diff:
```python
import functools
import math

import jax
import jax.numpy as jnp
from jax import lax
from jax.experimental import pallas as pl
from jax.experimental.pallas import tpu as pltpu
from jax.sharding import Mesh, PartitionSpec as P

NAMES = ("x", "zh", "y", "zl", "core")
SIZES = {"x": 4, "zh": 2, "y": 4, "zl": 2, "core": 2}
BF16, F32 = jnp.bfloat16, jnp.float32

STEP = {"b": lambda i: i ^ 1, "a": lambda i: 3 - i, "ab": lambda i: i ^ 2}


def swap(value, axis, step=None):
    move = STEP[step] if step else lambda i: 1 - i
    return lax.ppermute(value, axis, [(i, move(i)) for i in range(SIZES[axis])])


def around(axis):
    at = lax.axis_index(axis)
    return [at, at ^ 1, 3 - at, at ^ 2]


def after(value, *others):
    return lax.optimization_barrier((value,) + others)[0]


def gelu_parts(pre_float):
    cumulative = 0.5 * (1.0 + jax.scipy.special.erf(pre_float / math.sqrt(2.0)))
    density = jnp.exp(-0.5 * pre_float * pre_float) / math.sqrt(2.0 * math.pi)
    return (pre_float * cumulative, cumulative + pre_float * density)


def split_kernel(index, grad, near, away):
    size = near.shape[2] // 2
    for out, core in ((near, 0), (away, 1)):
        for y in range(4):
            for z in range(2):
                at = pl.multiple_of(index[core * 8 + y * 2 + z] * size, size)
                out[y, :, z * size : (z + 1) * size] = grad[:, pl.ds(at, size)]


def split_grad(grad, index):
    rows, width = grad.shape
    piece = jax.ShapeDtypeStruct((4, rows, width // 8), BF16)
    return pl.pallas_call(
        split_kernel,
        grid_spec=pltpu.PrefetchScalarGridSpec(
            num_scalar_prefetch=1,
            grid=(1,),
            in_specs=[pl.BlockSpec((rows, width), lambda i, s: (0, 0))],
            out_specs=[pl.BlockSpec(piece.shape, lambda i, s: (0, 0, 0))] * 2,
        ),
        out_shape=[piece, piece],
    )(index, grad)


def hidden_kernel(index, pre, left, right):
    value = gelu_parts(pre[...].astype(F32))[0].astype(BF16)
    half = value.shape[1] // 2
    left[...] = value[:, :half]
    right[...] = value[:, half:]


def make_hidden(pre, index):
    tokens, units = pre.shape
    rows, half = tokens // 8, units // 2
    out = jax.ShapeDtypeStruct((tokens, half), BF16)
    return pl.pallas_call(
        hidden_kernel,
        grid_spec=pltpu.PrefetchScalarGridSpec(
            num_scalar_prefetch=1,
            grid=(8,),
            in_specs=[pl.BlockSpec((rows, units), lambda i, s: (s[i], 0))],
            out_specs=[pl.BlockSpec((rows, half), lambda i, s: (i, 0))] * 2,
        ),
        out_shape=[out, out],
    )(index, pre)


def finish_kernel(index, pre, own_l, own_r, far_l, far_r, out):
    slope = gelu_parts(pre[...].astype(F32))[1]
    half = own_l.shape[1]
    out[:, :half] = ((own_l[...] + far_l[...].astype(F32)) * slope[:, :half]).astype(BF16)
    out[:, half:] = ((own_r[...] + far_r[...].astype(F32)) * slope[:, half:]).astype(BF16)


def finish(pre, own_l, own_r, far_l, far_r, index):
    tokens, units = pre.shape
    rows, half = tokens // 8, units // 2
    turned = pl.BlockSpec((rows, units), lambda i, s: (s[i], 0))
    plain = pl.BlockSpec((rows, half), lambda i, s: (i, 0))
    return pl.pallas_call(
        finish_kernel,
        grid_spec=pltpu.PrefetchScalarGridSpec(
            num_scalar_prefetch=1, grid=(8,), in_specs=[turned] + [plain] * 4, out_specs=turned
        ),
        out_shape=jax.ShapeDtypeStruct((tokens, units), BF16),
    )(index, pre, own_l, own_r, far_l, far_r)


def gather_square(first, second, axis):
    b1 = swap(first, axis, "b")
    a1 = swap(second, axis, "a")
    return b1, a1


def shards(grad_out, pre_act, weight):
    rows, width = grad_out.shape[1:]
    tokens, units = pre_act.shape
    half = units // 2
    own_rows = weight.shape[0]
    zl, core = lax.axis_index("zl"), lax.axis_index("core")
    grad_index = jnp.stack(
        [(y * 2 + (zl ^ z)) * 2 + (core ^ k) for k in range(2) for y in around("y") for z in range(2)]
    )
    zh = lax.axis_index("zh")
    token_index = jnp.stack([x * 2 + (zh ^ z) for x in around("x") for z in range(2)])

    near, away = split_grad(grad_out[0], grad_index)
    sibling = swap(away, "core")
    weight_l, weight_r = weight[:, :half], weight[:, half:]
    other_l = swap(weight_l, "zl")
    hidden_l, hidden_r = make_hidden(after(pre_act, away), token_index)

    both = jnp.stack([near, sibling])
    grad = jnp.stack([both[:, 0]] + [swap(both[:, s], "y", m) for s, m in ((1, "b"), (2, "a"), (3, "ab"))], 1)
    grad = grad.reshape(8, rows, 2 * own_rows)
    grad_far = swap(grad, "zh")

    def gather_x(piece):
        mine, theirs = piece[..., own_rows:], piece[..., :own_rows]
        mine_b = swap(mine, "x", "b")
        theirs_a = swap(theirs, "x", "a")
        mine = jnp.stack([mine, mine_b])
        theirs = jnp.stack([theirs, theirs_a])
        mine_a = swap(mine, "x", "a")
        theirs_b = swap(theirs, "x", "b")
        return [mine[0], mine[1], mine_a[0], mine_a[1]], [theirs[0], theirs_b[0], theirs[1], theirs_b[1]]

    hidden_lb = swap(after(hidden_l, grad), "y", "b")
    hidden_ra = swap(after(hidden_r, grad), "y", "a")
    near_o, near_t = gather_x(grad)
    other_r = swap(after(weight_r, grad_far), "zl")
    hidden_l = jnp.stack([hidden_l, hidden_lb])
    hidden_r = jnp.stack([hidden_r, hidden_ra])
    hidden_la = swap(hidden_l, "y", "a")
    hidden_rb = swap(hidden_r, "y", "b")
    far_o, far_t = gather_x(after(grad_far, near_o[3]))
    hidden_l = jnp.concatenate([hidden_l, hidden_la])
    hidden_r = jnp.stack([hidden_r[0], hidden_rb[0], hidden_r[1], hidden_rb[1]])
    hidden_l = jnp.concatenate([hidden_l, swap(hidden_l, "core")]).reshape(8 * tokens, half)
    hidden_r = jnp.concatenate([hidden_r, swap(hidden_r, "core")]).reshape(8 * tokens, half)

    def together(near, far):
        return jnp.stack([v for pair in zip(near, far) for v in pair], 1).reshape(8 * tokens, own_rows)

    grad_other, grad_own = together(near_o, far_o), together(near_t, far_t)
    grad_other, grad_own, hidden_l, hidden_r, other_l, other_r = lax.optimization_barrier(
        (grad_other, grad_own, hidden_l, hidden_r, other_l, other_r)
    )

    def outer(g, h):
        return lax.dot_general(g, h, (((0,), (0,)), ((), ())), preferred_element_type=F32)

    sent_l = outer(grad_other, hidden_l).astype(BF16)
    sent_r = outer(grad_other, hidden_r).astype(BF16)
    got_l = swap(sent_l, "zl")
    got_r = swap(sent_r, "zl")

    grad_both = after(jnp.concatenate([grad_own, grad_other], 1), sent_r)
    w_l = jnp.concatenate([weight_l, other_l])
    w_r = jnp.concatenate([weight_r, other_r])
    edge = 4 * tokens
    away_l = jnp.dot(grad_both[edge:], w_l, preferred_element_type=F32).astype(BF16)
    away_l = swap(away_l, "core")
    away_r = jnp.dot(grad_both[edge:], w_r, preferred_element_type=F32).astype(BF16)
    away_r = swap(away_r, "core")
    part_l = jnp.dot(grad_both[:edge], w_l, preferred_element_type=F32) + away_l.astype(F32)
    part_r = jnp.dot(grad_both[:edge], w_r, preferred_element_type=F32) + away_r.astype(F32)
    part_l = part_l.reshape(2, 2, tokens, half)
    part_r = part_r.reshape(2, 2, tokens, half)
    part_l = part_l[0] + swap(part_l[1].astype(BF16), "y", "a").astype(F32)
    part_r = part_r[:, 0] + swap(part_r[:, 1].astype(BF16), "y", "b").astype(F32)
    far_l = swap(part_l[1].astype(BF16), "y", "b")
    far_r = swap(part_r[1].astype(BF16), "y", "a")
    grad_pre = finish(pre_act, part_l[0], part_r[0], far_l, far_r, token_index)

    kept_l = outer(grad_own, hidden_l) + got_l.astype(F32)
    kept_r = outer(grad_own, hidden_r) + got_r.astype(F32)
    return (grad_pre, jnp.concatenate([kept_l, kept_r], 1).astype(BF16))


def solution(mesh):
    sizes = tuple(SIZES[name] for name in NAMES)
    inner = Mesh(mesh.devices.reshape(sizes), NAMES)
    col, row = ("y", "zl", "core"), ("x", "zh")
    in_specs = (P(col, row, None), P(col, row), P(col, row))
    out_specs = (P(col, row), P(col, row))
    return jax.shard_map(shards, mesh=inner, in_specs=in_specs, out_specs=out_specs, check_vma=False)
```

time: 584 us -> 164 us (0.28)
  waiting for transfers between devices: 463 us -> 83 us
  blocking collectives: 54.8 us -> 0 us
  starting transfers between devices: 0.12 us -> 32.5 us
  Pallas kernels: 0 us -> 15.3 us
  between operations: 13.8 us -> 1.18 us
  matrix products: 29.8 us -> 18.8 us
  local copies, waits for them, and re-layouts: 16.5 us -> 7.41 us
    reduce_scatter x1 -> x0, waiting for transfers between devices: 296 us -> none  [shards(): lax.psum_scatter(jnp.dot(row_slice, down_weight, preferred_element_type=j...]
    all_gather x2 -> x0, waiting for transfers between devices: 167 us -> none  [the longest x1 90.4 us: shards(): lax.all_gather(hidden, 'col', axis=0, tiled=True)]
    ppermute x0 -> x29, waiting for transfers between devices: none -> 83 us  [swap(): return lax.ppermute(value, axis, [(i, move(i)) for i in range(SIZES[axis])])]
    all_to_all x1 -> x0, blocking collectives: 54.8 us -> none  [shards(): lax.all_to_all(token_block, 'col', split_axis=1, concat_axis=0, tiled=True)]
    ppermute x0 -> x29, starting transfers between devices: none -> 32.5 us  [swap(): return lax.ppermute(value, axis, [(i, move(i)) for i in range(SIZES[axis])])]
    pallas_call x0 -> x3, Pallas kernels: none -> 15.3 us  [the longest x1 6.89 us: finish(): pl.pallas_call(finish_kernel, grid_spec=pltpu.PrefetchScalarGridSpec(num_...]
    dot_general x2 -> x8, matrix products: 29.8 us -> 18.8 us  [the longest x4 9.42 us: outer(): lax.dot_general(g, h, (((0,), (0,)), ((), ())), preferred_element_type=F32)]
    all_to_all x1 -> x0, local copies, waits for them, and re-layouts: 6.37 us -> none  [shards(): lax.all_to_all(token_block, 'col', split_axis=1, concat_axis=0, tiled=True)]
  transfers between devices with their start and end apart: 3 -> 29, of which waited for: 3 -> 15; matrix products, arithmetic and copies ran while one was open for 0% -> 14% of each run, Pallas kernels for 0% -> 4%
where the time goes in v2:
time: 164 us; the launch traced here: 163 us
  waiting for transfers between devices  83 us (51%)
  starting transfers between devices  32.5 us (20%)
  matrix products  18.8 us (11%)
  Pallas kernels  15.3 us (9%)
  local copies, waits for them, and re-layouts  7.41 us (5%)
  other arithmetic  4.81 us (3%)
    ppermute x29, waiting for transfers between devices, swap(): return lax.ppermute(value, axis, [(i, move(i)) for i in range(SIZES[axis])])  83 us
    ppermute x29, starting transfers between devices, swap(): return lax.ppermute(value, axis, [(i, move(i)) for i in range(SIZES[axis])])  32.5 us
    dot_general x4, matrix products, outer(): lax.dot_general(g, h, (((0,), (0,)), ((), ())), preferred_element_type=F32)  9.42 us
    pallas_call x1, Pallas kernels, finish(): pl.pallas_call(finish_kernel, grid_spec=pltpu.PrefetchScalarGridSpec(num_...  6.89 us
    pallas_call x1, Pallas kernels, make_hidden(): pl.pallas_call(hidden_kernel, grid_spec=pltpu.PrefetchScalarGridSpec(num_...  5.87 us
  transfers between devices with their start and end apart: 29, of which 15 were waited for; matrix products, arithmetic and copies ran while one was open for 14% of the time, Pallas kernels for 4%

profile of v2, /device:TPU:0, one launch (start us, length us, event | category | flops | bytes accessed | tf_op | source)
XLA Modules:
  0.0 163.0 jit_solution(936346919625992212)
XLA Ops:
  1.3 2.5 %shard_map.50 = (bf16[4,32,1024]{2,1,0:T(8,128)(2,1)}, bf16[4,32,1024]{2,1,0:T(8,128)(2,1)}) custom-call(s32[16]{0:T(128)} %stack.187.index, bf16[32,8192]{1,0:T(8,128)(2,1)} %bitcast.167), custom_call_target="tpu_custom_call" | custom-call | tf_op jit(solution)/shard_map/pallas_call | solution.py:50
  3.8 1.7 %collective-permute-done = bf16[4,32,1024]{2,1,0:T(8,128)(2,1)S(1)} collective-permute-done((bf16[4,32,1024]{2,1,0:T(8,128)(2,1)}, bf16[4,32,1024]{2,1,0:T(8,128)(2,1)S(1)}, u32[]{:S(2)}, u32[]{:S(2)}) %collective-permute-start) | collective-permute-done | bytes 262176 | tf_op jit(solution)/shard_map/ppermute | solution.py:20
  5.6 1.0 fusion.33
  6.6 1.7 %collective-permute-start.1 = (bf16[2,32,1024]{2,1,0:T(8,128)(2,1)S(1)}, bf16[2,32,1024]{2,1,0:T(8,128)(2,1)S(1)}, u32[]{:S(2)}, u32[]{:S(2)}) collective-permute-start(bf16[2,32,1024]{2,1,0:T(8,128)(2,1)S(1)} %get-tuple-element.50), channel_id=1, source_target_pairs={{0,4},{4,0},{8,12},{12,8},{1,5},{5,1},{9,13},{13,9},{2,6},{6,2},{1... | collective-permute-start | bytes 393224 | tf_op jit(solution)/shard_map/ppermute | solution.py:20
  8.3 2.2 %collective-permute-start.2 = (bf16[2,32,1024]{2,1,0:T(8,128)(2,1)S(1)}, bf16[2,32,1024]{2,1,0:T(8,128)(2,1)S(1)}, u32[]{:S(2)}, u32[]{:S(2)}) collective-permute-start(bf16[2,32,1024]{2,1,0:T(8,128)(2,1)S(1)} %get-tuple-element.52), channel_id=1, source_target_pairs={{0,12},{4,8},{8,4},{12,0},{1,13},{5,9},{9,5},{13,1},{2,14},{6,10},... | collective-permute-start | bytes 393224 | tf_op jit(solution)/shard_map/ppermute | solution.py:20
  11.2 1.6 fusion.41
  13.5 5.9 %shard_map.51 = (bf16[256,896]{1,0:T(8,128)(2,1)}, bf16[256,896]{1,0:T(8,128)(2,1)}) custom-call(s32[8]{0:T(128)} %stack.170.index, bf16[256,1792]{1,0:T(8,128)(2,1)} %pre.2), custom_call_target="tpu_custom_call" | custom-call | tf_op jit(solution)/shard_map/pallas_call | solution.py:73
  19.7 2.8 %collective-permute-start.9 = (bf16[8,32,512]{2,1,0:T(8,128)(2,1)S(1)}, bf16[8,32,512]{2,1,0:T(8,128)(2,1)S(1)}, u32[]{:S(2)}, u32[]{:S(2)}) collective-permute-start(bf16[8,32,512]{2,1,0:T(8,128)(2,1)S(1)} %get-tuple-element.43), channel_id=1, source_target_pairs={{0,96},{32,64},{64,32},{96,0},{1,97},{33,65},{65,33},{97,1},{2,98}... | collective-permute-start | bytes 786440 | tf_op jit(solution)/shard_map/ppermute | solution.py:20
  22.5 4.0 %collective-permute-start.4 = (bf16[8,32,1024]{2,1,0:T(8,128)(2,1)S(1)}, bf16[8,32,1024]{2,1,0:T(8,128)(2,1)S(1)}, u32[]{:S(2)}, u32[]{:S(2)}) collective-permute-start(bf16[8,32,1024]{2,1,0:T(8,128)(2,1)S(1)} %bitcast.146), channel_id=1, source_target_pairs={{0,16},{16,0},{1,17},{17,1},{2,18},{18,2},{3,19},{19,3},{4,20},{20... | collective-permute-start | bytes 1572872 | tf_op jit(solution)/shard_map/ppermute | solution.py:20
  26.5 2.6 %collective-permute-start.16 = (bf16[256,896]{1,0:T(8,128)(2,1)S(1)}, bf16[256,896]{1,0:T(8,128)(2,1)S(1)}, u32[]{:S(2)}, u32[]{:S(2)}) collective-permute-start(bf16[256,896]{1,0:T(8,128)(2,1)S(1)} %copy-done.2), channel_id=1, source_target_pairs={{0,12},{4,8},{8,4},{12,0},{1,13},{5,9},{9,5},{13,1},{2,14},{6,10},... | collective-permute-start | bytes 1376264 | tf_op jit(solution)/shard_map/ppermute | solution.py:20
  29.6 1.1 collective-permute-start.19
  30.7 5.1 %collective-permute-done.5 = bf16[8,32,512]{2,1,0:T(8,128)(2,1)S(1)} collective-permute-done((bf16[8,32,512]{2,1,0:T(8,128)(2,1)S(1)}, bf16[8,32,512]{2,1,0:T(8,128)(2,1)S(1)}, u32[]{:S(2)}, u32[]{:S(2)}) %collective-permute-start.5) | collective-permute-done | bytes 262176 | tf_op jit(solution)/shard_map/ppermute | solution.py:20
  36.1 3.0 %collective-permute-done.16 = bf16[256,896]{1,0:T(8,128)(2,1)S(1)} collective-permute-done((bf16[256,896]{1,0:T(8,128)(2,1)S(1)}, bf16[256,896]{1,0:T(8,128)(2,1)S(1)}, u32[]{:S(2)}, u32[]{:S(2)}) %collective-permute-start.16) | collective-permute-done | bytes 458784 | tf_op jit(solution)/shard_map/ppermute | solution.py:20
  39.2 0.9 collective-permute-start.7
  40.5 2.4 %collective-permute-start.11 = (bf16[8,32,512]{2,1,0:T(8,128)(2,1)S(1)}, bf16[8,32,512]{2,1,0:T(8,128)(2,1)S(1)}, u32[]{:S(2)}, u32[]{:S(2)}) collective-permute-start(bf16[8,32,512]{2,1,0:T(8,128)(2,1)S(1)} %get-tuple-element.39), channel_id=1, source_target_pairs={{0,96},{32,64},{64,32},{96,0},{1,97},{33,65},{65,33},{97,1},{2,98}... | collective-permute-start | bytes 786440 | tf_op jit(solution)/shard_map/ppermute | solution.py:20
  43.0 4.9 %collective-permute-done.10 = bf16[2,8,32,512]{3,2,1,0:T(8,128)(2,1)S(1)} collective-permute-done((bf16[2,8,32,512]{3,2,1,0:T(8,128)(2,1)S(1)}, bf16[2,8,32,512]{3,2,1,0:T(8,128)(2,1)S(1)}, u32[]{:S(2)}, u32[]{:S(2)}) %collective-permute-start.10) | collective-permute-done | bytes 524320 | tf_op jit(solution)/shard_map/ppermute | solution.py:20
  48.2 9.7 %collective-permute-done.11 = bf16[8,32,512]{2,1,0:T(8,128)(2,1)S(1)} collective-permute-done((bf16[8,32,512]{2,1,0:T(8,128)(2,1)S(1)}, bf16[8,32,512]{2,1,0:T(8,128)(2,1)S(1)}, u32[]{:S(2)}, u32[]{:S(2)}) %collective-permute-start.11) | collective-permute-done | bytes 262176 | tf_op jit(solution)/shard_map/ppermute | solution.py:20
  57.9 2.1 %collective-permute-start.14 = (bf16[2,256,896]{2,1,0:T(8,128)(2,1)S(1)}, bf16[2,256,896]{2,1,0:T(8,128)(2,1)S(1)}, u32[]{:S(2)}, u32[]{:S(2)}) collective-permute-start(bf16[2,256,896]{2,1,0:T(8,128)(2,1)S(1)} %pad_maximum_fusion.11), channel_id=1, source_target_pairs={{0,12},{4,8},{8,4},{12,0},{1,13},{5,9},{9,5},{13,1},{2,14},{6,10},... | collective-permute-start | bytes 2752520 | tf_op jit(solution)/shard_map/ppermute | solution.py:20
  60.2 1.1 collective-permute-start.20
  61.3 9.2 %collective-permute-done.12 = bf16[2,8,32,512]{3,2,1,0:T(8,128)(2,1)S(1)} collective-permute-done((bf16[2,8,32,512]{3,2,1,0:T(8,128)(2,1)S(1)}, bf16[2,8,32,512]{3,2,1,0:T(8,128)(2,1)S(1)}, u32[]{:S(2)}, u32[]{:S(2)}) %collective-permute-start.12) | collective-permute-done | bytes 524320 | tf_op jit(solution)/shard_map/ppermute | solution.py:20
  70.6 1.5 collective-permute-start.8
  72.6 5.9 %collective-permute-done.14 = bf16[2,256,896]{2,1,0:T(8,128)(2,1)S(1)} collective-permute-done((bf16[2,256,896]{2,1,0:T(8,128)(2,1)S(1)}, bf16[2,256,896]{2,1,0:T(8,128)(2,1)S(1)}, u32[]{:S(2)}, u32[]{:S(2)}) %collective-permute-start.14) | collective-permute-done | bytes 917536 | tf_op jit(solution)/shard_map/ppermute | solution.py:20
  79.2 2.0 %collective-permute-done.8 = bf16[2,8,32,512]{3,2,1,0:T(8,128)(2,1)S(1)} collective-permute-done((bf16[2,8,32,512]{3,2,1,0:T(8,128)(2,1)S(1)}, bf16[2,8,32,512]{3,2,1,0:T(8,128)(2,1)S(1)}, u32[]{:S(2)}, u32[]{:S(2)}) %collective-permute-start.8) | collective-permute-done | bytes 524320 | tf_op jit(solution)/shard_map/ppermute | solution.py:20
  81.9 0.9 collective-permute-done.15
  83.3 2.3 %convolution_convert_fusion.1 = bf16[512,896]{1,0:T(8,128)(2,1)S(1)} fusion(bf16[2048,512]{1,0:T(8,128)(2,1)S(1)} %bitcast.141, bf16[2048,896]{1,0:T(8,128)(2,1)S(1)} %bitcast.173), kind=kOutput, calls=%fused_computation.27 | convolution fusion | flops 1879506944 | bytes 6684672 | tf_op jit(solution)/shard_map/dot_general | solution.py:168
  86.3 2.3 %fusion.16 = bf16[1024,896]{1,0:T(8,128)(2,1)S(1)} fusion(bf16[2048,1024]{1,0:T(8,128)(2,1)S(1)} %pad_maximum_fusion, bf16[512,896]{1,0:T(8,128)(2,1)S(1)} %collective-permute-done.20, bf16[512,896]{1,0:T(8,128)(2,1)S(1)} %get-tuple-element.24), kind=kOutput, calls=%fused_computation.25 | convolution fusion | flops 1883635712 | bytes 5767168 | tf_op jit(solution)/shard_map/dot_general | solution.py:181
  88.9 2.3 %convolution_convert_fusion = bf16[512,896]{1,0:T(8,128)(2,1)S(1)} fusion(bf16[2048,512]{1,0:T(8,128)(2,1)S(1)} %bitcast.143, bf16[2048,896]{1,0:T(8,128)(2,1)S(1)} %bitcast.158), kind=kOutput, calls=%fused_computation.26 | convolution fusion | flops 1879506944 | bytes 6684672 | tf_op jit(solution)/shard_map/dot_general | solution.py:168
  91.2 1.1 collective-permute-start.27
  92.3 2.3 %fusion.13 = bf16[1024,896]{1,0:T(8,128)(2,1)S(1)} fusion(bf16[2048,1024]{1,0:T(8,128)(2,1)S(1)} %pad_maximum_fusion, bf16[512,896]{1,0:T(8,128)(2,1)S(1)} %collective-permute-done.19, bf16[512,896]{1,0:T(8,128)(2,1)S(1)} %get-tuple-element.33), kind=kOutput, calls=%fused_computation.24 | convolution fusion | flops 1883635712 | bytes 5767168 | tf_op jit(solution)/shard_map/dot_general | solution.py:179
  94.8 1.2 collective-permute-start.28
  96.1 18.4 %collective-permute-done.27 = bf16[512,896]{1,0:T(8,128)(2,1)S(1)} collective-permute-done((bf16[512,896]{1,0:T(8,128)(2,1)S(1)}, bf16[512,896]{1,0:T(8,128)(2,1)S(1)}, u32[]{:S(2)}, u32[]{:S(2)}) %collective-permute-start.27) | collective-permute-done | bytes 917536 | tf_op jit(solution)/shard_map/ppermute | solution.py:20
  114.5 2.4 %add_convert_fusion.1 = bf16[512,896]{1,0:T(8,128)(2,1)S(1)} fusion(bf16[512,896]{1,0:T(8,128)(2,1)S(1)} %collective-permute-done.27, bf16[2048,512]{1,0:T(8,128)(2,1)S(1)} %bitcast.139, bf16[2048,896]{1,0:T(8,128)(2,1)S(1)} %bitcast.159), kind=kOutput, calls=%fused_computation.22 | convolution fusion | flops 1880424448 | bytes 7602176 | tf_op jit(solution)/shard_map/dot_general | solution.py:168
  116.9 2.4 %convert_add_fusion = f32[1024,896]{1,0:T(8,128)S(1)} fusion(bf16[1024,896]{1,0:T(8,128)(2,1)S(1)} %collective-permute-done.23, bf16[2048,1024]{1,0:T(8,128)(2,1)S(1)} %pad_maximum_fusion, bf16[512,896]{1,0:T(8,128)(2,1)S(1)} %collective-permute-done.20, bf16[512,896]{1,0:T(8,128)(2,1)S(1)} %get-tuple-element.24), kind=kOutput, calls=%fused_computation.2 | convolution fusion | flops 1884553216 | bytes 9437184 | tf_op jit(solution)/shard_map/dot_general | solution.py:184
  119.5 2.4 %convert_add_fusion.1 = f32[1024,896]{1,0:T(8,128)S(1)} fusion(bf16[1024,896]{1,0:T(8,128)(2,1)S(1)} %collective-permute-done.21, bf16[2048,1024]{1,0:T(8,128)(2,1)S(1)} %pad_maximum_fusion, bf16[512,896]{1,0:T(8,128)(2,1)S(1)} %collective-permute-done.19, bf16[512,896]{1,0:T(8,128)(2,1)S(1)} %get-tuple-element.33), kind=kOutput, calls=%fused_computation.3 | convolution fusion | flops 1884553216 | bytes 9437184 | tf_op jit(solution)/shard_map/dot_general | solution.py:183
  121.9 1.9 %collective-permute-start.22 = (bf16[2,256,896]{2,1,0:T(8,128)(2,1)S(1)}, bf16[2,256,896]{2,1,0:T(8,128)(2,1)S(1)}, u32[]{:S(2)}, u32[]{:S(2)}) collective-permute-start(bf16[2,256,896]{2,1,0:T(8,128)(2,1)S(1)} %bitcast.166), channel_id=1, source_target_pairs={{0,12},{4,8},{8,4},{12,0},{1,13},{5,9},{9,5},{13,1},{2,14},{6,10},... | collective-permute-start | bytes 2752520 | tf_op jit(solution)/shard_map/ppermute | solution.py:20
  123.8 9.8 %collective-permute-done.28 = bf16[512,896]{1,0:T(8,128)(2,1)S(1)} collective-permute-done((bf16[512,896]{1,0:T(8,128)(2,1)S(1)}, bf16[512,896]{1,0:T(8,128)(2,1)S(1)}, u32[]{:S(2)}, u32[]{:S(2)}) %collective-permute-start.28) | collective-permute-done | bytes 917536 | tf_op jit(solution)/shard_map/ppermute | solution.py:20
  133.6 2.4 %add_convert_fusion = bf16[512,896]{1,0:T(8,128)(2,1)S(1)} fusion(bf16[512,896]{1,0:T(8,128)(2,1)S(1)} %collective-permute-done.28, bf16[2048,512]{1,0:T(8,128)(2,1)S(1)} %bitcast.140, bf16[2048,896]{1,0:T(8,128)(2,1)S(1)} %bitcast.174), kind=kOutput, calls=%fused_computation.21 | convolution fusion | flops 1880424448 | bytes 7602176 | tf_op jit(solution)/shard_map/dot_general | solution.py:168
  136.0 1.4 pad_maximum_fusion.6
  137.3 3.3 %collective-permute-done.24 = bf16[2,256,896]{2,1,0:T(8,128)(2,1)S(1)} collective-permute-done((bf16[2,256,896]{2,1,0:T(8,128)(2,1)S(1)}, bf16[2,256,896]{2,1,0:T(8,128)(2,1)S(1)}, u32[]{:S(2)}, u32[]{:S(2)}) %collective-permute-start.24) | collective-permute-done | bytes 917536 | tf_op jit(solution)/shard_map/ppermute | solution.py:20
  140.9 1.9 %collective-permute-start.26 = (bf16[256,896]{1,0:T(8,128)(2,1)S(1)}, bf16[256,896]{1,0:T(8,128)(2,1)S(1)}, u32[]{:S(2)}, u32[]{:S(2)}) collective-permute-start(bf16[256,896]{1,0:T(8,128)(2,1)S(1)} %fusion.21), channel_id=1, source_target_pairs={{0,12},{4,8},{8,4},{12,0},{1,13},{5,9},{9,5},{13,1},{2,14},{6,10},... | collective-permute-start | bytes 1376264 | tf_op jit(solution)/shard_map/ppermute | solution.py:20
  142.8 3.3 %collective-permute-done.22 = bf16[2,256,896]{2,1,0:T(8,128)(2,1)S(1)} collective-permute-done((bf16[2,256,896]{2,1,0:T(8,128)(2,1)S(1)}, bf16[2,256,896]{2,1,0:T(8,128)(2,1)S(1)}, u32[]{:S(2)}, u32[]{:S(2)}) %collective-permute-start.22) | collective-permute-done | bytes 917536 | tf_op jit(solution)/shard_map/ppermute | solution.py:20
  146.3 1.4 collective-permute-start.25
  147.7 1.0 slice_bitcast_fusion.own_r
  148.7 1.0 slice_bitcast_fusion.1.own_l
  149.7 4.6 %collective-permute-done.26.far_r = bf16[256,896]{1,0:T(8,128)(2,1)S(1)} collective-permute-done((bf16[256,896]{1,0:T(8,128)(2,1)S(1)}, bf16[256,896]{1,0:T(8,128)(2,1)S(1)}, u32[]{:S(2)}, u32[]{:S(2)}) %collective-permute-start.26) | collective-permute-done | bytes 458784 | tf_op jit(solution)/shard_map/ppermute | solution.py:20
  154.3 1.0 collective-permute-done.25.far_l
  155.3 0.8 copy-done.4
  156.1 6.9 %shard_map.52 = bf16[256,1792]{1,0:T(8,128)(2,1)} custom-call(s32[8]{0:T(128)} %stack.170.index, bf16[256,1792]{1,0:T(8,128)(2,1)} %pre.2, f32[256,896]{1,0:T(8,128)} %slice_bitcast_fusion.1.own_l, f32[256,896]{1,0:T(8,128)} %slice_bitcast_fusion.own_r, bf16[256,896]{1,0:T(8,128)(2,1)} %copy-done.4, bf16[256,896]{1,0:T(8,128)(2,1)} %copy-done.3), custom_call_target="tpu_custom_call" | custom-call | tf_op jit(solution)/shard_map/pallas_call | solution.py:97
  (81 shorter events, 8.2 us)
Async XLA Ops:
  3.8 1.7 %collective-permute-start = (bf16[4,32,1024]{2,1,0:T(8,128)(2,1)}, bf16[4,32,1024]{2,1,0:T(8,128)(2,1)S(1)}, u32[]{:S(2)}, u32[]{:S(2)}) collective-permute-start(bf16[4,32,1024]{2,1,0:T(8,128)(2,1)} %get-tuple-element.18), channel_id=1, source_target_pairs={{0,1},{1,0},{2,3},{3,2},{4,5},{5,4},{6,7},{7,6},{8,9},{9,8},{10,11... | collective-permute-start | bytes 786440 | tf_op jit(solution)/shard_map/ppermute | solution.py:20
  6.6 12.8 %collective-permute-start.1 = (bf16[2,32,1024]{2,1,0:T(8,128)(2,1)S(1)}, bf16[2,32,1024]{2,1,0:T(8,128)(2,1)S(1)}, u32[]{:S(2)}, u32[]{:S(2)}) collective-permute-start(bf16[2,32,1024]{2,1,0:T(8,128)(2,1)S(1)} %get-tuple-element.50), channel_id=1, source_target_pairs={{0,4},{4,0},{8,12},{12,8},{1,5},{5,1},{9,13},{13,9},{2,6},{6,2},{1... | collective-permute-start | bytes 393224 | tf_op jit(solution)/shard_map/ppermute | solution.py:20
  8.3 11.1 %collective-permute-start.2 = (bf16[2,32,1024]{2,1,0:T(8,128)(2,1)S(1)}, bf16[2,32,1024]{2,1,0:T(8,128)(2,1)S(1)}, u32[]{:S(2)}, u32[]{:S(2)}) collective-permute-start(bf16[2,32,1024]{2,1,0:T(8,128)(2,1)S(1)} %get-tuple-element.52), channel_id=1, source_target_pairs={{0,12},{4,8},{8,4},{12,0},{1,13},{5,9},{9,5},{13,1},{2,14},{6,10},... | collective-permute-start | bytes 393224 | tf_op jit(solution)/shard_map/ppermute | solution.py:20
  10.5 8.9 %collective-permute-start.3 = (bf16[2,32,1024]{2,1,0:T(8,128)(2,1)S(1)}, bf16[2,32,1024]{2,1,0:T(8,128)(2,1)S(1)}, u32[]{:S(2)}, u32[]{:S(2)}) collective-permute-start(bf16[2,32,1024]{2,1,0:T(8,128)(2,1)S(1)} %get-tuple-element.51), channel_id=1, source_target_pairs={{0,8},{4,12},{8,0},{12,4},{1,9},{5,13},{9,1},{13,5},{2,10},{6,14},... | collective-permute-start | bytes 393224 | tf_op jit(solution)/shard_map/ppermute | solution.py:20
  19.4 3.1 %copy-start.2 = (bf16[256,896]{1,0:T(8,128)(2,1)S(1)}, bf16[256,896]{1,0:T(8,128)(2,1)}, u32[]{:S(2)}) copy-start(bf16[256,896]{1,0:T(8,128)(2,1)} %get-tuple-element.23) | copy-start | bytes 1376260
  19.4 9.7 %copy-start.1 = (bf16[256,896]{1,0:T(8,128)(2,1)S(1)}, bf16[256,896]{1,0:T(8,128)(2,1)}, u32[]{:S(2)}) copy-start(bf16[256,896]{1,0:T(8,128)(2,1)} %get-tuple-element.21) | copy-start | bytes 1376260
  19.7 9.9 %collective-permute-start.9 = (bf16[8,32,512]{2,1,0:T(8,128)(2,1)S(1)}, bf16[8,32,512]{2,1,0:T(8,128)(2,1)S(1)}, u32[]{:S(2)}, u32[]{:S(2)}) collective-permute-start(bf16[8,32,512]{2,1,0:T(8,128)(2,1)S(1)} %get-tuple-element.43), channel_id=1, source_target_pairs={{0,96},{32,64},{64,32},{96,0},{1,97},{33,65},{65,33},{97,1},{2,98}... | collective-permute-start | bytes 786440 | tf_op jit(solution)/shard_map/ppermute | solution.py:20
  22.5 17.9 %collective-permute-start.4 = (bf16[8,32,1024]{2,1,0:T(8,128)(2,1)S(1)}, bf16[8,32,1024]{2,1,0:T(8,128)(2,1)S(1)}, u32[]{:S(2)}, u32[]{:S(2)}) collective-permute-start(bf16[8,32,1024]{2,1,0:T(8,128)(2,1)S(1)} %bitcast.146), channel_id=1, source_target_pairs={{0,16},{16,0},{1,17},{17,1},{2,18},{18,2},{3,19},{19,3},{4,20},{20... | collective-permute-start | bytes 1572872 | tf_op jit(solution)/shard_map/ppermute | solution.py:20
  26.5 12.7 %collective-permute-start.16 = (bf16[256,896]{1,0:T(8,128)(2,1)S(1)}, bf16[256,896]{1,0:T(8,128)(2,1)S(1)}, u32[]{:S(2)}, u32[]{:S(2)}) collective-permute-start(bf16[256,896]{1,0:T(8,128)(2,1)S(1)} %copy-done.2), channel_id=1, source_target_pairs={{0,12},{4,8},{8,4},{12,0},{1,13},{5,9},{9,5},{13,1},{2,14},{6,10},... | collective-permute-start | bytes 1376264 | tf_op jit(solution)/shard_map/ppermute | solution.py:20
  29.1 11.1 %collective-permute-start.13 = (bf16[256,896]{1,0:T(8,128)(2,1)S(1)}, bf16[256,896]{1,0:T(8,128)(2,1)S(1)}, u32[]{:S(2)}, u32[]{:S(2)}) collective-permute-start(bf16[256,896]{1,0:T(8,128)(2,1)S(1)} %copy-done.1), channel_id=1, source_target_pairs={{0,4},{4,0},{8,12},{12,8},{1,5},{5,1},{9,13},{13,9},{2,6},{6,2},{1... | collective-permute-start | bytes 1376264 | tf_op jit(solution)/shard_map/ppermute | solution.py:20
  29.3 6.5 %collective-permute-start.5 = (bf16[8,32,512]{2,1,0:T(8,128)(2,1)S(1)}, bf16[8,32,512]{2,1,0:T(8,128)(2,1)S(1)}, u32[]{:S(2)}, u32[]{:S(2)}) collective-permute-start(bf16[8,32,512]{2,1,0:T(8,128)(2,1)S(1)} %get-tuple-element.44), channel_id=1, source_target_pairs={{0,32},{32,0},{64,96},{96,64},{1,33},{33,1},{65,97},{97,65},{2,34}... | collective-permute-start | bytes 786440 | tf_op jit(solution)/shard_map/ppermute | solution.py:20
  29.6 53.7 %collective-permute-start.19 = (bf16[512,896]{1,0:T(8,128)(2,1)S(1)}, bf16[512,896]{1,0:T(8,128)(2,1)S(1)}, u32[]{:S(2)}, u32[]{:S(2)}) collective-permute-start(bf16[512,896]{1,0:T(8,128)(2,1)S(1)} %get-tuple-element.33), channel_id=1, source_target_pairs={{0,2},{2,0},{1,3},{3,1},{4,6},{6,4},{5,7},{7,5},{8,10},{10,8},{9,1... | collective-permute-start | bytes 2752520 | tf_op jit(solution)/shard_map/ppermute | solution.py:20
  35.8 12.1 %collective-permute-start.10 = (bf16[2,8,32,512]{3,2,1,0:T(8,128)(2,1)S(1)}, bf16[2,8,32,512]{3,2,1,0:T(8,128)(2,1)S(1)}, u32[]{:S(2)}, u32[]{:S(2)}) collective-permute-start(bf16[2,8,32,512]{3,2,1,0:T(8,128)(2,1)S(1)} %pad_maximum_fusion.16), channel_id=1, source_target_pairs={{0,32},{32,0},{64,96},{96,64},{1,33},{33,1},{65,97},{97,65},{2,34}... | collective-permute-start | bytes 1572872 | tf_op jit(solution)/shard_map/ppermute | solution.py:20
  39.2 21.1 %collective-permute-start.7 = (bf16[2,8,32,512]{3,2,1,0:T(8,128)(2,1)S(1)}, bf16[2,8,32,512]{3,2,1,0:T(8,128)(2,1)S(1)}, u32[]{:S(2)}, u32[]{:S(2)}) collective-permute-start(bf16[2,8,32,512]{3,2,1,0:T(8,128)(2,1)S(1)} %pad_maximum_fusion.14), channel_id=1, source_target_pairs={{0,96},{32,64},{64,32},{96,0},{1,97},{33,65},{65,33},{97,1},{2,98}... | collective-permute-start | bytes 1572872 | tf_op jit(solution)/shard_map/ppermute | solution.py:20
  40.2 31.9 %collective-permute-start.17 = (bf16[2,256,896]{2,1,0:T(8,128)(2,1)S(1)}, bf16[2,256,896]{2,1,0:T(8,128)(2,1)S(1)}, u32[]{:S(2)}, u32[]{:S(2)}) collective-permute-start(bf16[2,256,896]{2,1,0:T(8,128)(2,1)S(1)} %pad_maximum_fusion.12), channel_id=1, source_target_pairs={{0,4},{4,0},{8,12},{12,8},{1,5},{5,1},{9,13},{13,9},{2,6},{6,2},{1... | collective-permute-start | bytes 2752520 | tf_op jit(solution)/shard_map/ppermute | solution.py:20
  40.5 17.4 %collective-permute-start.11 = (bf16[8,32,512]{2,1,0:T(8,128)(2,1)S(1)}, bf16[8,32,512]{2,1,0:T(8,128)(2,1)S(1)}, u32[]{:S(2)}, u32[]{:S(2)}) collective-permute-start(bf16[8,32,512]{2,1,0:T(8,128)(2,1)S(1)} %get-tuple-element.39), channel_id=1, source_target_pairs={{0,96},{32,64},{64,32},{96,0},{1,97},{33,65},{65,33},{97,1},{2,98}... | collective-permute-start | bytes 786440 | tf_op jit(solution)/shard_map/ppermute | solution.py:20
  47.9 12.1 %collective-permute-start.6 = (bf16[8,32,512]{2,1,0:T(8,128)(2,1)S(1)}, bf16[8,32,512]{2,1,0:T(8,128)(2,1)S(1)}, u32[]{:S(2)}, u32[]{:S(2)}) collective-permute-start(bf16[8,32,512]{2,1,0:T(8,128)(2,1)S(1)} %get-tuple-element.40), channel_id=1, source_target_pairs={{0,32},{32,0},{64,96},{96,64},{1,33},{33,1},{65,97},{97,65},{2,34}... | collective-permute-start | bytes 786440 | tf_op jit(solution)/shard_map/ppermute | solution.py:20
  57.9 20.6 %collective-permute-start.14 = (bf16[2,256,896]{2,1,0:T(8,128)(2,1)S(1)}, bf16[2,256,896]{2,1,0:T(8,128)(2,1)S(1)}, u32[]{:S(2)}, u32[]{:S(2)}) collective-permute-start(bf16[2,256,896]{2,1,0:T(8,128)(2,1)S(1)} %pad_maximum_fusion.11), channel_id=1, source_target_pairs={{0,12},{4,8},{8,4},{12,0},{1,13},{5,9},{9,5},{13,1},{2,14},{6,10},... | collective-permute-start | bytes 2752520 | tf_op jit(solution)/shard_map/ppermute | solution.py:20
  60.0 10.5 %collective-permute-start.12 = (bf16[2,8,32,512]{3,2,1,0:T(8,128)(2,1)S(1)}, bf16[2,8,32,512]{3,2,1,0:T(8,128)(2,1)S(1)}, u32[]{:S(2)}, u32[]{:S(2)}) collective-permute-start(bf16[2,8,32,512]{3,2,1,0:T(8,128)(2,1)S(1)} %pad_maximum_fusion.17), channel_id=1, source_target_pairs={{0,32},{32,0},{64,96},{96,64},{1,33},{33,1},{65,97},{97,65},{2,34}... | collective-permute-start | bytes 1572872 | tf_op jit(solution)/shard_map/ppermute | solution.py:20
  60.2 23.1 %collective-permute-start.20 = (bf16[512,896]{1,0:T(8,128)(2,1)S(1)}, bf16[512,896]{1,0:T(8,128)(2,1)S(1)}, u32[]{:S(2)}, u32[]{:S(2)}) collective-permute-start(bf16[512,896]{1,0:T(8,128)(2,1)S(1)} %get-tuple-element.24), channel_id=1, source_target_pairs={{0,2},{2,0},{1,3},{3,1},{4,6},{6,4},{5,7},{7,5},{8,10},{10,8},{9,1... | collective-permute-start | bytes 2752520 | tf_op jit(solution)/shard_map/ppermute | solution.py:20
  70.6 10.7 %collective-permute-start.8 = (bf16[2,8,32,512]{3,2,1,0:T(8,128)(2,1)S(1)}, bf16[2,8,32,512]{3,2,1,0:T(8,128)(2,1)S(1)}, u32[]{:S(2)}, u32[]{:S(2)}) collective-permute-start(bf16[2,8,32,512]{3,2,1,0:T(8,128)(2,1)S(1)} %pad_maximum_fusion.15), channel_id=1, source_target_pairs={{0,96},{32,64},{64,32},{96,0},{1,97},{33,65},{65,33},{97,1},{2,98}... | collective-permute-start | bytes 1572872 | tf_op jit(solution)/shard_map/ppermute | solution.py:20
  72.6 9.1 %collective-permute-start.18 = (bf16[4,256,896]{2,1,0:T(8,128)(2,1)S(1)}, bf16[4,256,896]{2,1,0:T(8,128)(2,1)S(1)}, u32[]{:S(2)}, u32[]{:S(2)}) collective-permute-start(bf16[4,256,896]{2,1,0:T(8,128)(2,1)S(1)} %pad_maximum_fusion.3), channel_id=1, source_target_pairs={{0,1},{1,0},{2,3},{3,2},{4,5},{5,4},{6,7},{7,6},{8,9},{9,8},{10,11... | collective-permute-start | bytes 5505032 | tf_op jit(solution)/shard_map/ppermute | solution.py:20
  78.8 4.0 %collective-permute-start.15 = (bf16[4,256,896]{2,1,0:T(8,128)(2,1)S(1)}, bf16[4,256,896]{2,1,0:T(8,128)(2,1)S(1)}, u32[]{:S(2)}, u32[]{:S(2)}) collective-permute-start(bf16[4,256,896]{2,1,0:T(8,128)(2,1)S(1)} %pad_maximum_fusion.2), channel_id=1, source_target_pairs={{0,1},{1,0},{2,3},{3,2},{4,5},{5,4},{6,7},{7,6},{8,9},{9,8},{10,11... | collective-permute-start | bytes 5505032 | tf_op jit(solution)/shard_map/ppermute | solution.py:20
  88.7 28.2 %collective-permute-start.23 = (bf16[1024,896]{1,0:T(8,128)(2,1)S(1)}, bf16[1024,896]{1,0:T(8,128)(2,1)S(1)}, u32[]{:S(2)}, u32[]{:S(2)}) collective-permute-start(bf16[1024,896]{1,0:T(8,128)(2,1)S(1)} %fusion.16), channel_id=1, source_target_pairs={{0,1},{1,0},{2,3},{3,2},{4,5},{5,4},{6,7},{7,6},{8,9},{9,8},{10,11... | collective-permute-start | bytes 5505032 | tf_op jit(solution)/shard_map/ppermute | solution.py:20
  91.2 23.3 %collective-permute-start.27 = (bf16[512,896]{1,0:T(8,128)(2,1)S(1)}, bf16[512,896]{1,0:T(8,128)(2,1)S(1)}, u32[]{:S(2)}, u32[]{:S(2)}) collective-permute-start(bf16[512,896]{1,0:T(8,128)(2,1)S(1)} %convolution_convert_fusion), channel_id=1, source_target_pairs={{0,2},{2,0},{1,3},{3,1},{4,6},{6,4},{5,7},{7,5},{8,10},{10,8},{9,1... | collective-permute-start | bytes 2752520 | tf_op jit(solution)/shard_map/ppermute | solution.py:20
  94.7 24.8 %collective-permute-start.21 = (bf16[1024,896]{1,0:T(8,128)(2,1)S(1)}, bf16[1024,896]{1,0:T(8,128)(2,1)S(1)}, u32[]{:S(2)}, u32[]{:S(2)}) collective-permute-start(bf16[1024,896]{1,0:T(8,128)(2,1)S(1)} %fusion.13), channel_id=1, source_target_pairs={{0,1},{1,0},{2,3},{3,2},{4,5},{5,4},{6,7},{7,6},{8,9},{9,8},{10,11... | collective-permute-start | bytes 5505032 | tf_op jit(solution)/shard_map/ppermute | solution.py:20
  94.8 38.8 %collective-permute-start.28 = (bf16[512,896]{1,0:T(8,128)(2,1)S(1)}, bf16[512,896]{1,0:T(8,128)(2,1)S(1)}, u32[]{:S(2)}, u32[]{:S(2)}) collective-permute-start(bf16[512,896]{1,0:T(8,128)(2,1)S(1)} %convolution_convert_fusion.1), channel_id=1, source_target_pairs={{0,2},{2,0},{1,3},{3,1},{4,6},{6,4},{5,7},{7,5},{8,10},{10,8},{9,1... | collective-permute-start | bytes 2752520 | tf_op jit(solution)/shard_map/ppermute | solution.py:20
  119.4 21.3 %collective-permute-start.24 = (bf16[2,256,896]{2,1,0:T(8,128)(2,1)S(1)}, bf16[2,256,896]{2,1,0:T(8,128)(2,1)S(1)}, u32[]{:S(2)}, u32[]{:S(2)}) collective-permute-start(bf16[2,256,896]{2,1,0:T(8,128)(2,1)S(1)} %fusion.19), channel_id=1, source_target_pairs={{0,4},{4,0},{8,12},{12,8},{1,5},{5,1},{9,13},{13,9},{2,6},{6,2},{1... | collective-permute-start | bytes 2752520 | tf_op jit(solution)/shard_map/ppermute | solution.py:20
  121.8 15.5 %copy-start = (f32[1024,896]{1,0:T(8,128)}, f32[1024,896]{1,0:T(8,128)S(1)}, u32[]{:S(2)}) copy-start(f32[1024,896]{1,0:T(8,128)S(1)} %convert_add_fusion.1) | copy-start | bytes 11010052
  121.9 24.1 %collective-permute-start.22 = (bf16[2,256,896]{2,1,0:T(8,128)(2,1)S(1)}, bf16[2,256,896]{2,1,0:T(8,128)(2,1)S(1)}, u32[]{:S(2)}, u32[]{:S(2)}) collective-permute-start(bf16[2,256,896]{2,1,0:T(8,128)(2,1)S(1)} %bitcast.166), channel_id=1, source_target_pairs={{0,12},{4,8},{8,4},{12,0},{1,13},{5,9},{9,5},{13,1},{2,14},{6,10},... | collective-permute-start | bytes 2752520 | tf_op jit(solution)/shard_map/ppermute | solution.py:20
  137.3 8.7 %slice-start = ((f32[1024,896]{1,0:T(8,128)}), f32[512,896]{1,0:T(8,128)S(1)}, s32[]{:S(2)}) async-start(f32[1024,896]{1,0:T(8,128)} %copy-done), calls=%async_computation | async-start | bytes 3670016 | tf_op jit(solution)/shard_map/slice | solution.py:187
  140.9 13.4 %collective-permute-start.26 = (bf16[256,896]{1,0:T(8,128)(2,1)S(1)}, bf16[256,896]{1,0:T(8,128)(2,1)S(1)}, u32[]{:S(2)}, u32[]{:S(2)}) collective-permute-start(bf16[256,896]{1,0:T(8,128)(2,1)S(1)} %fusion.21), channel_id=1, source_target_pairs={{0,12},{4,8},{8,4},{12,0},{1,13},{5,9},{9,5},{13,1},{2,14},{6,10},... | collective-permute-start | bytes 1376264 | tf_op jit(solution)/shard_map/ppermute | solution.py:20
  146.3 9.0 %collective-permute-start.25 = (bf16[256,896]{1,0:T(8,128)(2,1)S(1)}, bf16[256,896]{1,0:T(8,128)(2,1)S(1)}, u32[]{:S(2)}, u32[]{:S(2)}) collective-permute-start(bf16[256,896]{1,0:T(8,128)(2,1)S(1)} %fusion.20), channel_id=1, source_target_pairs={{0,4},{4,0},{8,12},{12,8},{1,5},{5,1},{9,13},{13,9},{2,6},{6,2},{1... | collective-permute-start | bytes 1376264 | tf_op jit(solution)/shard_map/ppermute | solution.py:20
  154.3 1.0 copy-start.3
  155.3 0.8 copy-start.4

commit v3 on v0

v3 whole, which is shorter than its diff:
```python
import functools
import math

import jax
import jax.numpy as jnp
from jax import lax
from jax.experimental import pallas as pl
from jax.experimental.pallas import tpu as pltpu
from jax.sharding import Mesh, PartitionSpec as P

NAMES = ("x", "zh", "y", "zl", "core")
SIZES = {"x": 4, "zh": 2, "y": 4, "zl": 2, "core": 2}
BF16, F32 = jnp.bfloat16, jnp.float32
VMEM = pl.BlockSpec(memory_space=pltpu.VMEM)

STEP = {"b": lambda i: i ^ 1, "a": lambda i: 3 - i, "ab": lambda i: i ^ 2}


def swap(value, axis, step=None):
    move = STEP[step] if step else lambda i: 1 - i
    return lax.ppermute(value, axis, [(i, move(i)) for i in range(SIZES[axis])])


def around(axis):
    at = lax.axis_index(axis)
    return [at, at ^ 1, 3 - at, at ^ 2]


def after(value, *others):
    return lax.optimization_barrier((value,) + others)[0]


def gelu_parts(pre_float):
    cumulative = 0.5 * (1.0 + jax.scipy.special.erf(pre_float / math.sqrt(2.0)))
    density = jnp.exp(-0.5 * pre_float * pre_float) / math.sqrt(2.0 * math.pi)
    return (pre_float * cumulative, cumulative + pre_float * density)


def split_kernel(grad, near, away):
    size = near.shape[2] // 2
    zl, core = lax.axis_index("zl"), lax.axis_index("core")
    for out, k in ((near, core), (away, 1 - core)):
        for n, y in enumerate(around("y")):
            for z, other in enumerate((zl, 1 - zl)):
                at = pl.multiple_of(((y * 2 + other) * 2 + k) * size, size)
                out[n, :, z * size : (z + 1) * size] = grad[:, pl.ds(at, size)]


def split_grad(grad):
    rows, width = grad.shape
    piece = jax.ShapeDtypeStruct((4, rows, width // 8), BF16)
    return pl.pallas_call(split_kernel, in_specs=[VMEM], out_specs=[VMEM] * 2, out_shape=[piece, piece])(grad)


def token_blocks(rows):
    zh = lax.axis_index("zh")
    return [pl.multiple_of((x * 2 + z) * rows, rows) for x in around("x") for z in (zh, 1 - zh)]


def hidden_kernel(pre, left, right, slope_l, slope_r):
    rows, half = pre.shape[0] // 8, pre.shape[1] // 2
    for n, at in enumerate(token_blocks(rows)):
        value, slope = gelu_parts(pre[pl.ds(at, rows), :].astype(F32))
        here = pl.ds(n * rows, rows)
        left[here, :] = value[:, :half].astype(BF16)
        right[here, :] = value[:, half:].astype(BF16)
        slope_l[here, :] = slope[:, :half]
        slope_r[here, :] = slope[:, half:]


def make_hidden(pre):
    tokens, units = pre.shape
    out = [jax.ShapeDtypeStruct((tokens, units // 2), t) for t in (BF16, BF16, F32, F32)]
    return pl.pallas_call(hidden_kernel, in_specs=[VMEM], out_specs=[VMEM] * 4, out_shape=out)(pre)


def finish_kernel(slope_l, slope_r, own_l, own_r, far_l, far_r, out):
    rows, half = out.shape[0] // 8, out.shape[1] // 2
    for n, at in enumerate(token_blocks(rows)):
        here = pl.ds(n * rows, rows)
        left = (own_l[here, :] + far_l[here, :].astype(F32)) * slope_l[here, :]
        right = (own_r[here, :] + far_r[here, :].astype(F32)) * slope_r[here, :]
        out[pl.ds(at, rows), :half] = left.astype(BF16)
        out[pl.ds(at, rows), half:] = right.astype(BF16)


def finish(*args):
    tokens, half = args[0].shape
    out = jax.ShapeDtypeStruct((tokens, 2 * half), BF16)
    return pl.pallas_call(finish_kernel, in_specs=[VMEM] * 6, out_specs=VMEM, out_shape=out)(*args)


def outer(g, h):
    return lax.dot_general(g, h, (((0,), (0,)), ((), ())), preferred_element_type=F32)


def inner(g, w):
    return jnp.dot(g, w, preferred_element_type=F32)


def shards(grad_out, pre_act, weight):
    rows, width = grad_out.shape[1:]
    tokens, units = pre_act.shape
    half = units // 2
    own_rows = weight.shape[0]

    near, away = split_grad(grad_out[0])
    sibling = swap(away, "core")
    weight_l, weight_r = weight[:, :half], weight[:, half:]
    other_l = swap(weight_l, "zl")
    hidden_l, hidden_r, slope_l, slope_r = make_hidden(after(pre_act, near))

    both = jnp.stack([near, after(sibling, hidden_l)])
    grad = jnp.stack([both[:, 0]] + [swap(both[:, s], "y", m) for s, m in ((1, "b"), (2, "a"), (3, "ab"))], 1)
    grad = grad.reshape(8, rows, 2 * own_rows)

    near_o, near_t = grad[..., own_rows:], grad[..., :own_rows]
    near_ob, near_ta = swap(near_o, "x", "b"), swap(near_t, "x", "a")
    hidden_l, hidden_r = after(hidden_l, grad), after(hidden_r, grad)
    hidden_lb, hidden_ra = swap(hidden_l, "y", "b"), swap(hidden_r, "y", "a")
    near_ob, near_ta, hidden_lb, hidden_ra, other_l, grad = lax.optimization_barrier(
        (near_ob, near_ta, hidden_lb, hidden_ra, other_l, grad)
    )
    near_o, near_t = jnp.stack([near_o, near_ob]), jnp.stack([near_t, near_ta])
    hidden_l, hidden_r = jnp.stack([hidden_l, hidden_lb]), jnp.stack([hidden_r, hidden_ra])
    grad_far = swap(grad, "zh")
    near_oa, near_tb = swap(near_o, "x", "a"), swap(near_t, "x", "b")
    hidden_la, hidden_rb = swap(hidden_l, "y", "a"), swap(hidden_r, "y", "b")
    near_oa, near_tb, grad_far = lax.optimization_barrier((near_oa, near_tb, grad_far))
    far_o, far_t = grad_far[..., own_rows:], grad_far[..., :own_rows]
    far_ob, far_ta = swap(far_o, "x", "b"), swap(far_t, "x", "a")
    other_r = swap(after(weight_r, grad_far), "zl")
    far_ob, far_ta, hidden_la, hidden_rb = lax.optimization_barrier((far_ob, far_ta, hidden_la, hidden_rb))
    far_o, far_t = jnp.stack([far_o, far_ob]), jnp.stack([far_t, far_ta])
    far_oa, far_tb = swap(far_o, "x", "a"), swap(far_t, "x", "b")
    hidden_l = jnp.concatenate([hidden_l, hidden_la])
    hidden_r = jnp.stack([hidden_r[0], hidden_rb[0], hidden_r[1], hidden_rb[1]])
    hidden_l = jnp.concatenate([hidden_l, swap(hidden_l, "core")]).reshape(8 * tokens, half)
    hidden_r = jnp.concatenate([hidden_r, swap(hidden_r, "core")]).reshape(8 * tokens, half)

    grad_o = [near_o[0], far_o[0], near_o[1], far_o[1], near_oa[0], far_oa[0], near_oa[1], far_oa[1]]
    grad_t = [near_t[0], far_t[0], near_tb[0], far_tb[0], near_t[1], far_t[1], near_tb[1], far_tb[1]]
    grad_other = jnp.stack(grad_o, 1).reshape(8 * tokens, own_rows)
    grad_own = jnp.stack(grad_t, 1).reshape(8 * tokens, own_rows)
    grad_other, grad_own, hidden_l, hidden_r, other_l, other_r = lax.optimization_barrier(
        (grad_other, grad_own, hidden_l, hidden_r, other_l, other_r)
    )

    grad_both = jnp.concatenate([grad_own, grad_other], 1)
    w_l = jnp.concatenate([weight_l, other_l])
    w_r = jnp.concatenate([weight_r, other_r])
    edge = 4 * tokens
    away_l = inner(grad_both[edge:], w_l).astype(BF16)
    away_r = inner(after(grad_both, away_l)[edge:], w_r).astype(BF16)
    sent_l = outer(after(grad_other, away_r), hidden_l).astype(BF16)
    sent_r = outer(after(grad_other, sent_l), hidden_r).astype(BF16)
    got_l, got_r = swap(sent_l, "zl"), swap(sent_r, "zl")
    back_l, back_r = swap(away_l, "core"), swap(away_r, "core")
    back_l = after(back_l, sent_r)
    part_l = inner(grad_both[:edge], w_l) + back_l.astype(F32)
    back_r = after(back_r, part_l)
    part_r = inner(grad_both[:edge], w_r) + back_r.astype(F32)
    part_l = part_l.reshape(2, 2, tokens, half)
    part_r = part_r.reshape(2, 2, tokens, half)
    next_l, next_r = swap(part_l[1].astype(BF16), "y", "a"), swap(part_r[:, 1].astype(BF16), "y", "b")
    kept_l = outer(after(grad_own, part_r), hidden_l)
    kept_r = outer(after(grad_own, kept_l), hidden_r)
    next_l, next_r, kept_l, kept_r = lax.optimization_barrier((next_l, next_r, kept_l, kept_r))
    part_l = part_l[0] + next_l.astype(F32)
    part_r = part_r[:, 0] + next_r.astype(F32)
    far_l, far_r = swap(part_l[1].astype(BF16), "y", "b"), swap(part_r[1].astype(BF16), "y", "a")
    grad_pre = finish(slope_l, slope_r, part_l[0], part_r[0], far_l, far_r)
    kept = jnp.concatenate([kept_l + got_l.astype(F32), kept_r + got_r.astype(F32)], 1)
    return (grad_pre, kept.astype(BF16))


def solution(mesh):
    sizes = tuple(SIZES[name] for name in NAMES)
    inner_mesh = Mesh(mesh.devices.reshape(sizes), NAMES)
    col, row = ("y", "zl", "core"), ("x", "zh")
    in_specs = (P(col, row, None), P(col, row), P(col, row))
    out_specs = (P(col, row), P(col, row))
    return jax.shard_map(shards, mesh=inner_mesh, in_specs=in_specs, out_specs=out_specs, check_vma=False)
```

time: 584 us -> 137 us (0.23)
  waiting for transfers between devices: 463 us -> 67.9 us
  blocking collectives: 54.8 us -> 0 us
  starting transfers between devices: 0.12 us -> 29.4 us
  between operations: 13.8 us -> 1.13 us
  matrix products: 29.8 us -> 18.7 us
  local copies, waits for them, and re-layouts: 16.5 us -> 6.98 us
  Pallas kernels: 0 us -> 8.64 us
    reduce_scatter x1 -> x0, waiting for transfers between devices: 296 us -> none  [shards(): lax.psum_scatter(jnp.dot(row_slice, down_weight, preferred_element_type=j...]
    all_gather x2 -> x0, waiting for transfers between devices: 167 us -> none  [the longest x1 90.4 us: shards(): lax.all_gather(hidden, 'col', axis=0, tiled=True)]
    ppermute x0 -> x29, waiting for transfers between devices: none -> 67.9 us  [swap(): return lax.ppermute(value, axis, [(i, move(i)) for i in range(SIZES[axis])])]
    all_to_all x1 -> x0, blocking collectives: 54.8 us -> none  [shards(): lax.all_to_all(token_block, 'col', split_axis=1, concat_axis=0, tiled=True)]
    ppermute x0 -> x29, starting transfers between devices: none -> 29.4 us  [swap(): return lax.ppermute(value, axis, [(i, move(i)) for i in range(SIZES[axis])])]
    dot_general x2 -> x8, matrix products: 29.8 us -> 18.7 us  [the longest x4 9.37 us: outer(): lax.dot_general(g, h, (((0,), (0,)), ((), ())), preferred_element_type=F32)]
    pallas_call x0 -> x3, Pallas kernels: none -> 8.64 us  [the longest x1 3.4 us: finish(): pl.pallas_call(finish_kernel, in_specs=[VMEM] * 6, out_specs=VMEM, out_sh...]
    all_to_all x1 -> x0, local copies, waits for them, and re-layouts: 6.37 us -> none  [shards(): lax.all_to_all(token_block, 'col', split_axis=1, concat_axis=0, tiled=True)]
  transfers between devices with their start and end apart: 3 -> 29, of which waited for: 3 -> 19; matrix products, arithmetic and copies ran while one was open for 0% -> 19% of each run, Pallas kernels for 0% -> 2%
where the time goes in v3:
time: 137 us; the launch traced here: 136 us
  waiting for transfers between devices  67.9 us (50%)
  starting transfers between devices  29.4 us (21%)
  matrix products  18.7 us (14%)
  Pallas kernels  8.64 us (6%)
  local copies, waits for them, and re-layouts  6.98 us (5%)
  other arithmetic  3.6 us (3%)
    ppermute x29, waiting for transfers between devices, swap(): return lax.ppermute(value, axis, [(i, move(i)) for i in range(SIZES[axis])])  67.9 us
    ppermute x29, starting transfers between devices, swap(): return lax.ppermute(value, axis, [(i, move(i)) for i in range(SIZES[axis])])  29.4 us
    dot_general x4, matrix products, outer(): lax.dot_general(g, h, (((0,), (0,)), ((), ())), preferred_element_type=F32)  9.37 us
    dot_general x4, matrix products, inner(): return jnp.dot(g, w, preferred_element_type=F32)  9.37 us
    pallas_call x1, Pallas kernels, finish(): pl.pallas_call(finish_kernel, in_specs=[VMEM] * 6, out_specs=VMEM, out_sh...  3.4 us
    pallas_call x1, Pallas kernels, make_hidden(): pl.pallas_call(hidden_kernel, in_specs=[VMEM], out_specs=[VMEM] * 4, out_...  3.35 us
  transfers between devices with their start and end apart: 29, of which 19 were waited for; matrix products, arithmetic and copies ran while one was open for 19% of the time, Pallas kernels for 2%

profile of v3, /device:TPU:0, one launch (start us, length us, event | category | flops | bytes accessed | tf_op | source)
XLA Modules:
  0.0 136.4 jit_solution(14192229949924197772)
XLA Ops:
  0.6 1.9 %shard_map.50 = (bf16[4,32,1024]{2,1,0:T(8,128)(2,1)}, bf16[4,32,1024]{2,1,0:T(8,128)(2,1)}) custom-call(bf16[32,8192]{1,0:T(8,128)(2,1)} %bitcast.135), custom_call_target="tpu_custom_call" | custom-call | tf_op jit(solution)/shard_map/pallas_call | solution.py:52
  2.5 1.6 %fusion.37 = (bf16[512,896]{1,0:T(8,128)(2,1)S(1)}, bf16[512,896]{1,0:T(8,128)(2,1)S(1)}) fusion(bf16[512,1792]{1,0:T(8,128)(2,1)} %param.5), kind=kLoop, calls=%fused_computation.90 | loop fusion | bytes 3670016 | tf_op jit(solution)/shard_map/slice | solution.py:109
  4.2 2.1 %collective-permute-start.8 = (bf16[512,896]{1,0:T(8,128)(2,1)S(1)}, bf16[512,896]{1,0:T(8,128)(2,1)S(1)}, u32[]{:S(2)}, u32[]{:S(2)}) collective-permute-start(bf16[512,896]{1,0:T(8,128)(2,1)S(1)} %get-tuple-element.85), channel_id=1, source_target_pairs={{0,2},{2,0},{1,3},{3,1},{4,6},{6,4},{5,7},{7,5},{8,10},{10,8},{9,1... | collective-permute-start | bytes 2752520 | tf_op jit(solution)/shard_map/ppermute | solution.py:21
  6.2 3.4 %shard_map.51 = (bf16[256,896]{1,0:T(8,128)(2,1)}, bf16[256,896]{1,0:T(8,128)(2,1)}, f32[256,896]{1,0:T(8,128)}, f32[256,896]{1,0:T(8,128)}) custom-call(bf16[256,1792]{1,0:T(8,128)(2,1)} %pre), custom_call_target="tpu_custom_call" | custom-call | tf_op jit(solution)/shard_map/pallas_call | solution.py:74
  9.7 1.7 %collective-permute-start.1 = (bf16[2,32,1024]{2,1,0:T(8,128)(2,1)S(1)}, bf16[2,32,1024]{2,1,0:T(8,128)(2,1)S(1)}, u32[]{:S(2)}, u32[]{:S(2)}) collective-permute-start(bf16[2,32,1024]{2,1,0:T(8,128)(2,1)S(1)} %get-tuple-element.102), channel_id=1, source_target_pairs={{0,4},{4,0},{8,12},{12,8},{1,5},{5,1},{9,13},{13,9},{2,6},{6,2},{1... | collective-permute-start | bytes 393224 | tf_op jit(solution)/shard_map/ppermute | solution.py:21
  11.3 2.9 %collective-permute-start.3 = (bf16[2,32,1024]{2,1,0:T(8,128)(2,1)S(1)}, bf16[2,32,1024]{2,1,0:T(8,128)(2,1)S(1)}, u32[]{:S(2)}, u32[]{:S(2)}) collective-permute-start(bf16[2,32,1024]{2,1,0:T(8,128)(2,1)S(1)} %get-tuple-element.103), channel_id=1, source_target_pairs={{0,8},{4,12},{8,0},{12,4},{1,9},{5,13},{9,1},{13,5},{2,10},{6,14},... | collective-permute-start | bytes 393224 | tf_op jit(solution)/shard_map/ppermute | solution.py:21
  14.5 1.3 collective-permute-done.1
  15.8 4.9 %collective-permute-done.3 = bf16[2,32,1024]{2,1,0:T(8,128)(2,1)S(1)} collective-permute-done((bf16[2,32,1024]{2,1,0:T(8,128)(2,1)S(1)}, bf16[2,32,1024]{2,1,0:T(8,128)(2,1)S(1)}, u32[]{:S(2)}, u32[]{:S(2)}) %collective-permute-start.3) | collective-permute-done | bytes 131104 | tf_op jit(solution)/shard_map/ppermute | solution.py:21
  20.7 2.3 %collective-permute-done.2 = bf16[2,32,1024]{2,1,0:T(8,128)(2,1)S(1)} collective-permute-done((bf16[2,32,1024]{2,1,0:T(8,128)(2,1)S(1)}, bf16[2,32,1024]{2,1,0:T(8,128)(2,1)S(1)}, u32[]{:S(2)}, u32[]{:S(2)}) %collective-permute-start.2) | collective-permute-done | bytes 131104 | tf_op jit(solution)/shard_map/ppermute | solution.py:21
  23.8 2.8 %collective-permute-start.5 = (bf16[8,32,512]{2,1,0:T(8,128)(2,1)S(1)}, bf16[8,32,512]{2,1,0:T(8,128)(2,1)S(1)}, u32[]{:S(2)}, u32[]{:S(2)}) collective-permute-start(bf16[8,32,512]{2,1,0:T(8,128)(2,1)S(1)} %get-tuple-element.99), channel_id=1, source_target_pairs={{0,96},{32,64},{64,32},{96,0},{1,97},{33,65},{65,33},{97,1},{2,98}... | collective-permute-start | bytes 786440 | tf_op jit(solution)/shard_map/ppermute | solution.py:21
  26.9 5.9 %collective-permute-done.5 = bf16[8,32,512]{2,1,0:T(8,128)(2,1)S(1)} collective-permute-done((bf16[8,32,512]{2,1,0:T(8,128)(2,1)S(1)}, bf16[8,32,512]{2,1,0:T(8,128)(2,1)S(1)}, u32[]{:S(2)}, u32[]{:S(2)}) %collective-permute-start.5) | collective-permute-done | bytes 262176 | tf_op jit(solution)/shard_map/ppermute | solution.py:21
  32.8 1.3 collective-permute-done.4
  34.0 1.1 collective-permute-done.6
  35.1 1.3 collective-permute-done.7
  36.5 2.8 %collective-permute-start.9 = (bf16[2,8,32,512]{3,2,1,0:T(8,128)(2,1)S(1)}, bf16[2,8,32,512]{3,2,1,0:T(8,128)(2,1)S(1)}, u32[]{:S(2)}, u32[]{:S(2)}) collective-permute-start(bf16[2,8,32,512]{3,2,1,0:T(8,128)(2,1)S(1)} %pad_maximum_fusion.13), channel_id=1, source_target_pairs={{0,96},{32,64},{64,32},{96,0},{1,97},{33,65},{65,33},{97,1},{2,98}... | collective-permute-start | bytes 1572872 | tf_op jit(solution)/shard_map/ppermute | solution.py:21
  39.7 3.6 %collective-permute-start.11 = (bf16[8,32,1024]{2,1,0:T(8,128)(2,1)S(1)}, bf16[8,32,1024]{2,1,0:T(8,128)(2,1)S(1)}, u32[]{:S(2)}, u32[]{:S(2)}) collective-permute-start(bf16[8,32,1024]{2,1,0:T(8,128)(2,1)S(1)} %bitcast.114), channel_id=1, source_target_pairs={{0,16},{16,0},{1,17},{17,1},{2,18},{18,2},{3,19},{19,3},{4,20},{20... | collective-permute-start | bytes 1572872 | tf_op jit(solution)/shard_map/ppermute | solution.py:21
  43.5 0.5 collective-permute-start.15
  44.1 1.0 collective-permute-start.14
  45.1 5.2 %collective-permute-done.9 = bf16[2,8,32,512]{3,2,1,0:T(8,128)(2,1)S(1)} collective-permute-done((bf16[2,8,32,512]{3,2,1,0:T(8,128)(2,1)S(1)}, bf16[2,8,32,512]{3,2,1,0:T(8,128)(2,1)S(1)}, u32[]{:S(2)}, u32[]{:S(2)}) %collective-permute-start.9) | collective-permute-done | bytes 524320 | tf_op jit(solution)/shard_map/ppermute | solution.py:21
  50.2 1.4 %collective-permute-done.10 = bf16[2,8,32,512]{3,2,1,0:T(8,128)(2,1)S(1)} collective-permute-done((bf16[2,8,32,512]{3,2,1,0:T(8,128)(2,1)S(1)}, bf16[2,8,32,512]{3,2,1,0:T(8,128)(2,1)S(1)}, u32[]{:S(2)}, u32[]{:S(2)}) %collective-permute-start.10) | collective-permute-done | bytes 524320 | tf_op jit(solution)/shard_map/ppermute | solution.py:21
  51.6 2.4 %collective-permute-done.11 = bf16[8,32,1024]{2,1,0:T(8,128)(2,1)S(1)} collective-permute-done((bf16[8,32,1024]{2,1,0:T(8,128)(2,1)S(1)}, bf16[8,32,1024]{2,1,0:T(8,128)(2,1)S(1)}, u32[]{:S(2)}, u32[]{:S(2)}) %collective-permute-start.11) | collective-permute-done | bytes 524320 | tf_op jit(solution)/shard_map/ppermute | solution.py:21
  54.2 1.2 collective-permute-start.13
  55.4 0.8 collective-permute-start.12
  56.3 5.6 %collective-permute-done.13 = bf16[8,32,512]{2,1,0:T(8,128)(2,1)S(1)} collective-permute-done((bf16[8,32,512]{2,1,0:T(8,128)(2,1)S(1)}, bf16[8,32,512]{2,1,0:T(8,128)(2,1)S(1)}, u32[]{:S(2)}, u32[]{:S(2)}) %collective-permute-start.13) | collective-permute-done | bytes 262176 | tf_op jit(solution)/shard_map/ppermute | solution.py:21
  61.9 1.9 %collective-permute-done.15 = bf16[2,256,896]{2,1,0:T(8,128)(2,1)S(1)} collective-permute-done((bf16[2,256,896]{2,1,0:T(8,128)(2,1)S(1)}, bf16[2,256,896]{2,1,0:T(8,128)(2,1)S(1)}, u32[]{:S(2)}, u32[]{:S(2)}) %collective-permute-start.15) | collective-permute-done | bytes 917536 | tf_op jit(solution)/shard_map/ppermute | solution.py:21
  63.7 1.4 %collective-permute-done.14 = bf16[2,256,896]{2,1,0:T(8,128)(2,1)S(1)} collective-permute-done((bf16[2,256,896]{2,1,0:T(8,128)(2,1)S(1)}, bf16[2,256,896]{2,1,0:T(8,128)(2,1)S(1)}, u32[]{:S(2)}, u32[]{:S(2)}) %collective-permute-start.14) | collective-permute-done | bytes 917536 | tf_op jit(solution)/shard_map/ppermute | solution.py:21
  65.2 1.1 collective-permute-start.16
  66.3 0.8 collective-permute-start.17
  67.8 0.6 collective-permute-start.19
  68.6 7.8 %collective-permute-done.17 = bf16[2,8,32,512]{3,2,1,0:T(8,128)(2,1)S(1)} collective-permute-done((bf16[2,8,32,512]{3,2,1,0:T(8,128)(2,1)S(1)}, bf16[2,8,32,512]{3,2,1,0:T(8,128)(2,1)S(1)}, u32[]{:S(2)}, u32[]{:S(2)}) %collective-permute-start.17) | collective-permute-done | bytes 524320 | tf_op jit(solution)/shard_map/ppermute | solution.py:21
  79.0 2.3 %fusion.16 = bf16[1024,896]{1,0:T(8,128)(2,1)S(1)} fusion(bf16[2048,1024]{1,0:T(8,128)(2,1)S(1)} %constant_dynamic-update-slice_fusion.5, bf16[512,896]{1,0:T(8,128)(2,1)S(1)} %collective-permute-done.8, bf16[512,896]{1,0:T(8,128)(2,1)S(1)} %get-tuple-element.85), kind=kOutput, calls=%fused_computation.24 | convolution fusion | flops 1883635712 | bytes 5767168 | tf_op jit(solution)/shard_map/dot_general | solution.py:98
  81.6 2.3 %fusion.13 = bf16[1024,896]{1,0:T(8,128)(2,1)S(1)} fusion(bf16[2048,1024]{1,0:T(8,128)(2,1)S(1)} %constant_dynamic-update-slice_fusion.5, bf16[512,896]{1,0:T(8,128)(2,1)S(1)} %collective-permute-done.20, bf16[512,896]{1,0:T(8,128)(2,1)S(1)} %get-tuple-element.66), kind=kOutput, calls=%fused_computation.23 | convolution fusion | flops 1883635712 | bytes 5767168 | tf_op jit(solution)/shard_map/dot_general | solution.py:98
  84.0 0.6 collective-permute-start.23
  84.5 2.3 %convolution_convert_fusion.1 = bf16[512,896]{1,0:T(8,128)(2,1)S(1)} fusion(bf16[2048,512]{1,0:T(8,128)(2,1)S(1)} %bitcast.110, bf16[2048,896]{1,0:T(8,128)(2,1)S(1)} %bitcast.126), kind=kOutput, calls=%fused_computation.26 | convolution fusion | flops 1879506944 | bytes 6684672 | tf_op jit(solution)/shard_map/dot_general | solution.py:94
  87.0 2.3 %convolution_convert_fusion = bf16[512,896]{1,0:T(8,128)(2,1)S(1)} fusion(bf16[2048,512]{1,0:T(8,128)(2,1)S(1)} %bitcast.111, bf16[2048,896]{1,0:T(8,128)(2,1)S(1)} %bitcast.141), kind=kOutput, calls=%fused_computation.25 | convolution fusion | flops 1879506944 | bytes 6684672 | tf_op jit(solution)/shard_map/dot_general | solution.py:94
  89.3 2.1 %collective-permute-start.28 = (bf16[512,896]{1,0:T(8,128)(2,1)S(1)}, bf16[512,896]{1,0:T(8,128)(2,1)S(1)}, u32[]{:S(2)}, u32[]{:S(2)}) collective-permute-start(bf16[512,896]{1,0:T(8,128)(2,1)S(1)} %convolution_convert_fusion), channel_id=1, source_target_pairs={{0,2},{2,0},{1,3},{3,1},{4,6},{6,4},{5,7},{7,5},{8,10},{10,8},{9,1... | collective-permute-start | bytes 2752520 | tf_op jit(solution)/shard_map/ppermute | solution.py:21
  91.4 2.4 %convert_add_fusion.1 = f32[1024,896]{1,0:T(8,128)S(1)} fusion(bf16[1024,896]{1,0:T(8,128)(2,1)S(1)} %collective-permute-done.21, bf16[2048,1024]{1,0:T(8,128)(2,1)S(1)} %constant_dynamic-update-slice_fusion.5, bf16[512,896]{1,0:T(8,128)(2,1)S(1)} %collective-permute-done.8, bf16[512,896]{1,0:T(8,128)(2,1)S(1)} %get-tuple-element.85), kind=kOutput, calls=%fused_computation.2 | convolution fusion | flops 1884553216 | bytes 9437184 | tf_op jit(solution)/shard_map/dot_general | solution.py:98
  93.8 2.4 %convert_add_fusion = f32[1024,896]{1,0:T(8,128)S(1)} fusion(bf16[1024,896]{1,0:T(8,128)(2,1)S(1)} %collective-permute-done.23, bf16[2048,1024]{1,0:T(8,128)(2,1)S(1)} %constant_dynamic-update-slice_fusion.5, bf16[512,896]{1,0:T(8,128)(2,1)S(1)} %collective-permute-done.20, bf16[512,896]{1,0:T(8,128)(2,1)S(1)} %get-tuple-element.66), kind=kOutput, calls=%fused_computation.1 | convolution fusion | flops 1884553216 | bytes 9437184 | tf_op jit(solution)/shard_map/dot_general | solution.py:98
  96.4 1.2 collective-permute-start.22
  97.7 2.3 %fusion.39 = f32[512,896]{1,0:T(8,128)S(1)} fusion(bf16[2048,512]{1,0:T(8,128)(2,1)S(1)} %bitcast.107, bf16[2048,896]{1,0:T(8,128)(2,1)S(1)} %bitcast.127), kind=kOutput, calls=%fused_computation.92 | convolution fusion | flops 1879048192 | bytes 7602176 | tf_op jit(solution)/shard_map/dot_general | solution.py:94
  100.0 2.3 %fusion.40 = f32[512,896]{1,0:T(8,128)S(1)} fusion(bf16[2048,512]{1,0:T(8,128)(2,1)S(1)} %bitcast.108, bf16[2048,896]{1,0:T(8,128)(2,1)S(1)} %bitcast.142), kind=kOutput, calls=%fused_computation.93 | convolution fusion | flops 1879048192 | bytes 7602176 | tf_op jit(solution)/shard_map/dot_general | solution.py:94
  102.4 17.0 %collective-permute-done.22 = bf16[2,256,896]{2,1,0:T(8,128)(2,1)S(1)} collective-permute-done((bf16[2,256,896]{2,1,0:T(8,128)(2,1)S(1)}, bf16[2,256,896]{2,1,0:T(8,128)(2,1)S(1)}, u32[]{:S(2)}, u32[]{:S(2)}) %collective-permute-start.22) | collective-permute-done | bytes 917536 | tf_op jit(solution)/shard_map/ppermute | solution.py:21
  119.6 1.8 %collective-permute-start.26 = (bf16[256,896]{1,0:T(8,128)(2,1)S(1)}, bf16[256,896]{1,0:T(8,128)(2,1)S(1)}, u32[]{:S(2)}, u32[]{:S(2)}) collective-permute-start(bf16[256,896]{1,0:T(8,128)(2,1)S(1)} %fusion.21), channel_id=1, source_target_pairs={{0,12},{4,8},{8,4},{12,0},{1,13},{5,9},{9,5},{13,1},{2,14},{6,10},... | collective-permute-start | bytes 1376264 | tf_op jit(solution)/shard_map/ppermute | solution.py:21
  121.8 1.0 slice_bitcast_fusion.1.own_l
  122.8 6.1 %collective-permute-done.28 = bf16[512,896]{1,0:T(8,128)(2,1)S(1)} collective-permute-done((bf16[512,896]{1,0:T(8,128)(2,1)S(1)}, bf16[512,896]{1,0:T(8,128)(2,1)S(1)}, u32[]{:S(2)}, u32[]{:S(2)}) %collective-permute-start.28) | collective-permute-done | bytes 917536 | tf_op jit(solution)/shard_map/ppermute | solution.py:21
  129.3 1.0 slice_bitcast_fusion.own_r
  130.3 1.4 pad_maximum_fusion.5
  133.0 3.4 %shard_map.52 = bf16[256,1792]{1,0:T(8,128)(2,1)} custom-call(f32[256,896]{1,0:T(8,128)} %get-tuple-element.45.slope_l, f32[256,896]{1,0:T(8,128)} %get-tuple-element.46.slope_r, f32[256,896]{1,0:T(8,128)} %slice_bitcast_fusion.1.own_l, f32[256,896]{1,0:T(8,128)} %slice_bitcast_fusion.own_r, bf16[256,896]{1,0:T(8,128)(2,1)} %copy-done.4, ...), custom_call_target="tpu_custom_call" | custom-call | tf_op jit(solution)/shard_map/pallas_call | solution.py:90
  (83 shorter events, 8.6 us)
Async XLA Ops:
  2.5 7.1 %copy-start.5 = (bf16[4,32,1024]{2,1,0:T(8,128)(2,1)S(1)}, bf16[4,32,1024]{2,1,0:T(8,128)(2,1)}, u32[]{:S(2)}) copy-start(bf16[4,32,1024]{2,1,0:T(8,128)(2,1)} %get-tuple-element.43) | copy-start | bytes 786436
  2.5 7.1 %collective-permute-start = (bf16[4,32,1024]{2,1,0:T(8,128)(2,1)}, bf16[4,32,1024]{2,1,0:T(8,128)(2,1)S(1)}, u32[]{:S(2)}, u32[]{:S(2)}) collective-permute-start(bf16[4,32,1024]{2,1,0:T(8,128)(2,1)} %get-tuple-element.47), channel_id=1, source_target_pairs={{0,1},{1,0},{2,3},{3,2},{4,5},{5,4},{6,7},{7,6},{8,9},{9,8},{10,11... | collective-permute-start | bytes 786440 | tf_op jit(solution)/shard_map/ppermute | solution.py:21
  4.2 32.3 %collective-permute-start.8 = (bf16[512,896]{1,0:T(8,128)(2,1)S(1)}, bf16[512,896]{1,0:T(8,128)(2,1)S(1)}, u32[]{:S(2)}, u32[]{:S(2)}) collective-permute-start(bf16[512,896]{1,0:T(8,128)(2,1)S(1)} %get-tuple-element.85), channel_id=1, source_target_pairs={{0,2},{2,0},{1,3},{3,1},{4,6},{6,4},{5,7},{7,5},{8,10},{10,8},{9,1... | collective-permute-start | bytes 2752520 | tf_op jit(solution)/shard_map/ppermute | solution.py:21
  9.6 13.5 %copy-start.1 = (bf16[256,896]{1,0:T(8,128)(2,1)S(1)}, bf16[256,896]{1,0:T(8,128)(2,1)}, u32[]{:S(2)}) copy-start(bf16[256,896]{1,0:T(8,128)(2,1)} %get-tuple-element.50) | copy-start | bytes 1376260
  9.6 13.6 %copy-start.2 = (bf16[256,896]{1,0:T(8,128)(2,1)S(1)}, bf16[256,896]{1,0:T(8,128)(2,1)}, u32[]{:S(2)}) copy-start(bf16[256,896]{1,0:T(8,128)(2,1)} %get-tuple-element.52) | copy-start | bytes 1376260
  9.7 6.1 %collective-permute-start.1 = (bf16[2,32,1024]{2,1,0:T(8,128)(2,1)S(1)}, bf16[2,32,1024]{2,1,0:T(8,128)(2,1)S(1)}, u32[]{:S(2)}, u32[]{:S(2)}) collective-permute-start(bf16[2,32,1024]{2,1,0:T(8,128)(2,1)S(1)} %get-tuple-element.102), channel_id=1, source_target_pairs={{0,4},{4,0},{8,12},{12,8},{1,5},{5,1},{9,13},{13,9},{2,6},{6,2},{1... | collective-permute-start | bytes 393224 | tf_op jit(solution)/shard_map/ppermute | solution.py:21
  11.3 9.4 %collective-permute-start.3 = (bf16[2,32,1024]{2,1,0:T(8,128)(2,1)S(1)}, bf16[2,32,1024]{2,1,0:T(8,128)(2,1)S(1)}, u32[]{:S(2)}, u32[]{:S(2)}) collective-permute-start(bf16[2,32,1024]{2,1,0:T(8,128)(2,1)S(1)} %get-tuple-element.103), channel_id=1, source_target_pairs={{0,8},{4,12},{8,0},{12,4},{1,9},{5,13},{9,1},{13,5},{2,10},{6,14},... | collective-permute-start | bytes 393224 | tf_op jit(solution)/shard_map/ppermute | solution.py:21
  14.2 8.7 %collective-permute-start.2 = (bf16[2,32,1024]{2,1,0:T(8,128)(2,1)S(1)}, bf16[2,32,1024]{2,1,0:T(8,128)(2,1)S(1)}, u32[]{:S(2)}, u32[]{:S(2)}) collective-permute-start(bf16[2,32,1024]{2,1,0:T(8,128)(2,1)S(1)} %get-tuple-element.104), channel_id=1, source_target_pairs={{0,12},{4,8},{8,4},{12,0},{1,13},{5,9},{9,5},{13,1},{2,14},{6,10},... | collective-permute-start | bytes 393224 | tf_op jit(solution)/shard_map/ppermute | solution.py:21
  23.1 12.0 %collective-permute-start.6 = (bf16[256,896]{1,0:T(8,128)(2,1)S(1)}, bf16[256,896]{1,0:T(8,128)(2,1)S(1)}, u32[]{:S(2)}, u32[]{:S(2)}) collective-permute-start(bf16[256,896]{1,0:T(8,128)(2,1)S(1)} %copy-done.1), channel_id=1, source_target_pairs={{0,4},{4,0},{8,12},{12,8},{1,5},{5,1},{9,13},{13,9},{2,6},{6,2},{1... | collective-permute-start | bytes 1376264 | tf_op jit(solution)/shard_map/ppermute | solution.py:21
  23.2 13.2 %collective-permute-start.7 = (bf16[256,896]{1,0:T(8,128)(2,1)S(1)}, bf16[256,896]{1,0:T(8,128)(2,1)S(1)}, u32[]{:S(2)}, u32[]{:S(2)}) collective-permute-start(bf16[256,896]{1,0:T(8,128)(2,1)S(1)} %copy-done.2), channel_id=1, source_target_pairs={{0,12},{4,8},{8,4},{12,0},{1,13},{5,9},{9,5},{13,1},{2,14},{6,10},... | collective-permute-start | bytes 1376264 | tf_op jit(solution)/shard_map/ppermute | solution.py:21
  23.8 8.9 %collective-permute-start.5 = (bf16[8,32,512]{2,1,0:T(8,128)(2,1)S(1)}, bf16[8,32,512]{2,1,0:T(8,128)(2,1)S(1)}, u32[]{:S(2)}, u32[]{:S(2)}) collective-permute-start(bf16[8,32,512]{2,1,0:T(8,128)(2,1)S(1)} %get-tuple-element.99), channel_id=1, source_target_pairs={{0,96},{32,64},{64,32},{96,0},{1,97},{33,65},{65,33},{97,1},{2,98}... | collective-permute-start | bytes 786440 | tf_op jit(solution)/shard_map/ppermute | solution.py:21
  26.7 7.4 %collective-permute-start.4 = (bf16[8,32,512]{2,1,0:T(8,128)(2,1)S(1)}, bf16[8,32,512]{2,1,0:T(8,128)(2,1)S(1)}, u32[]{:S(2)}, u32[]{:S(2)}) collective-permute-start(bf16[8,32,512]{2,1,0:T(8,128)(2,1)S(1)} %get-tuple-element.100), channel_id=1, source_target_pairs={{0,32},{32,0},{64,96},{96,64},{1,33},{33,1},{65,97},{97,65},{2,34}... | collective-permute-start | bytes 786440 | tf_op jit(solution)/shard_map/ppermute | solution.py:21
  36.5 13.7 %collective-permute-start.9 = (bf16[2,8,32,512]{3,2,1,0:T(8,128)(2,1)S(1)}, bf16[2,8,32,512]{3,2,1,0:T(8,128)(2,1)S(1)}, u32[]{:S(2)}, u32[]{:S(2)}) collective-permute-start(bf16[2,8,32,512]{3,2,1,0:T(8,128)(2,1)S(1)} %pad_maximum_fusion.13), channel_id=1, source_target_pairs={{0,96},{32,64},{64,32},{96,0},{1,97},{33,65},{65,33},{97,1},{2,98}... | collective-permute-start | bytes 1572872 | tf_op jit(solution)/shard_map/ppermute | solution.py:21
  39.4 12.2 %collective-permute-start.10 = (bf16[2,8,32,512]{3,2,1,0:T(8,128)(2,1)S(1)}, bf16[2,8,32,512]{3,2,1,0:T(8,128)(2,1)S(1)}, u32[]{:S(2)}, u32[]{:S(2)}) collective-permute-start(bf16[2,8,32,512]{3,2,1,0:T(8,128)(2,1)S(1)} %pad_maximum_fusion.14), channel_id=1, source_target_pairs={{0,32},{32,0},{64,96},{96,64},{1,33},{33,1},{65,97},{97,65},{2,34}... | collective-permute-start | bytes 1572872 | tf_op jit(solution)/shard_map/ppermute | solution.py:21
  39.7 14.4 %collective-permute-start.11 = (bf16[8,32,1024]{2,1,0:T(8,128)(2,1)S(1)}, bf16[8,32,1024]{2,1,0:T(8,128)(2,1)S(1)}, u32[]{:S(2)}, u32[]{:S(2)}) collective-permute-start(bf16[8,32,1024]{2,1,0:T(8,128)(2,1)S(1)} %bitcast.114), channel_id=1, source_target_pairs={{0,16},{16,0},{1,17},{17,1},{2,18},{18,2},{3,19},{19,3},{4,20},{20... | collective-permute-start | bytes 1572872 | tf_op jit(solution)/shard_map/ppermute | solution.py:21
  43.5 20.3 %collective-permute-start.15 = (bf16[2,256,896]{2,1,0:T(8,128)(2,1)S(1)}, bf16[2,256,896]{2,1,0:T(8,128)(2,1)S(1)}, u32[]{:S(2)}, u32[]{:S(2)}) collective-permute-start(bf16[2,256,896]{2,1,0:T(8,128)(2,1)S(1)} %pad_maximum_fusion.11), channel_id=1, source_target_pairs={{0,4},{4,0},{8,12},{12,8},{1,5},{5,1},{9,13},{13,9},{2,6},{6,2},{1... | collective-permute-start | bytes 2752520 | tf_op jit(solution)/shard_map/ppermute | solution.py:21
  44.1 21.1 %collective-permute-start.14 = (bf16[2,256,896]{2,1,0:T(8,128)(2,1)S(1)}, bf16[2,256,896]{2,1,0:T(8,128)(2,1)S(1)}, u32[]{:S(2)}, u32[]{:S(2)}) collective-permute-start(bf16[2,256,896]{2,1,0:T(8,128)(2,1)S(1)} %pad_maximum_fusion.10), channel_id=1, source_target_pairs={{0,12},{4,8},{8,4},{12,0},{1,13},{5,9},{9,5},{13,1},{2,14},{6,10},... | collective-permute-start | bytes 2752520 | tf_op jit(solution)/shard_map/ppermute | solution.py:21
  54.1 24.3 %collective-permute-start.20 = (bf16[512,896]{1,0:T(8,128)(2,1)S(1)}, bf16[512,896]{1,0:T(8,128)(2,1)S(1)}, u32[]{:S(2)}, u32[]{:S(2)}) collective-permute-start(bf16[512,896]{1,0:T(8,128)(2,1)S(1)} %get-tuple-element.66), channel_id=1, source_target_pairs={{0,2},{2,0},{1,3},{3,1},{4,6},{6,4},{5,7},{7,5},{8,10},{10,8},{9,1... | collective-permute-start | bytes 2752520 | tf_op jit(solution)/shard_map/ppermute | solution.py:21
  54.2 7.7 %collective-permute-start.13 = (bf16[8,32,512]{2,1,0:T(8,128)(2,1)S(1)}, bf16[8,32,512]{2,1,0:T(8,128)(2,1)S(1)}, u32[]{:S(2)}, u32[]{:S(2)}) collective-permute-start(bf16[8,32,512]{2,1,0:T(8,128)(2,1)S(1)} %get-tuple-element.91), channel_id=1, source_target_pairs={{0,96},{32,64},{64,32},{96,0},{1,97},{33,65},{65,33},{97,1},{2,98}... | collective-permute-start | bytes 786440 | tf_op jit(solution)/shard_map/ppermute | solution.py:21
  55.4 6.4 %collective-permute-start.12 = (bf16[8,32,512]{2,1,0:T(8,128)(2,1)S(1)}, bf16[8,32,512]{2,1,0:T(8,128)(2,1)S(1)}, u32[]{:S(2)}, u32[]{:S(2)}) collective-permute-start(bf16[8,32,512]{2,1,0:T(8,128)(2,1)S(1)} %get-tuple-element.92), channel_id=1, source_target_pairs={{0,32},{32,0},{64,96},{96,64},{1,33},{33,1},{65,97},{97,65},{2,34}... | collective-permute-start | bytes 786440 | tf_op jit(solution)/shard_map/ppermute | solution.py:21
  65.2 11.7 %collective-permute-start.16 = (bf16[2,8,32,512]{3,2,1,0:T(8,128)(2,1)S(1)}, bf16[2,8,32,512]{3,2,1,0:T(8,128)(2,1)S(1)}, u32[]{:S(2)}, u32[]{:S(2)}) collective-permute-start(bf16[2,8,32,512]{3,2,1,0:T(8,128)(2,1)S(1)} %pad_maximum_fusion.15), channel_id=1, source_target_pairs={{0,96},{32,64},{64,32},{96,0},{1,97},{33,65},{65,33},{97,1},{2,98}... | collective-permute-start | bytes 1572872 | tf_op jit(solution)/shard_map/ppermute | solution.py:21
  66.3 10.1 %collective-permute-start.17 = (bf16[2,8,32,512]{3,2,1,0:T(8,128)(2,1)S(1)}, bf16[2,8,32,512]{3,2,1,0:T(8,128)(2,1)S(1)}, u32[]{:S(2)}, u32[]{:S(2)}) collective-permute-start(bf16[2,8,32,512]{3,2,1,0:T(8,128)(2,1)S(1)} %pad_maximum_fusion.16), channel_id=1, source_target_pairs={{0,32},{32,0},{64,96},{96,64},{1,33},{33,1},{65,97},{97,65},{2,34}... | collective-permute-start | bytes 1572872 | tf_op jit(solution)/shard_map/ppermute | solution.py:21
  67.3 10.5 %collective-permute-start.18 = (bf16[4,256,896]{2,1,0:T(8,128)(2,1)S(1)}, bf16[4,256,896]{2,1,0:T(8,128)(2,1)S(1)}, u32[]{:S(2)}, u32[]{:S(2)}) collective-permute-start(bf16[4,256,896]{2,1,0:T(8,128)(2,1)S(1)} %pad_maximum_fusion.1), channel_id=1, source_target_pairs={{0,1},{1,0},{2,3},{3,2},{4,5},{5,4},{6,7},{7,6},{8,9},{9,8},{10,11... | collective-permute-start | bytes 5505032 | tf_op jit(solution)/shard_map/ppermute | solution.py:21
  67.8 9.7 %collective-permute-start.19 = (bf16[4,256,896]{2,1,0:T(8,128)(2,1)S(1)}, bf16[4,256,896]{2,1,0:T(8,128)(2,1)S(1)}, u32[]{:S(2)}, u32[]{:S(2)}) collective-permute-start(bf16[4,256,896]{2,1,0:T(8,128)(2,1)S(1)} %pad_maximum_fusion.2), channel_id=1, source_target_pairs={{0,1},{1,0},{2,3},{3,2},{4,5},{5,4},{6,7},{7,6},{8,9},{9,8},{10,11... | collective-permute-start | bytes 5505032 | tf_op jit(solution)/shard_map/ppermute | solution.py:21
  81.4 10.1 %collective-permute-start.21 = (bf16[1024,896]{1,0:T(8,128)(2,1)S(1)}, bf16[1024,896]{1,0:T(8,128)(2,1)S(1)}, u32[]{:S(2)}, u32[]{:S(2)}) collective-permute-start(bf16[1024,896]{1,0:T(8,128)(2,1)S(1)} %fusion.16), channel_id=1, source_target_pairs={{0,1},{1,0},{2,3},{3,2},{4,5},{5,4},{6,7},{7,6},{8,9},{9,8},{10,11... | collective-permute-start | bytes 5505032 | tf_op jit(solution)/shard_map/ppermute | solution.py:21
  84.0 9.8 %collective-permute-start.23 = (bf16[1024,896]{1,0:T(8,128)(2,1)S(1)}, bf16[1024,896]{1,0:T(8,128)(2,1)S(1)}, u32[]{:S(2)}, u32[]{:S(2)}) collective-permute-start(bf16[1024,896]{1,0:T(8,128)(2,1)S(1)} %fusion.13), channel_id=1, source_target_pairs={{0,1},{1,0},{2,3},{3,2},{4,5},{5,4},{6,7},{7,6},{8,9},{9,8},{10,11... | collective-permute-start | bytes 5505032 | tf_op jit(solution)/shard_map/ppermute | solution.py:21
  86.9 42.2 %collective-permute-start.27 = (bf16[512,896]{1,0:T(8,128)(2,1)S(1)}, bf16[512,896]{1,0:T(8,128)(2,1)S(1)}, u32[]{:S(2)}, u32[]{:S(2)}) collective-permute-start(bf16[512,896]{1,0:T(8,128)(2,1)S(1)} %convolution_convert_fusion.1), channel_id=1, source_target_pairs={{0,2},{2,0},{1,3},{3,1},{4,6},{6,4},{5,7},{7,5},{8,10},{10,8},{9,1... | collective-permute-start | bytes 2752520 | tf_op jit(solution)/shard_map/ppermute | solution.py:21
  89.3 39.6 %collective-permute-start.28 = (bf16[512,896]{1,0:T(8,128)(2,1)S(1)}, bf16[512,896]{1,0:T(8,128)(2,1)S(1)}, u32[]{:S(2)}, u32[]{:S(2)}) collective-permute-start(bf16[512,896]{1,0:T(8,128)(2,1)S(1)} %convolution_convert_fusion), channel_id=1, source_target_pairs={{0,2},{2,0},{1,3},{3,1},{4,6},{6,4},{5,7},{7,5},{8,10},{10,8},{9,1... | collective-permute-start | bytes 2752520 | tf_op jit(solution)/shard_map/ppermute | solution.py:21
  93.8 2.6 %copy-start = (f32[1024,896]{1,0:T(8,128)}, f32[1024,896]{1,0:T(8,128)S(1)}, u32[]{:S(2)}) copy-start(f32[1024,896]{1,0:T(8,128)S(1)} %convert_add_fusion.1) | copy-start | bytes 11010052
  96.4 23.0 %collective-permute-start.22 = (bf16[2,256,896]{2,1,0:T(8,128)(2,1)S(1)}, bf16[2,256,896]{2,1,0:T(8,128)(2,1)S(1)}, u32[]{:S(2)}, u32[]{:S(2)}) collective-permute-start(bf16[2,256,896]{2,1,0:T(8,128)(2,1)S(1)} %bitcast.134), channel_id=1, source_target_pairs={{0,12},{4,8},{8,4},{12,0},{1,13},{5,9},{9,5},{13,1},{2,14},{6,10},... | collective-permute-start | bytes 2752520 | tf_op jit(solution)/shard_map/ppermute | solution.py:21
  97.6 21.8 %collective-permute-start.24 = (bf16[2,256,896]{2,1,0:T(8,128)(2,1)S(1)}, bf16[2,256,896]{2,1,0:T(8,128)(2,1)S(1)}, u32[]{:S(2)}, u32[]{:S(2)}) collective-permute-start(bf16[2,256,896]{2,1,0:T(8,128)(2,1)S(1)} %fusion.19), channel_id=1, source_target_pairs={{0,4},{4,0},{8,12},{12,8},{1,5},{5,1},{9,13},{13,9},{2,6},{6,2},{1... | collective-permute-start | bytes 2752520 | tf_op jit(solution)/shard_map/ppermute | solution.py:21
  102.4 19.1 %slice-start = ((f32[1024,896]{1,0:T(8,128)}), f32[512,896]{1,0:T(8,128)S(1)}, s32[]{:S(2)}) async-start(f32[1024,896]{1,0:T(8,128)} %copy-done), calls=%async_computation | async-start | bytes 3670016 | tf_op jit(solution)/shard_map/slice | solution.py:169
  119.6 12.2 %collective-permute-start.26 = (bf16[256,896]{1,0:T(8,128)(2,1)S(1)}, bf16[256,896]{1,0:T(8,128)(2,1)S(1)}, u32[]{:S(2)}, u32[]{:S(2)}) collective-permute-start(bf16[256,896]{1,0:T(8,128)(2,1)S(1)} %fusion.21), channel_id=1, source_target_pairs={{0,12},{4,8},{8,4},{12,0},{1,13},{5,9},{9,5},{13,1},{2,14},{6,10},... | collective-permute-start | bytes 1376264 | tf_op jit(solution)/shard_map/ppermute | solution.py:21
  121.7 10.5 %collective-permute-start.25 = (bf16[256,896]{1,0:T(8,128)(2,1)S(1)}, bf16[256,896]{1,0:T(8,128)(2,1)S(1)}, u32[]{:S(2)}, u32[]{:S(2)}) collective-permute-start(bf16[256,896]{1,0:T(8,128)(2,1)S(1)} %fusion.20), channel_id=1, source_target_pairs={{0,4},{4,0},{8,12},{12,8},{1,5},{5,1},{9,13},{13,9},{2,6},{6,2},{1... | collective-permute-start | bytes 1376264 | tf_op jit(solution)/shard_map/ppermute | solution.py:21
  131.9 0.8 copy-start.3
  132.2 0.8 copy-start.4

commit v4 on v3

--- a/solution.py
+++ b/solution.py
@@ -12,6 +12,7 @@
 SIZES = {"x": 4, "zh": 2, "y": 4, "zl": 2, "core": 2}
 BF16, F32 = jnp.bfloat16, jnp.float32
 VMEM = pl.BlockSpec(memory_space=pltpu.VMEM)
+SMALL = pltpu.CompilerParams(vmem_limit_bytes=16 * 1024 * 1024)
 
 STEP = {"b": lambda i: i ^ 1, "a": lambda i: 3 - i, "ab": lambda i: i ^ 2}
 
@@ -49,7 +50,7 @@
 def split_grad(grad):
     rows, width = grad.shape
     piece = jax.ShapeDtypeStruct((4, rows, width // 8), BF16)
-    return pl.pallas_call(split_kernel, in_specs=[VMEM], out_specs=[VMEM] * 2, out_shape=[piece, piece])(grad)
+    return pl.pallas_call(split_kernel, in_specs=[VMEM], out_specs=[VMEM] * 2, out_shape=[piece, piece], compiler_params=SMALL)(grad)
 
 
 def token_blocks(rows):
@@ -71,7 +72,7 @@
 def make_hidden(pre):
     tokens, units = pre.shape
     out = [jax.ShapeDtypeStruct((tokens, units // 2), t) for t in (BF16, BF16, F32, F32)]
-    return pl.pallas_call(hidden_kernel, in_specs=[VMEM], out_specs=[VMEM] * 4, out_shape=out)(pre)
+    return pl.pallas_call(hidden_kernel, in_specs=[VMEM], out_specs=[VMEM] * 4, out_shape=out, compiler_params=SMALL)(pre)
 
 
 def finish_kernel(slope_l, slope_r, own_l, own_r, far_l, far_r, out):
@@ -87,7 +88,7 @@
 def finish(*args):
     tokens, half = args[0].shape
     out = jax.ShapeDtypeStruct((tokens, 2 * half), BF16)
-    return pl.pallas_call(finish_kernel, in_specs=[VMEM] * 6, out_specs=VMEM, out_shape=out)(*args)
+    return pl.pallas_call(finish_kernel, in_specs=[VMEM] * 6, out_specs=VMEM, out_shape=out, compiler_params=SMALL)(*args)
 
 
 def outer(g, h):
@@ -108,9 +109,9 @@
     sibling = swap(away, "core")
     weight_l, weight_r = weight[:, :half], weight[:, half:]
     other_l = swap(weight_l, "zl")
-    hidden_l, hidden_r, slope_l, slope_r = make_hidden(after(pre_act, near))
 
-    both = jnp.stack([near, after(sibling, hidden_l)])
+    both = jnp.stack([near, after(sibling, weight_l)])
+    hidden_l, hidden_r, slope_l, slope_r = make_hidden(after(pre_act, both))
     grad = jnp.stack([both[:, 0]] + [swap(both[:, s], "y", m) for s, m in ((1, "b"), (2, "a"), (3, "ab"))], 1)
     grad = grad.reshape(8, rows, 2 * own_rows)
 
@@ -130,7 +131,7 @@
     far_o, far_t = grad_far[..., own_rows:], grad_far[..., :own_rows]
     far_ob, far_ta = swap(far_o, "x", "b"), swap(far_t, "x", "a")
     other_r = swap(after(weight_r, grad_far), "zl")
-    far_ob, far_ta, hidden_la, hidden_rb = lax.optimization_barrier((far_ob, far_ta, hidden_la, hidden_rb))
+    far_ob, far_ta = lax.optimization_barrier((far_ob, far_ta))
     far_o, far_t = jnp.stack([far_o, far_ob]), jnp.stack([far_t, far_ta])
     far_oa, far_tb = swap(far_o, "x", "a"), swap(far_t, "x", "b")
     hidden_l = jnp.concatenate([hidden_l, hidden_la])
@@ -150,28 +151,32 @@
     w_l = jnp.concatenate([weight_l, other_l])
     w_r = jnp.concatenate([weight_r, other_r])
     edge = 4 * tokens
-    away_l = inner(grad_both[edge:], w_l).astype(BF16)
+    sent_l = outer(grad_other, hidden_l).astype(BF16)
+    got_l = swap(sent_l, "zl")
+    away_l = inner(after(grad_both, sent_l)[edge:], w_l).astype(BF16)
     away_r = inner(after(grad_both, away_l)[edge:], w_r).astype(BF16)
-    sent_l = outer(after(grad_other, away_r), hidden_l).astype(BF16)
-    sent_r = outer(after(grad_other, sent_l), hidden_r).astype(BF16)
-    got_l, got_r = swap(sent_l, "zl"), swap(sent_r, "zl")
     back_l, back_r = swap(away_l, "core"), swap(away_r, "core")
+    sent_r = outer(after(grad_other, away_r), hidden_r).astype(BF16)
+    got_r = swap(sent_r, "zl")
     back_l = after(back_l, sent_r)
     part_l = inner(grad_both[:edge], w_l) + back_l.astype(F32)
+    part_l = part_l.reshape(2, 2, tokens, half)
+    next_l = swap(part_l[1].astype(BF16), "y", "a")
     back_r = after(back_r, part_l)
     part_r = inner(grad_both[:edge], w_r) + back_r.astype(F32)
-    part_l = part_l.reshape(2, 2, tokens, half)
     part_r = part_r.reshape(2, 2, tokens, half)
-    next_l, next_r = swap(part_l[1].astype(BF16), "y", "a"), swap(part_r[:, 1].astype(BF16), "y", "b")
+    next_r = swap(part_r[:, 1].astype(BF16), "y", "b")
     kept_l = outer(after(grad_own, part_r), hidden_l)
     kept_r = outer(after(grad_own, kept_l), hidden_r)
     next_l, next_r, kept_l, kept_r = lax.optimization_barrier((next_l, next_r, kept_l, kept_r))
-    part_l = part_l[0] + next_l.astype(F32)
-    part_r = part_r[:, 0] + next_r.astype(F32)
-    far_l, far_r = swap(part_l[1].astype(BF16), "y", "b"), swap(part_r[1].astype(BF16), "y", "a")
-    grad_pre = finish(slope_l, slope_r, part_l[0], part_r[0], far_l, far_r)
-    kept = jnp.concatenate([kept_l + got_l.astype(F32), kept_r + got_r.astype(F32)], 1)
-    return (grad_pre, kept.astype(BF16))
+    far_l = swap((part_l[0, 1] + next_l[1].astype(F32)).astype(BF16), "y", "b")
+    far_r = swap((part_r[1, 0] + next_r[1].astype(F32)).astype(BF16), "y", "a")
+    own_l = part_l[0, 0] + next_l[0].astype(F32)
+    own_r = part_r[0, 0] + next_r[0].astype(F32)
+    grad_pre = finish(slope_l, slope_r, own_l, own_r, far_l, far_r)
+    kept_l = (kept_l + after(got_l, own_l, own_r).astype(F32)).astype(BF16)
+    kept_r = (kept_r + after(got_r, grad_pre).astype(F32)).astype(BF16)
+    return (grad_pre, jnp.concatenate([kept_l, kept_r], 1))
 
 
 def solution(mesh):

time: 137 us -> 128 us (0.934)
  Pallas kernels: 8.64 us -> 2.11 us
  waiting for transfers between devices: 67.9 us -> 62.9 us
  starting transfers between devices: 29.4 us -> 33.7 us
  local copies, waits for them, and re-layouts: 6.98 us -> 5.16 us
    ppermute x29, waiting for transfers between devices: 67.9 us -> 62.9 us  [swap(): return lax.ppermute(value, axis, [(i, move(i)) for i in range(SIZES[axis])])]
    ppermute x29, starting transfers between devices: 29.4 us -> 33.7 us  [swap(): return lax.ppermute(value, axis, [(i, move(i)) for i in range(SIZES[axis])])]
    pallas_call x1, Pallas kernels: 3.35 us -> 0.81 us  [make_hidden(): pl.pallas_call(hidden_kernel, in_specs=[VMEM], out_specs=[VMEM] * 4, out_...]
    pallas_call x1, Pallas kernels: 3.4 us -> 1.26 us  [finish(): pl.pallas_call(finish_kernel, in_specs=[VMEM] * 6, out_specs=VMEM, out_sh...]
    squeeze x2 -> x0, local copies, waits for them, and re-layouts: 1.98 us -> none  [shards(): grad_pre = finish(slope_l, slope_r, part_l[0], part_r[0], far_l, far_r)]
    pallas_call x1, Pallas kernels: 1.88 us -> 0.03 us  [split_grad(): pl.pallas_call(split_kernel, in_specs=[VMEM], out_specs=[VMEM] * 2, out_s...]
  transfers between devices with their start and end apart: 29 -> 29, of which waited for: 19 -> 15; matrix products, arithmetic and copies ran while one was open for 19% -> 15% of each run, Pallas kernels for 2% -> 2%
where the time goes in v4:
time: 128 us; the launch traced here: 127 us
  waiting for transfers between devices  62.9 us (49%)
  starting transfers between devices  33.7 us (26%)
  matrix products  18.8 us (15%)
  local copies, waits for them, and re-layouts  5.16 us (4%)
  other arithmetic  3.56 us (3%)
  Pallas kernels  2.11 us (2%)
    ppermute x29, waiting for transfers between devices, swap(): return lax.ppermute(value, axis, [(i, move(i)) for i in range(SIZES[axis])])  62.9 us
    ppermute x29, starting transfers between devices, swap(): return lax.ppermute(value, axis, [(i, move(i)) for i in range(SIZES[axis])])  33.7 us
    dot_general x4, matrix products, outer(): lax.dot_general(g, h, (((0,), (0,)), ((), ())), preferred_element_type=F32)  9.38 us
    dot_general x4, matrix products, inner(): return jnp.dot(g, w, preferred_element_type=F32)  9.37 us
  transfers between devices with their start and end apart: 29, of which 15 were waited for; matrix products, arithmetic and copies ran while one was open for 15% of the time, Pallas kernels for 2%

profile of v4, /device:TPU:0, one launch (start us, length us, event | category | flops | bytes accessed | tf_op | source)
XLA Modules:
  0.0 127.2 jit_solution(4440047297473177320)
XLA Ops:
  0.6 1.0 copy-done.1
  1.8 1.7 %fusion.41 = (bf16[512,896]{1,0:T(8,128)(2,1)S(1)}, bf16[512,896]{1,0:T(8,128)(2,1)S(1)}) fusion(bf16[512,1792]{1,0:T(8,128)(2,1)} %param.5), kind=kLoop, calls=%fused_computation.94 | loop fusion | bytes 3670016 | tf_op jit(solution)/shard_map/slice | solution.py:110
  3.5 2.1 %collective-permute-start.8 = (bf16[512,896]{1,0:T(8,128)(2,1)S(1)}, bf16[512,896]{1,0:T(8,128)(2,1)S(1)}, u32[]{:S(2)}, u32[]{:S(2)}) collective-permute-start(bf16[512,896]{1,0:T(8,128)(2,1)S(1)} %get-tuple-element.89), channel_id=1, source_target_pairs={{0,2},{2,0},{1,3},{3,1},{4,6},{6,4},{5,7},{7,5},{8,10},{10,8},{9,1... | collective-permute-start | bytes 2752520 | tf_op jit(solution)/shard_map/ppermute | solution.py:22
  5.6 1.7 %collective-permute-start.1 = (bf16[2,32,1024]{2,1,0:T(8,128)(2,1)S(1)}, bf16[2,32,1024]{2,1,0:T(8,128)(2,1)S(1)}, u32[]{:S(2)}, u32[]{:S(2)}) collective-permute-start(bf16[2,32,1024]{2,1,0:T(8,128)(2,1)S(1)} %get-tuple-element.106), channel_id=1, source_target_pairs={{0,4},{4,0},{8,12},{12,8},{1,5},{5,1},{9,13},{13,9},{2,6},{6,2},{1... | collective-permute-start | bytes 393224 | tf_op jit(solution)/shard_map/ppermute | solution.py:22
  7.3 2.2 %collective-permute-start.2 = (bf16[2,32,1024]{2,1,0:T(8,128)(2,1)S(1)}, bf16[2,32,1024]{2,1,0:T(8,128)(2,1)S(1)}, u32[]{:S(2)}, u32[]{:S(2)}) collective-permute-start(bf16[2,32,1024]{2,1,0:T(8,128)(2,1)S(1)} %get-tuple-element.107), channel_id=1, source_target_pairs={{0,12},{4,8},{8,4},{12,0},{1,13},{5,9},{9,5},{13,1},{2,14},{6,10},... | collective-permute-start | bytes 393224 | tf_op jit(solution)/shard_map/ppermute | solution.py:22
  9.5 0.7 collective-permute-start.3
  10.2 0.8 shard_map.51
  11.3 3.8 %collective-permute-done.2 = bf16[2,32,1024]{2,1,0:T(8,128)(2,1)S(1)} collective-permute-done((bf16[2,32,1024]{2,1,0:T(8,128)(2,1)S(1)}, bf16[2,32,1024]{2,1,0:T(8,128)(2,1)S(1)}, u32[]{:S(2)}, u32[]{:S(2)}) %collective-permute-start.2) | collective-permute-done | bytes 131104 | tf_op jit(solution)/shard_map/ppermute | solution.py:22
  15.1 1.5 %collective-permute-done.3 = bf16[2,32,1024]{2,1,0:T(8,128)(2,1)S(1)} collective-permute-done((bf16[2,32,1024]{2,1,0:T(8,128)(2,1)S(1)}, bf16[2,32,1024]{2,1,0:T(8,128)(2,1)S(1)}, u32[]{:S(2)}, u32[]{:S(2)}) %collective-permute-start.3) | collective-permute-done | bytes 131104 | tf_op jit(solution)/shard_map/ppermute | solution.py:22
  16.7 2.3 %collective-permute-start.7 = (bf16[256,896]{1,0:T(8,128)(2,1)S(1)}, bf16[256,896]{1,0:T(8,128)(2,1)S(1)}, u32[]{:S(2)}, u32[]{:S(2)}) collective-permute-start(bf16[256,896]{1,0:T(8,128)(2,1)S(1)} %get-tuple-element.52), channel_id=1, source_target_pairs={{0,12},{4,8},{8,4},{12,0},{1,13},{5,9},{9,5},{13,1},{2,14},{6,10},... | collective-permute-start | bytes 1376264 | tf_op jit(solution)/shard_map/ppermute | solution.py:22
  19.1 2.8 %collective-permute-start.5 = (bf16[8,32,512]{2,1,0:T(8,128)(2,1)S(1)}, bf16[8,32,512]{2,1,0:T(8,128)(2,1)S(1)}, u32[]{:S(2)}, u32[]{:S(2)}) collective-permute-start(bf16[8,32,512]{2,1,0:T(8,128)(2,1)S(1)} %get-tuple-element.103), channel_id=1, source_target_pairs={{0,96},{32,64},{64,32},{96,0},{1,97},{33,65},{65,33},{97,1},{2,98}... | collective-permute-start | bytes 786440 | tf_op jit(solution)/shard_map/ppermute | solution.py:22
  22.2 5.2 %collective-permute-done.5 = bf16[8,32,512]{2,1,0:T(8,128)(2,1)S(1)} collective-permute-done((bf16[8,32,512]{2,1,0:T(8,128)(2,1)S(1)}, bf16[8,32,512]{2,1,0:T(8,128)(2,1)S(1)}, u32[]{:S(2)}, u32[]{:S(2)}) %collective-permute-start.5) | collective-permute-done | bytes 262176 | tf_op jit(solution)/shard_map/ppermute | solution.py:22
  27.3 1.3 collective-permute-done.4
  28.6 1.0 collective-permute-done.7
  29.6 0.5 collective-permute-done.6
  30.2 2.8 %collective-permute-start.9 = (bf16[2,8,32,512]{3,2,1,0:T(8,128)(2,1)S(1)}, bf16[2,8,32,512]{3,2,1,0:T(8,128)(2,1)S(1)}, u32[]{:S(2)}, u32[]{:S(2)}) collective-permute-start(bf16[2,8,32,512]{3,2,1,0:T(8,128)(2,1)S(1)} %pad_maximum_fusion.14), channel_id=1, source_target_pairs={{0,96},{32,64},{64,32},{96,0},{1,97},{33,65},{65,33},{97,1},{2,98}... | collective-permute-start | bytes 1572872 | tf_op jit(solution)/shard_map/ppermute | solution.py:22
  33.4 3.6 %collective-permute-start.11 = (bf16[8,32,1024]{2,1,0:T(8,128)(2,1)S(1)}, bf16[8,32,1024]{2,1,0:T(8,128)(2,1)S(1)}, u32[]{:S(2)}, u32[]{:S(2)}) collective-permute-start(bf16[8,32,1024]{2,1,0:T(8,128)(2,1)S(1)} %bitcast.140), channel_id=1, source_target_pairs={{0,16},{16,0},{1,17},{17,1},{2,18},{18,2},{3,19},{19,3},{4,20},{20... | collective-permute-start | bytes 1572872 | tf_op jit(solution)/shard_map/ppermute | solution.py:22
  37.2 0.4 collective-permute-start.18
  37.6 1.3 %collective-permute-start.16 = (bf16[2,256,896]{2,1,0:T(8,128)(2,1)S(1)}, bf16[2,256,896]{2,1,0:T(8,128)(2,1)S(1)}, u32[]{:S(2)}, u32[]{:S(2)}) collective-permute-start(bf16[2,256,896]{2,1,0:T(8,128)(2,1)S(1)} %pad_maximum_fusion.10), channel_id=1, source_target_pairs={{0,12},{4,8},{8,4},{12,0},{1,13},{5,9},{9,5},{13,1},{2,14},{6,10},... | collective-permute-start | bytes 2752520 | tf_op jit(solution)/shard_map/ppermute | solution.py:22
  39.0 4.2 %collective-permute-done.9 = bf16[2,8,32,512]{3,2,1,0:T(8,128)(2,1)S(1)} collective-permute-done((bf16[2,8,32,512]{3,2,1,0:T(8,128)(2,1)S(1)}, bf16[2,8,32,512]{3,2,1,0:T(8,128)(2,1)S(1)}, u32[]{:S(2)}, u32[]{:S(2)}) %collective-permute-start.9) | collective-permute-done | bytes 524320 | tf_op jit(solution)/shard_map/ppermute | solution.py:22
  43.1 1.4 %collective-permute-done.10 = bf16[2,8,32,512]{3,2,1,0:T(8,128)(2,1)S(1)} collective-permute-done((bf16[2,8,32,512]{3,2,1,0:T(8,128)(2,1)S(1)}, bf16[2,8,32,512]{3,2,1,0:T(8,128)(2,1)S(1)}, u32[]{:S(2)}, u32[]{:S(2)}) %collective-permute-start.10) | collective-permute-done | bytes 524320 | tf_op jit(solution)/shard_map/ppermute | solution.py:22
  44.5 3.0 %collective-permute-done.11 = bf16[8,32,1024]{2,1,0:T(8,128)(2,1)S(1)} collective-permute-done((bf16[8,32,1024]{2,1,0:T(8,128)(2,1)S(1)}, bf16[8,32,1024]{2,1,0:T(8,128)(2,1)S(1)}, u32[]{:S(2)}, u32[]{:S(2)}) %collective-permute-start.11) | collective-permute-done | bytes 524320 | tf_op jit(solution)/shard_map/ppermute | solution.py:22
  47.8 1.2 collective-permute-start.13
  49.0 0.8 collective-permute-start.12
  49.8 6.8 %collective-permute-done.13 = bf16[8,32,512]{2,1,0:T(8,128)(2,1)S(1)} collective-permute-done((bf16[8,32,512]{2,1,0:T(8,128)(2,1)S(1)}, bf16[8,32,512]{2,1,0:T(8,128)(2,1)S(1)}, u32[]{:S(2)}, u32[]{:S(2)}) %collective-permute-start.13) | collective-permute-done | bytes 262176 | tf_op jit(solution)/shard_map/ppermute | solution.py:22
  56.6 2.3 %collective-permute-start.14 = (bf16[2,8,32,512]{3,2,1,0:T(8,128)(2,1)S(1)}, bf16[2,8,32,512]{3,2,1,0:T(8,128)(2,1)S(1)}, u32[]{:S(2)}, u32[]{:S(2)}) collective-permute-start(bf16[2,8,32,512]{3,2,1,0:T(8,128)(2,1)S(1)} %pad_maximum_fusion.16), channel_id=1, source_target_pairs={{0,96},{32,64},{64,32},{96,0},{1,97},{33,65},{65,33},{97,1},{2,98}... | collective-permute-start | bytes 1572872 | tf_op jit(solution)/shard_map/ppermute | solution.py:22
  59.0 1.7 %collective-permute-start.15 = (bf16[2,8,32,512]{3,2,1,0:T(8,128)(2,1)S(1)}, bf16[2,8,32,512]{3,2,1,0:T(8,128)(2,1)S(1)}, u32[]{:S(2)}, u32[]{:S(2)}) collective-permute-start(bf16[2,8,32,512]{3,2,1,0:T(8,128)(2,1)S(1)} %pad_maximum_fusion.17), channel_id=1, source_target_pairs={{0,32},{32,0},{64,96},{96,64},{1,33},{33,1},{65,97},{97,65},{2,34}... | collective-permute-start | bytes 1572872 | tf_op jit(solution)/shard_map/ppermute | solution.py:22
  61.4 0.7 collective-permute-start.19
  62.3 5.9 %collective-permute-done.15 = bf16[2,8,32,512]{3,2,1,0:T(8,128)(2,1)S(1)} collective-permute-done((bf16[2,8,32,512]{3,2,1,0:T(8,128)(2,1)S(1)}, bf16[2,8,32,512]{3,2,1,0:T(8,128)(2,1)S(1)}, u32[]{:S(2)}, u32[]{:S(2)}) %collective-permute-start.15) | collective-permute-done | bytes 524320 | tf_op jit(solution)/shard_map/ppermute | solution.py:22
  69.3 0.5 pad_maximum_fusion
  70.2 2.4 %convolution_convert_fusion.1 = bf16[512,896]{1,0:T(8,128)(2,1)S(1)} fusion(bf16[2048,512]{1,0:T(8,128)(2,1)S(1)} %bitcast.136, bf16[2048,896]{1,0:T(8,128)(2,1)S(1)} %bitcast.147), kind=kOutput, calls=%fused_computation.23 | convolution fusion | flops 1879506944 | bytes 6684672 | tf_op jit(solution)/shard_map/dot_general | solution.py:95
  72.5 0.3 constant_dynamic-update-slice_fusion.5
  72.9 2.3 %fusion.12 = bf16[1024,896]{1,0:T(8,128)(2,1)S(1)} fusion(bf16[2048,1024]{1,0:T(8,128)(2,1)S(1)} %constant_dynamic-update-slice_fusion.5, bf16[512,896]{1,0:T(8,128)(2,1)S(1)} %collective-permute-done.8, bf16[512,896]{1,0:T(8,128)(2,1)S(1)} %get-tuple-element.89), kind=kOutput, calls=%fused_computation.20 | convolution fusion | flops 1883635712 | bytes 5767168 | tf_op jit(solution)/shard_map/dot_general | solution.py:99
  75.3 2.3 %fusion.15 = bf16[1024,896]{1,0:T(8,128)(2,1)S(1)} fusion(bf16[2048,1024]{1,0:T(8,128)(2,1)S(1)} %constant_dynamic-update-slice_fusion.5, bf16[512,896]{1,0:T(8,128)(2,1)S(1)} %collective-permute-done.20, bf16[512,896]{1,0:T(8,128)(2,1)S(1)} %get-tuple-element.64), kind=kOutput, calls=%fused_computation.21 | convolution fusion | flops 1883635712 | bytes 5767168 | tf_op jit(solution)/shard_map/dot_general | solution.py:99
  77.6 0.6 collective-permute-start.23
  78.2 2.3 %collective-permute-start.27 = (bf16[512,896]{1,0:T(8,128)(2,1)S(1)}, bf16[512,896]{1,0:T(8,128)(2,1)S(1)}, u32[]{:S(2)}, u32[]{:S(2)}) collective-permute-start(bf16[512,896]{1,0:T(8,128)(2,1)S(1)} %convolution_convert_fusion.1), channel_id=1, source_target_pairs={{0,2},{2,0},{1,3},{3,1},{4,6},{6,4},{5,7},{7,5},{8,10},{10,8},{9,1... | collective-permute-start | bytes 2752520 | tf_op jit(solution)/shard_map/ppermute | solution.py:22
  80.5 2.3 %convolution_convert_fusion = bf16[512,896]{1,0:T(8,128)(2,1)S(1)} fusion(bf16[2048,512]{1,0:T(8,128)(2,1)S(1)} %bitcast.138, bf16[2048,896]{1,0:T(8,128)(2,1)S(1)} %bitcast.161), kind=kOutput, calls=%fused_computation.22 | convolution fusion | flops 1879506944 | bytes 6684672 | tf_op jit(solution)/shard_map/dot_general | solution.py:95
  83.1 2.4 %convert_add_fusion.1 = f32[1024,896]{1,0:T(8,128)S(1)} fusion(bf16[1024,896]{1,0:T(8,128)(2,1)S(1)} %collective-permute-done.21, bf16[2048,1024]{1,0:T(8,128)(2,1)S(1)} %constant_dynamic-update-slice_fusion.5, bf16[512,896]{1,0:T(8,128)(2,1)S(1)} %collective-permute-done.8, bf16[512,896]{1,0:T(8,128)(2,1)S(1)} %get-tuple-element.89), kind=kOutput, calls=%fused_computation.2 | convolution fusion | flops 1884553216 | bytes 9437184 | tf_op jit(solution)/shard_map/dot_general | solution.py:99
  85.5 2.3 %convert_add_fusion = f32[1024,896]{1,0:T(8,128)S(1)} fusion(bf16[1024,896]{1,0:T(8,128)(2,1)S(1)} %collective-permute-done.23, bf16[2048,1024]{1,0:T(8,128)(2,1)S(1)} %constant_dynamic-update-slice_fusion.5, bf16[512,896]{1,0:T(8,128)(2,1)S(1)} %collective-permute-done.20, bf16[512,896]{1,0:T(8,128)(2,1)S(1)} %get-tuple-element.64), kind=kOutput, calls=%fused_computation.1 | convolution fusion | flops 1884553216 | bytes 9437184 | tf_op jit(solution)/shard_map/dot_general | solution.py:99
  88.1 0.4 collective-permute-start.22
  88.5 0.9 collective-permute-start.24
  89.3 2.3 %fusion.43 = f32[512,896]{1,0:T(8,128)S(1)} fusion(bf16[2048,512]{1,0:T(8,128)(2,1)S(1)} %bitcast.134, bf16[2048,896]{1,0:T(8,128)(2,1)S(1)} %bitcast.148), kind=kOutput, calls=%fused_computation.96 | convolution fusion | flops 1879048192 | bytes 7602176 | tf_op jit(solution)/shard_map/dot_general | solution.py:95
  91.7 2.3 %fusion.44 = f32[512,896]{1,0:T(8,128)S(1)} fusion(bf16[2048,512]{1,0:T(8,128)(2,1)S(1)} %bitcast.135, bf16[2048,896]{1,0:T(8,128)(2,1)S(1)} %bitcast.162), kind=kOutput, calls=%fused_computation.97 | convolution fusion | flops 1879048192 | bytes 7602176 | tf_op jit(solution)/shard_map/dot_general | solution.py:95
  94.0 17.4 %collective-permute-done.22 = bf16[2,256,896]{2,1,0:T(8,128)(2,1)S(1)} collective-permute-done((bf16[2,256,896]{2,1,0:T(8,128)(2,1)S(1)}, bf16[2,256,896]{2,1,0:T(8,128)(2,1)S(1)}, u32[]{:S(2)}, u32[]{:S(2)}) %collective-permute-start.22) | collective-permute-done | bytes 917536 | tf_op jit(solution)/shard_map/ppermute | solution.py:22
  111.6 1.8 %collective-permute-start.26 = (bf16[256,896]{1,0:T(8,128)(2,1)S(1)}, bf16[256,896]{1,0:T(8,128)(2,1)S(1)}, u32[]{:S(2)}, u32[]{:S(2)}) collective-permute-start(bf16[256,896]{1,0:T(8,128)(2,1)S(1)} %get-tuple-element.84), channel_id=1, source_target_pairs={{0,12},{4,8},{8,4},{12,0},{1,13},{5,9},{9,5},{13,1},{2,14},{6,10},... | collective-permute-start | bytes 1376264 | tf_op jit(solution)/shard_map/ppermute | solution.py:22
  113.9 10.3 %collective-permute-done.26.far_r = bf16[256,896]{1,0:T(8,128)(2,1)S(1)} collective-permute-done((bf16[256,896]{1,0:T(8,128)(2,1)S(1)}, bf16[256,896]{1,0:T(8,128)(2,1)S(1)}, u32[]{:S(2)}, u32[]{:S(2)}) %collective-permute-start.26) | collective-permute-done | bytes 458784 | tf_op jit(solution)/shard_map/ppermute | solution.py:22
  124.4 1.3 shard_map.52
  125.9 1.4 %pad_maximum_fusion.5 = bf16[512,1792]{1,0:T(8,128)(2,1)} fusion(bf16[512,896]{1,0:T(8,128)(2,1)S(1)} %add_convert_fusion, bf16[512,896]{1,0:T(8,128)(2,1)S(1)} %add_convert_fusion.1), kind=kLoop, calls=%fused_computation.17 | loop fusion | flops 3670016 | bytes 3670016 | tf_op jit(solution)/shard_map/concatenate | solution.py:179
  (69 shorter events, 5.7 us)
Async XLA Ops:
  0.6 1.0 copy-start.1
  1.7 8.5 %copy-start = (bf16[256,1792]{1,0:T(8,128)(2,1)S(1)}, bf16[256,1792]{1,0:T(8,128)(2,1)}, u32[]{:S(2)}) copy-start(bf16[256,1792]{1,0:T(8,128)(2,1)} %pre) | copy-start | bytes 2752516
  1.7 3.8 %collective-permute-start = (bf16[4,32,1024]{2,1,0:T(8,128)(2,1)S(1)}, bf16[4,32,1024]{2,1,0:T(8,128)(2,1)S(1)}, u32[]{:S(2)}, u32[]{:S(2)}) collective-permute-start(bf16[4,32,1024]{2,1,0:T(8,128)(2,1)S(1)} %get-tuple-element.44), channel_id=1, source_target_pairs={{0,1},{1,0},{2,3},{3,2},{4,5},{5,4},{6,7},{7,6},{8,9},{9,8},{10,11... | collective-permute-start | bytes 786440 | tf_op jit(solution)/shard_map/ppermute | solution.py:22
  3.5 26.7 %collective-permute-start.8 = (bf16[512,896]{1,0:T(8,128)(2,1)S(1)}, bf16[512,896]{1,0:T(8,128)(2,1)S(1)}, u32[]{:S(2)}, u32[]{:S(2)}) collective-permute-start(bf16[512,896]{1,0:T(8,128)(2,1)S(1)} %get-tuple-element.89), channel_id=1, source_target_pairs={{0,2},{2,0},{1,3},{3,1},{4,6},{6,4},{5,7},{7,5},{8,10},{10,8},{9,1... | collective-permute-start | bytes 2752520 | tf_op jit(solution)/shard_map/ppermute | solution.py:22
  5.6 5.6 %collective-permute-start.1 = (bf16[2,32,1024]{2,1,0:T(8,128)(2,1)S(1)}, bf16[2,32,1024]{2,1,0:T(8,128)(2,1)S(1)}, u32[]{:S(2)}, u32[]{:S(2)}) collective-permute-start(bf16[2,32,1024]{2,1,0:T(8,128)(2,1)S(1)} %get-tuple-element.106), channel_id=1, source_target_pairs={{0,4},{4,0},{8,12},{12,8},{1,5},{5,1},{9,13},{13,9},{2,6},{6,2},{1... | collective-permute-start | bytes 393224 | tf_op jit(solution)/shard_map/ppermute | solution.py:22
  7.3 7.8 %collective-permute-start.2 = (bf16[2,32,1024]{2,1,0:T(8,128)(2,1)S(1)}, bf16[2,32,1024]{2,1,0:T(8,128)(2,1)S(1)}, u32[]{:S(2)}, u32[]{:S(2)}) collective-permute-start(bf16[2,32,1024]{2,1,0:T(8,128)(2,1)S(1)} %get-tuple-element.107), channel_id=1, source_target_pairs={{0,12},{4,8},{8,4},{12,0},{1,13},{5,9},{9,5},{13,1},{2,14},{6,10},... | collective-permute-start | bytes 393224 | tf_op jit(solution)/shard_map/ppermute | solution.py:22
  9.5 7.1 %collective-permute-start.3 = (bf16[2,32,1024]{2,1,0:T(8,128)(2,1)S(1)}, bf16[2,32,1024]{2,1,0:T(8,128)(2,1)S(1)}, u32[]{:S(2)}, u32[]{:S(2)}) collective-permute-start(bf16[2,32,1024]{2,1,0:T(8,128)(2,1)S(1)} %get-tuple-element.108), channel_id=1, source_target_pairs={{0,8},{4,12},{8,0},{12,4},{1,9},{5,13},{9,1},{13,5},{2,10},{6,14},... | collective-permute-start | bytes 393224 | tf_op jit(solution)/shard_map/ppermute | solution.py:22
  16.7 12.9 %collective-permute-start.7 = (bf16[256,896]{1,0:T(8,128)(2,1)S(1)}, bf16[256,896]{1,0:T(8,128)(2,1)S(1)}, u32[]{:S(2)}, u32[]{:S(2)}) collective-permute-start(bf16[256,896]{1,0:T(8,128)(2,1)S(1)} %get-tuple-element.52), channel_id=1, source_target_pairs={{0,12},{4,8},{8,4},{12,0},{1,13},{5,9},{9,5},{13,1},{2,14},{6,10},... | collective-permute-start | bytes 1376264 | tf_op jit(solution)/shard_map/ppermute | solution.py:22
  19.0 11.2 %collective-permute-start.6 = (bf16[256,896]{1,0:T(8,128)(2,1)S(1)}, bf16[256,896]{1,0:T(8,128)(2,1)S(1)}, u32[]{:S(2)}, u32[]{:S(2)}) collective-permute-start(bf16[256,896]{1,0:T(8,128)(2,1)S(1)} %get-tuple-element.50), channel_id=1, source_target_pairs={{0,4},{4,0},{8,12},{12,8},{1,5},{5,1},{9,13},{13,9},{2,6},{6,2},{1... | collective-permute-start | bytes 1376264 | tf_op jit(solution)/shard_map/ppermute | solution.py:22
  19.1 8.2 %collective-permute-start.5 = (bf16[8,32,512]{2,1,0:T(8,128)(2,1)S(1)}, bf16[8,32,512]{2,1,0:T(8,128)(2,1)S(1)}, u32[]{:S(2)}, u32[]{:S(2)}) collective-permute-start(bf16[8,32,512]{2,1,0:T(8,128)(2,1)S(1)} %get-tuple-element.103), channel_id=1, source_target_pairs={{0,96},{32,64},{64,32},{96,0},{1,97},{33,65},{65,33},{97,1},{2,98}... | collective-permute-start | bytes 786440 | tf_op jit(solution)/shard_map/ppermute | solution.py:22
  21.9 6.7 %collective-permute-start.4 = (bf16[8,32,512]{2,1,0:T(8,128)(2,1)S(1)}, bf16[8,32,512]{2,1,0:T(8,128)(2,1)S(1)}, u32[]{:S(2)}, u32[]{:S(2)}) collective-permute-start(bf16[8,32,512]{2,1,0:T(8,128)(2,1)S(1)} %get-tuple-element.104), channel_id=1, source_target_pairs={{0,32},{32,0},{64,96},{96,64},{1,33},{33,1},{65,97},{97,65},{2,34}... | collective-permute-start | bytes 786440 | tf_op jit(solution)/shard_map/ppermute | solution.py:22
  30.2 12.9 %collective-permute-start.9 = (bf16[2,8,32,512]{3,2,1,0:T(8,128)(2,1)S(1)}, bf16[2,8,32,512]{3,2,1,0:T(8,128)(2,1)S(1)}, u32[]{:S(2)}, u32[]{:S(2)}) collective-permute-start(bf16[2,8,32,512]{3,2,1,0:T(8,128)(2,1)S(1)} %pad_maximum_fusion.14), channel_id=1, source_target_pairs={{0,96},{32,64},{64,32},{96,0},{1,97},{33,65},{65,33},{97,1},{2,98}... | collective-permute-start | bytes 1572872 | tf_op jit(solution)/shard_map/ppermute | solution.py:22
  33.1 11.5 %collective-permute-start.10 = (bf16[2,8,32,512]{3,2,1,0:T(8,128)(2,1)S(1)}, bf16[2,8,32,512]{3,2,1,0:T(8,128)(2,1)S(1)}, u32[]{:S(2)}, u32[]{:S(2)}) collective-permute-start(bf16[2,8,32,512]{3,2,1,0:T(8,128)(2,1)S(1)} %pad_maximum_fusion.15), channel_id=1, source_target_pairs={{0,32},{32,0},{64,96},{96,64},{1,33},{33,1},{65,97},{97,65},{2,34}... | collective-permute-start | bytes 1572872 | tf_op jit(solution)/shard_map/ppermute | solution.py:22
  33.4 14.2 %collective-permute-start.11 = (bf16[8,32,1024]{2,1,0:T(8,128)(2,1)S(1)}, bf16[8,32,1024]{2,1,0:T(8,128)(2,1)S(1)}, u32[]{:S(2)}, u32[]{:S(2)}) collective-permute-start(bf16[8,32,1024]{2,1,0:T(8,128)(2,1)S(1)} %bitcast.140), channel_id=1, source_target_pairs={{0,16},{16,0},{1,17},{17,1},{2,18},{18,2},{3,19},{19,3},{4,20},{20... | collective-permute-start | bytes 1572872 | tf_op jit(solution)/shard_map/ppermute | solution.py:22
  37.2 23.8 %collective-permute-start.18 = (bf16[2,256,896]{2,1,0:T(8,128)(2,1)S(1)}, bf16[2,256,896]{2,1,0:T(8,128)(2,1)S(1)}, u32[]{:S(2)}, u32[]{:S(2)}) collective-permute-start(bf16[2,256,896]{2,1,0:T(8,128)(2,1)S(1)} %pad_maximum_fusion.11), channel_id=1, source_target_pairs={{0,4},{4,0},{8,12},{12,8},{1,5},{5,1},{9,13},{13,9},{2,6},{6,2},{1... | collective-permute-start | bytes 2752520 | tf_op jit(solution)/shard_map/ppermute | solution.py:22
  37.6 23.0 %collective-permute-start.16 = (bf16[2,256,896]{2,1,0:T(8,128)(2,1)S(1)}, bf16[2,256,896]{2,1,0:T(8,128)(2,1)S(1)}, u32[]{:S(2)}, u32[]{:S(2)}) collective-permute-start(bf16[2,256,896]{2,1,0:T(8,128)(2,1)S(1)} %pad_maximum_fusion.10), channel_id=1, source_target_pairs={{0,12},{4,8},{8,4},{12,0},{1,13},{5,9},{9,5},{13,1},{2,14},{6,10},... | collective-permute-start | bytes 2752520 | tf_op jit(solution)/shard_map/ppermute | solution.py:22
  47.7 22.2 %collective-permute-start.20 = (bf16[512,896]{1,0:T(8,128)(2,1)S(1)}, bf16[512,896]{1,0:T(8,128)(2,1)S(1)}, u32[]{:S(2)}, u32[]{:S(2)}) collective-permute-start(bf16[512,896]{1,0:T(8,128)(2,1)S(1)} %get-tuple-element.64), channel_id=1, source_target_pairs={{0,2},{2,0},{1,3},{3,1},{4,6},{6,4},{5,7},{7,5},{8,10},{10,8},{9,1... | collective-permute-start | bytes 2752520 | tf_op jit(solution)/shard_map/ppermute | solution.py:22
  47.8 8.8 %collective-permute-start.13 = (bf16[8,32,512]{2,1,0:T(8,128)(2,1)S(1)}, bf16[8,32,512]{2,1,0:T(8,128)(2,1)S(1)}, u32[]{:S(2)}, u32[]{:S(2)}) collective-permute-start(bf16[8,32,512]{2,1,0:T(8,128)(2,1)S(1)} %get-tuple-element.95), channel_id=1, source_target_pairs={{0,96},{32,64},{64,32},{96,0},{1,97},{33,65},{65,33},{97,1},{2,98}... | collective-permute-start | bytes 786440 | tf_op jit(solution)/shard_map/ppermute | solution.py:22
  49.0 7.6 %collective-permute-start.12 = (bf16[8,32,512]{2,1,0:T(8,128)(2,1)S(1)}, bf16[8,32,512]{2,1,0:T(8,128)(2,1)S(1)}, u32[]{:S(2)}, u32[]{:S(2)}) collective-permute-start(bf16[8,32,512]{2,1,0:T(8,128)(2,1)S(1)} %get-tuple-element.96), channel_id=1, source_target_pairs={{0,32},{32,0},{64,96},{96,64},{1,33},{33,1},{65,97},{97,65},{2,34}... | collective-permute-start | bytes 786440 | tf_op jit(solution)/shard_map/ppermute | solution.py:22
  56.6 12.0 %collective-permute-start.14 = (bf16[2,8,32,512]{3,2,1,0:T(8,128)(2,1)S(1)}, bf16[2,8,32,512]{3,2,1,0:T(8,128)(2,1)S(1)}, u32[]{:S(2)}, u32[]{:S(2)}) collective-permute-start(bf16[2,8,32,512]{3,2,1,0:T(8,128)(2,1)S(1)} %pad_maximum_fusion.16), channel_id=1, source_target_pairs={{0,96},{32,64},{64,32},{96,0},{1,97},{33,65},{65,33},{97,1},{2,98}... | collective-permute-start | bytes 1572872 | tf_op jit(solution)/shard_map/ppermute | solution.py:22
  59.0 9.3 %collective-permute-start.15 = (bf16[2,8,32,512]{3,2,1,0:T(8,128)(2,1)S(1)}, bf16[2,8,32,512]{3,2,1,0:T(8,128)(2,1)S(1)}, u32[]{:S(2)}, u32[]{:S(2)}) collective-permute-start(bf16[2,8,32,512]{3,2,1,0:T(8,128)(2,1)S(1)} %pad_maximum_fusion.17), channel_id=1, source_target_pairs={{0,32},{32,0},{64,96},{96,64},{1,33},{33,1},{65,97},{97,65},{2,34}... | collective-permute-start | bytes 1572872 | tf_op jit(solution)/shard_map/ppermute | solution.py:22
  60.9 8.4 %collective-permute-start.17 = (bf16[4,256,896]{2,1,0:T(8,128)(2,1)S(1)}, bf16[4,256,896]{2,1,0:T(8,128)(2,1)S(1)}, u32[]{:S(2)}, u32[]{:S(2)}) collective-permute-start(bf16[4,256,896]{2,1,0:T(8,128)(2,1)S(1)} %pad_maximum_fusion.1), channel_id=1, source_target_pairs={{0,1},{1,0},{2,3},{3,2},{4,5},{5,4},{6,7},{7,6},{8,9},{9,8},{10,11... | collective-permute-start | bytes 5505032 | tf_op jit(solution)/shard_map/ppermute | solution.py:22
  61.4 7.6 %collective-permute-start.19 = (bf16[4,256,896]{2,1,0:T(8,128)(2,1)S(1)}, bf16[4,256,896]{2,1,0:T(8,128)(2,1)S(1)}, u32[]{:S(2)}, u32[]{:S(2)}) collective-permute-start(bf16[4,256,896]{2,1,0:T(8,128)(2,1)S(1)} %pad_maximum_fusion.2), channel_id=1, source_target_pairs={{0,1},{1,0},{2,3},{3,2},{4,5},{5,4},{6,7},{7,6},{8,9},{9,8},{10,11... | collective-permute-start | bytes 5505032 | tf_op jit(solution)/shard_map/ppermute | solution.py:22
  75.2 7.9 %collective-permute-start.21 = (bf16[1024,896]{1,0:T(8,128)(2,1)S(1)}, bf16[1024,896]{1,0:T(8,128)(2,1)S(1)}, u32[]{:S(2)}, u32[]{:S(2)}) collective-permute-start(bf16[1024,896]{1,0:T(8,128)(2,1)S(1)} %fusion.12), channel_id=1, source_target_pairs={{0,1},{1,0},{2,3},{3,2},{4,5},{5,4},{6,7},{7,6},{8,9},{9,8},{10,11... | collective-permute-start | bytes 5505032 | tf_op jit(solution)/shard_map/ppermute | solution.py:22
  77.6 7.9 %collective-permute-start.23 = (bf16[1024,896]{1,0:T(8,128)(2,1)S(1)}, bf16[1024,896]{1,0:T(8,128)(2,1)S(1)}, u32[]{:S(2)}, u32[]{:S(2)}) collective-permute-start(bf16[1024,896]{1,0:T(8,128)(2,1)S(1)} %fusion.15), channel_id=1, source_target_pairs={{0,1},{1,0},{2,3},{3,2},{4,5},{5,4},{6,7},{7,6},{8,9},{9,8},{10,11... | collective-permute-start | bytes 5505032 | tf_op jit(solution)/shard_map/ppermute | solution.py:22
  78.2 35.5 %collective-permute-start.27 = (bf16[512,896]{1,0:T(8,128)(2,1)S(1)}, bf16[512,896]{1,0:T(8,128)(2,1)S(1)}, u32[]{:S(2)}, u32[]{:S(2)}) collective-permute-start(bf16[512,896]{1,0:T(8,128)(2,1)S(1)} %convolution_convert_fusion.1), channel_id=1, source_target_pairs={{0,2},{2,0},{1,3},{3,1},{4,6},{6,4},{5,7},{7,5},{8,10},{10,8},{9,1... | collective-permute-start | bytes 2752520 | tf_op jit(solution)/shard_map/ppermute | solution.py:22
  82.8 42.9 %collective-permute-start.28 = (bf16[512,896]{1,0:T(8,128)(2,1)S(1)}, bf16[512,896]{1,0:T(8,128)(2,1)S(1)}, u32[]{:S(2)}, u32[]{:S(2)}) collective-permute-start(bf16[512,896]{1,0:T(8,128)(2,1)S(1)} %convolution_convert_fusion), channel_id=1, source_target_pairs={{0,2},{2,0},{1,3},{3,1},{4,6},{6,4},{5,7},{7,5},{8,10},{10,8},{9,1... | collective-permute-start | bytes 2752520 | tf_op jit(solution)/shard_map/ppermute | solution.py:22
  88.1 23.4 %collective-permute-start.22 = (bf16[2,256,896]{2,1,0:T(8,128)(2,1)S(1)}, bf16[2,256,896]{2,1,0:T(8,128)(2,1)S(1)}, u32[]{:S(2)}, u32[]{:S(2)}) collective-permute-start(bf16[2,256,896]{2,1,0:T(8,128)(2,1)S(1)} %bitcast.156), channel_id=1, source_target_pairs={{0,12},{4,8},{8,4},{12,0},{1,13},{5,9},{9,5},{13,1},{2,14},{6,10},... | collective-permute-start | bytes 2752520 | tf_op jit(solution)/shard_map/ppermute | solution.py:22
  88.5 23.0 %collective-permute-start.24 = (bf16[2,256,896]{2,1,0:T(8,128)(2,1)S(1)}, bf16[2,256,896]{2,1,0:T(8,128)(2,1)S(1)}, u32[]{:S(2)}, u32[]{:S(2)}) collective-permute-start(bf16[2,256,896]{2,1,0:T(8,128)(2,1)S(1)} %fusion.18), channel_id=1, source_target_pairs={{0,4},{4,0},{8,12},{12,8},{1,5},{5,1},{9,13},{13,9},{2,6},{6,2},{1... | collective-permute-start | bytes 2752520 | tf_op jit(solution)/shard_map/ppermute | solution.py:22
  111.6 12.6 %collective-permute-start.26 = (bf16[256,896]{1,0:T(8,128)(2,1)S(1)}, bf16[256,896]{1,0:T(8,128)(2,1)S(1)}, u32[]{:S(2)}, u32[]{:S(2)}) collective-permute-start(bf16[256,896]{1,0:T(8,128)(2,1)S(1)} %get-tuple-element.84), channel_id=1, source_target_pairs={{0,12},{4,8},{8,4},{12,0},{1,13},{5,9},{9,5},{13,1},{2,14},{6,10},... | collective-permute-start | bytes 1376264 | tf_op jit(solution)/shard_map/ppermute | solution.py:22
  113.6 10.8 %collective-permute-start.25 = (bf16[256,896]{1,0:T(8,128)(2,1)S(1)}, bf16[256,896]{1,0:T(8,128)(2,1)S(1)}, u32[]{:S(2)}, u32[]{:S(2)}) collective-permute-start(bf16[256,896]{1,0:T(8,128)(2,1)S(1)} %get-tuple-element.86), channel_id=1, source_target_pairs={{0,4},{4,0},{8,12},{12,8},{1,5},{5,1},{9,13},{13,9},{2,6},{6,2},{1... | collective-permute-start | bytes 1376264 | tf_op jit(solution)/shard_map/ppermute | solution.py:22

commit v5 on v4

--- a/solution.py
+++ b/solution.py
@@ -107,30 +107,28 @@
 
     near, away = split_grad(grad_out[0])
     sibling = swap(away, "core")
-    weight_l, weight_r = weight[:, :half], weight[:, half:]
-    other_l = swap(weight_l, "zl")
+    cut = own_rows * 5 // 16
+    other_top = swap(weight[:cut], "zl")
 
-    both = jnp.stack([near, after(sibling, weight_l)])
+    both = jnp.stack([near, sibling])
     hidden_l, hidden_r, slope_l, slope_r = make_hidden(after(pre_act, both))
     grad = jnp.stack([both[:, 0]] + [swap(both[:, s], "y", m) for s, m in ((1, "b"), (2, "a"), (3, "ab"))], 1)
     grad = grad.reshape(8, rows, 2 * own_rows)
 
     near_o, near_t = grad[..., own_rows:], grad[..., :own_rows]
     near_ob, near_ta = swap(near_o, "x", "b"), swap(near_t, "x", "a")
+    grad_far = swap(after(grad, other_top), "zh")
     hidden_l, hidden_r = after(hidden_l, grad), after(hidden_r, grad)
     hidden_lb, hidden_ra = swap(hidden_l, "y", "b"), swap(hidden_r, "y", "a")
-    near_ob, near_ta, hidden_lb, hidden_ra, other_l, grad = lax.optimization_barrier(
-        (near_ob, near_ta, hidden_lb, hidden_ra, other_l, grad)
-    )
+    near_ob, near_ta = lax.optimization_barrier((near_ob, near_ta))
     near_o, near_t = jnp.stack([near_o, near_ob]), jnp.stack([near_t, near_ta])
+    near_oa, near_tb = swap(near_o, "x", "a"), swap(near_t, "x", "b")
     hidden_l, hidden_r = jnp.stack([hidden_l, hidden_lb]), jnp.stack([hidden_r, hidden_ra])
-    grad_far = swap(grad, "zh")
-    near_oa, near_tb = swap(near_o, "x", "a"), swap(near_t, "x", "b")
     hidden_la, hidden_rb = swap(hidden_l, "y", "a"), swap(hidden_r, "y", "b")
+    other_low = swap(after(weight[cut:], grad_far), "zl")
     near_oa, near_tb, grad_far = lax.optimization_barrier((near_oa, near_tb, grad_far))
     far_o, far_t = grad_far[..., own_rows:], grad_far[..., :own_rows]
     far_ob, far_ta = swap(far_o, "x", "b"), swap(far_t, "x", "a")
-    other_r = swap(after(weight_r, grad_far), "zl")
     far_ob, far_ta = lax.optimization_barrier((far_ob, far_ta))
     far_o, far_t = jnp.stack([far_o, far_ob]), jnp.stack([far_t, far_ta])
     far_oa, far_tb = swap(far_o, "x", "a"), swap(far_t, "x", "b")
@@ -143,22 +141,20 @@
     grad_t = [near_t[0], far_t[0], near_tb[0], far_tb[0], near_t[1], far_t[1], near_tb[1], far_tb[1]]
     grad_other = jnp.stack(grad_o, 1).reshape(8 * tokens, own_rows)
     grad_own = jnp.stack(grad_t, 1).reshape(8 * tokens, own_rows)
-    grad_other, grad_own, hidden_l, hidden_r, other_l, other_r = lax.optimization_barrier(
-        (grad_other, grad_own, hidden_l, hidden_r, other_l, other_r)
+    grad_other, grad_own, hidden_l, hidden_r, other_top, other_low = lax.optimization_barrier(
+        (grad_other, grad_own, hidden_l, hidden_r, other_top, other_low)
     )
 
     grad_both = jnp.concatenate([grad_own, grad_other], 1)
-    w_l = jnp.concatenate([weight_l, other_l])
-    w_r = jnp.concatenate([weight_r, other_r])
+    weights = jnp.concatenate([weight, other_top, other_low])
+    w_l, w_r = weights[:, :half], weights[:, half:]
     edge = 4 * tokens
-    sent_l = outer(grad_other, hidden_l).astype(BF16)
-    got_l = swap(sent_l, "zl")
-    away_l = inner(after(grad_both, sent_l)[edge:], w_l).astype(BF16)
+    away_l = inner(grad_both[edge:], w_l).astype(BF16)
     away_r = inner(after(grad_both, away_l)[edge:], w_r).astype(BF16)
     back_l, back_r = swap(away_l, "core"), swap(away_r, "core")
-    sent_r = outer(after(grad_other, away_r), hidden_r).astype(BF16)
-    got_r = swap(sent_r, "zl")
-    back_l = after(back_l, sent_r)
+    sent_l = outer(after(grad_other, away_r), hidden_l).astype(BF16)
+    got_l = swap(sent_l, "zl")
+    back_l = after(back_l, sent_l)
     part_l = inner(grad_both[:edge], w_l) + back_l.astype(F32)
     part_l = part_l.reshape(2, 2, tokens, half)
     next_l = swap(part_l[1].astype(BF16), "y", "a")
@@ -166,15 +162,19 @@
     part_r = inner(grad_both[:edge], w_r) + back_r.astype(F32)
     part_r = part_r.reshape(2, 2, tokens, half)
     next_r = swap(part_r[:, 1].astype(BF16), "y", "b")
-    kept_l = outer(after(grad_own, part_r), hidden_l)
+    sent_r = outer(after(grad_other, part_r), hidden_r).astype(BF16)
+    got_r = swap(sent_r, "zl")
+    next_l, next_r, got_l, sent_r = lax.optimization_barrier((next_l, next_r, got_l, sent_r))
+    give_l = (part_l[0, 1] + next_l[1].astype(F32)).astype(BF16)
+    give_r = (part_r[1, 0] + next_r[1].astype(F32)).astype(BF16)
+    far_l, far_r = swap(give_l, "y", "b"), swap(give_r, "y", "a")
+    kept_l = outer(after(grad_own, give_l, give_r), hidden_l)
     kept_r = outer(after(grad_own, kept_l), hidden_r)
-    next_l, next_r, kept_l, kept_r = lax.optimization_barrier((next_l, next_r, kept_l, kept_r))
-    far_l = swap((part_l[0, 1] + next_l[1].astype(F32)).astype(BF16), "y", "b")
-    far_r = swap((part_r[1, 0] + next_r[1].astype(F32)).astype(BF16), "y", "a")
     own_l = part_l[0, 0] + next_l[0].astype(F32)
     own_r = part_r[0, 0] + next_r[0].astype(F32)
+    kept_l, kept_r, far_l, far_r = lax.optimization_barrier((kept_l, kept_r, far_l, far_r))
     grad_pre = finish(slope_l, slope_r, own_l, own_r, far_l, far_r)
-    kept_l = (kept_l + after(got_l, own_l, own_r).astype(F32)).astype(BF16)
+    kept_l = (kept_l + got_l.astype(F32)).astype(BF16)
     kept_r = (kept_r + after(got_r, grad_pre).astype(F32)).astype(BF16)
     return (grad_pre, jnp.concatenate([kept_l, kept_r], 1))
 

time: 128 us -> 121 us (0.945)
  waiting for transfers between devices: 62.9 us -> 55.2 us
    ppermute x29, waiting for transfers between devices: 62.9 us -> 55.2 us  [swap(): return lax.ppermute(value, axis, [(i, move(i)) for i in range(SIZES[axis])])]
  transfers between devices with their start and end apart: 29 -> 29, of which waited for: 15 -> 17; matrix products, arithmetic and copies ran while one was open for 15% -> 18% of each run, Pallas kernels for 2% -> 2%
where the time goes in v5:
time: 121 us; the launch traced here: 120 us
  waiting for transfers between devices  55.2 us (46%)
  starting transfers between devices  34.6 us (29%)
  matrix products  18.8 us (16%)
  local copies, waits for them, and re-layouts  4.88 us (4%)
  other arithmetic  3.54 us (3%)
  Pallas kernels  2.13 us (2%)
    ppermute x29, waiting for transfers between devices, swap(): return lax.ppermute(value, axis, [(i, move(i)) for i in range(SIZES[axis])])  55.2 us
    ppermute x29, starting transfers between devices, swap(): return lax.ppermute(value, axis, [(i, move(i)) for i in range(SIZES[axis])])  34.6 us
    dot_general x4, matrix products, inner(): return jnp.dot(g, w, preferred_element_type=F32)  9.38 us
    dot_general x4, matrix products, outer(): lax.dot_general(g, h, (((0,), (0,)), ((), ())), preferred_element_type=F32)  9.37 us
  transfers between devices with their start and end apart: 29, of which 17 were waited for; matrix products, arithmetic and copies ran while one was open for 18% of the time, Pallas kernels for 2%

profile of v5, /device:TPU:0, one launch (start us, length us, event | category | flops | bytes accessed | tf_op | source)
XLA Modules:
  0.0 120.3 jit_solution(4480407749784164329)
XLA Ops:
  0.6 1.0 copy-done.1
  1.8 1.5 %collective-permute-done = bf16[4,32,1024]{2,1,0:T(8,128)(2,1)S(1)} collective-permute-done((bf16[4,32,1024]{2,1,0:T(8,128)(2,1)S(1)}, bf16[4,32,1024]{2,1,0:T(8,128)(2,1)S(1)}, u32[]{:S(2)}, u32[]{:S(2)}) %collective-permute-start) | collective-permute-done | bytes 262176 | tf_op jit(solution)/shard_map/ppermute | solution.py:22
  3.4 1.7 %collective-permute-start.1 = (bf16[2,32,1024]{2,1,0:T(8,128)(2,1)S(1)}, bf16[2,32,1024]{2,1,0:T(8,128)(2,1)S(1)}, u32[]{:S(2)}, u32[]{:S(2)}) collective-permute-start(bf16[2,32,1024]{2,1,0:T(8,128)(2,1)S(1)} %get-tuple-element.100), channel_id=1, source_target_pairs={{0,4},{4,0},{8,12},{12,8},{1,5},{5,1},{9,13},{13,9},{2,6},{6,2},{1... | collective-permute-start | bytes 393224 | tf_op jit(solution)/shard_map/ppermute | solution.py:22
  5.1 2.2 %collective-permute-start.2 = (bf16[2,32,1024]{2,1,0:T(8,128)(2,1)S(1)}, bf16[2,32,1024]{2,1,0:T(8,128)(2,1)S(1)}, u32[]{:S(2)}, u32[]{:S(2)}) collective-permute-start(bf16[2,32,1024]{2,1,0:T(8,128)(2,1)S(1)} %get-tuple-element.101), channel_id=1, source_target_pairs={{0,12},{4,8},{8,4},{12,0},{1,13},{5,9},{9,5},{13,1},{2,14},{6,10},... | collective-permute-start | bytes 393224 | tf_op jit(solution)/shard_map/ppermute | solution.py:22
  7.3 0.7 collective-permute-start.3
  8.0 1.1 slice.115
  9.1 2.0 %collective-permute-start.8 = (bf16[160,1792]{1,0:T(8,128)(2,1)S(1)}, bf16[160,1792]{1,0:T(8,128)(2,1)S(1)}, u32[]{:S(2)}, u32[]{:S(2)}) collective-permute-start(bf16[160,1792]{1,0:T(8,128)(2,1)S(1)} %slice.115), channel_id=1, source_target_pairs={{0,2},{2,0},{1,3},{3,1},{4,6},{6,4},{5,7},{7,5},{8,10},{10,8},{9,1... | collective-permute-start | bytes 1720328 | tf_op jit(solution)/shard_map/ppermute | solution.py:22
  11.2 0.8 shard_map.51
  12.1 0.8 collective-permute-done.2
  12.9 1.5 %collective-permute-done.3 = bf16[2,32,1024]{2,1,0:T(8,128)(2,1)S(1)} collective-permute-done((bf16[2,32,1024]{2,1,0:T(8,128)(2,1)S(1)}, bf16[2,32,1024]{2,1,0:T(8,128)(2,1)S(1)}, u32[]{:S(2)}, u32[]{:S(2)}) %collective-permute-start.3) | collective-permute-done | bytes 131104 | tf_op jit(solution)/shard_map/ppermute | solution.py:22
  14.6 2.8 %collective-permute-start.5 = (bf16[8,32,512]{2,1,0:T(8,128)(2,1)S(1)}, bf16[8,32,512]{2,1,0:T(8,128)(2,1)S(1)}, u32[]{:S(2)}, u32[]{:S(2)}) collective-permute-start(bf16[8,32,512]{2,1,0:T(8,128)(2,1)S(1)} %get-tuple-element.97), channel_id=1, source_target_pairs={{0,96},{32,64},{64,32},{96,0},{1,97},{33,65},{65,33},{97,1},{2,98}... | collective-permute-start | bytes 786440 | tf_op jit(solution)/shard_map/ppermute | solution.py:22
  17.8 2.3 %collective-permute-start.17 = (bf16[256,896]{1,0:T(8,128)(2,1)S(1)}, bf16[256,896]{1,0:T(8,128)(2,1)S(1)}, u32[]{:S(2)}, u32[]{:S(2)}) collective-permute-start(bf16[256,896]{1,0:T(8,128)(2,1)S(1)} %get-tuple-element.57), channel_id=1, source_target_pairs={{0,12},{4,8},{8,4},{12,0},{1,13},{5,9},{9,5},{13,1},{2,14},{6,10},... | collective-permute-start | bytes 1376264 | tf_op jit(solution)/shard_map/ppermute | solution.py:22
  20.1 3.8 %collective-permute-done.8 = bf16[160,1792]{1,0:T(8,128)(2,1)S(1)} collective-permute-done((bf16[160,1792]{1,0:T(8,128)(2,1)S(1)}, bf16[160,1792]{1,0:T(8,128)(2,1)S(1)}, u32[]{:S(2)}, u32[]{:S(2)}) %collective-permute-start.8) | collective-permute-done | bytes 573472 | tf_op jit(solution)/shard_map/ppermute | solution.py:22
  23.8 3.7 %collective-permute-start.9 = (bf16[8,32,1024]{2,1,0:T(8,128)(2,1)S(1)}, bf16[8,32,1024]{2,1,0:T(8,128)(2,1)S(1)}, u32[]{:S(2)}, u32[]{:S(2)}) collective-permute-start(bf16[8,32,1024]{2,1,0:T(8,128)(2,1)S(1)} %bitcast.140), channel_id=1, source_target_pairs={{0,16},{16,0},{1,17},{17,1},{2,18},{18,2},{3,19},{19,3},{4,20},{20... | collective-permute-start | bytes 1572872 | tf_op jit(solution)/shard_map/ppermute | solution.py:22
  27.6 2.8 %collective-permute-start.6 = (bf16[2,8,32,512]{3,2,1,0:T(8,128)(2,1)S(1)}, bf16[2,8,32,512]{3,2,1,0:T(8,128)(2,1)S(1)}, u32[]{:S(2)}, u32[]{:S(2)}) collective-permute-start(bf16[2,8,32,512]{3,2,1,0:T(8,128)(2,1)S(1)} %pad_maximum_fusion.8), channel_id=1, source_target_pairs={{0,96},{32,64},{64,32},{96,0},{1,97},{33,65},{65,33},{97,1},{2,98}... | collective-permute-start | bytes 1572872 | tf_op jit(solution)/shard_map/ppermute | solution.py:22
  31.0 1.0 collective-permute-start.18
  32.1 2.3 %collective-permute-start.15 = (bf16[2,256,896]{2,1,0:T(8,128)(2,1)S(1)}, bf16[2,256,896]{2,1,0:T(8,128)(2,1)S(1)}, u32[]{:S(2)}, u32[]{:S(2)}) collective-permute-start(bf16[2,256,896]{2,1,0:T(8,128)(2,1)S(1)} %pad_maximum_fusion.4), channel_id=1, source_target_pairs={{0,12},{4,8},{8,4},{12,0},{1,13},{5,9},{9,5},{13,1},{2,14},{6,10},... | collective-permute-start | bytes 2752520 | tf_op jit(solution)/shard_map/ppermute | solution.py:22
  34.4 4.0 %collective-permute-done.9 = bf16[8,32,1024]{2,1,0:T(8,128)(2,1)S(1)} collective-permute-done((bf16[8,32,1024]{2,1,0:T(8,128)(2,1)S(1)}, bf16[8,32,1024]{2,1,0:T(8,128)(2,1)S(1)}, u32[]{:S(2)}, u32[]{:S(2)}) %collective-permute-start.9) | collective-permute-done | bytes 524320 | tf_op jit(solution)/shard_map/ppermute | solution.py:22
  38.4 1.2 %collective-permute-start.20 = (bf16[352,1792]{1,0:T(8,128)(2,1)S(1)}, bf16[352,1792]{1,0:T(8,128)(2,1)S(1)}, u32[]{:S(2)}, u32[]{:S(2)}) collective-permute-start(bf16[352,1792]{1,0:T(8,128)(2,1)S(1)} %slice.128), channel_id=1, source_target_pairs={{0,2},{2,0},{1,3},{3,1},{4,6},{6,4},{5,7},{7,5},{8,10},{10,8},{9,1... | collective-permute-start | bytes 3784712 | tf_op jit(solution)/shard_map/ppermute | solution.py:22
  39.6 1.5 %collective-permute-done.6 = bf16[2,8,32,512]{3,2,1,0:T(8,128)(2,1)S(1)} collective-permute-done((bf16[2,8,32,512]{3,2,1,0:T(8,128)(2,1)S(1)}, bf16[2,8,32,512]{3,2,1,0:T(8,128)(2,1)S(1)}, u32[]{:S(2)}, u32[]{:S(2)}) %collective-permute-start.6) | collective-permute-done | bytes 524320 | tf_op jit(solution)/shard_map/ppermute | solution.py:22
  41.1 1.4 %collective-permute-done.7 = bf16[2,8,32,512]{3,2,1,0:T(8,128)(2,1)S(1)} collective-permute-done((bf16[2,8,32,512]{3,2,1,0:T(8,128)(2,1)S(1)}, bf16[2,8,32,512]{3,2,1,0:T(8,128)(2,1)S(1)}, u32[]{:S(2)}, u32[]{:S(2)}) %collective-permute-start.7) | collective-permute-done | bytes 524320 | tf_op jit(solution)/shard_map/ppermute | solution.py:22
  42.6 1.4 %collective-permute-start.11 = (bf16[8,32,512]{2,1,0:T(8,128)(2,1)S(1)}, bf16[8,32,512]{2,1,0:T(8,128)(2,1)S(1)}, u32[]{:S(2)}, u32[]{:S(2)}) collective-permute-start(bf16[8,32,512]{2,1,0:T(8,128)(2,1)S(1)} %get-tuple-element.89), channel_id=1, source_target_pairs={{0,96},{32,64},{64,32},{96,0},{1,97},{33,65},{65,33},{97,1},{2,98}... | collective-permute-start | bytes 786440 | tf_op jit(solution)/shard_map/ppermute | solution.py:22
  44.1 6.1 %collective-permute-done.11 = bf16[8,32,512]{2,1,0:T(8,128)(2,1)S(1)} collective-permute-done((bf16[8,32,512]{2,1,0:T(8,128)(2,1)S(1)}, bf16[8,32,512]{2,1,0:T(8,128)(2,1)S(1)}, u32[]{:S(2)}, u32[]{:S(2)}) %collective-permute-start.11) | collective-permute-done | bytes 262176 | tf_op jit(solution)/shard_map/ppermute | solution.py:22
  50.5 2.0 %collective-permute-start.12 = (bf16[2,8,32,512]{3,2,1,0:T(8,128)(2,1)S(1)}, bf16[2,8,32,512]{3,2,1,0:T(8,128)(2,1)S(1)}, u32[]{:S(2)}, u32[]{:S(2)}) collective-permute-start(bf16[2,8,32,512]{3,2,1,0:T(8,128)(2,1)S(1)} %pad_maximum_fusion.10), channel_id=1, source_target_pairs={{0,96},{32,64},{64,32},{96,0},{1,97},{33,65},{65,33},{97,1},{2,98}... | collective-permute-start | bytes 1572872 | tf_op jit(solution)/shard_map/ppermute | solution.py:22
  52.6 0.4 collective-permute-done.15
  53.7 0.7 collective-permute-start.19
  54.6 7.6 %collective-permute-done.13 = bf16[2,8,32,512]{3,2,1,0:T(8,128)(2,1)S(1)} collective-permute-done((bf16[2,8,32,512]{3,2,1,0:T(8,128)(2,1)S(1)}, bf16[2,8,32,512]{3,2,1,0:T(8,128)(2,1)S(1)}, u32[]{:S(2)}, u32[]{:S(2)}) %collective-permute-start.13) | collective-permute-done | bytes 524320 | tf_op jit(solution)/shard_map/ppermute | solution.py:22
  63.3 0.5 pad_maximum_fusion
  63.8 2.3 %collective-permute-done.20 = bf16[352,1792]{1,0:T(8,128)(2,1)S(1)} collective-permute-done((bf16[352,1792]{1,0:T(8,128)(2,1)S(1)}, bf16[352,1792]{1,0:T(8,128)(2,1)S(1)}, u32[]{:S(2)}, u32[]{:S(2)}) %collective-permute-start.20) | collective-permute-done | bytes 1261600 | tf_op jit(solution)/shard_map/ppermute | solution.py:22
  66.9 2.3 %fusion.15 = bf16[1024,896]{1,0:T(8,128)(2,1)S(1)} fusion(bf16[2048,1024]{1,0:T(8,128)(2,1)S(1)} %constant_dynamic-update-slice_fusion.5, bf16[1024,1792]{1,0:T(8,128)(2,1)S(1)} %constant_dynamic-update-slice_fusion.7), kind=kOutput, calls=%fused_computation.19 | convolution fusion | flops 1879965696 | bytes 5767168 | tf_op jit(solution)/shard_map/dot_general | solution.py:99
  69.3 2.3 %fusion.12 = bf16[1024,896]{1,0:T(8,128)(2,1)S(1)} fusion(bf16[2048,1024]{1,0:T(8,128)(2,1)S(1)} %constant_dynamic-update-slice_fusion.5, bf16[1024,1792]{1,0:T(8,128)(2,1)S(1)} %constant_dynamic-update-slice_fusion.7), kind=kOutput, calls=%fused_computation.18 | convolution fusion | flops 1879965696 | bytes 5767168 | tf_op jit(solution)/shard_map/dot_general | solution.py:99
  71.7 0.6 collective-permute-start.23
  72.2 2.3 %convolution_convert_fusion.1 = bf16[512,896]{1,0:T(8,128)(2,1)S(1)} fusion(bf16[2048,512]{1,0:T(8,128)(2,1)S(1)} %bitcast.137, bf16[2048,896]{1,0:T(8,128)(2,1)S(1)} %bitcast.147), kind=kOutput, calls=%fused_computation.25 | convolution fusion | flops 1879506944 | bytes 6684672 | tf_op jit(solution)/shard_map/dot_general | solution.py:95
  74.6 1.0 collective-permute-start.25
  75.6 2.4 %convert_add_fusion.1 = f32[1024,896]{1,0:T(8,128)S(1)} fusion(bf16[1024,896]{1,0:T(8,128)(2,1)S(1)} %collective-permute-done.21, bf16[2048,1024]{1,0:T(8,128)(2,1)S(1)} %constant_dynamic-update-slice_fusion.5, bf16[1024,1792]{1,0:T(8,128)(2,1)S(1)} %constant_dynamic-update-slice_fusion.7), kind=kOutput, calls=%fused_computation.2 | convolution fusion | flops 1880883200 | bytes 9437184 | tf_op jit(solution)/shard_map/dot_general | solution.py:99
  78.1 2.4 %convert_add_fusion = f32[1024,896]{1,0:T(8,128)S(1)} fusion(bf16[1024,896]{1,0:T(8,128)(2,1)S(1)} %collective-permute-done.23, bf16[2048,1024]{1,0:T(8,128)(2,1)S(1)} %constant_dynamic-update-slice_fusion.5, bf16[1024,1792]{1,0:T(8,128)(2,1)S(1)} %constant_dynamic-update-slice_fusion.7), kind=kOutput, calls=%fused_computation.1 | convolution fusion | flops 1880883200 | bytes 9437184 | tf_op jit(solution)/shard_map/dot_general | solution.py:99
  80.6 2.1 %collective-permute-start.22 = (bf16[2,256,896]{2,1,0:T(8,128)(2,1)S(1)}, bf16[2,256,896]{2,1,0:T(8,128)(2,1)S(1)}, u32[]{:S(2)}, u32[]{:S(2)}) collective-permute-start(bf16[2,256,896]{2,1,0:T(8,128)(2,1)S(1)} %bitcast.156), channel_id=1, source_target_pairs={{0,12},{4,8},{8,4},{12,0},{1,13},{5,9},{9,5},{13,1},{2,14},{6,10},... | collective-permute-start | bytes 2752520 | tf_op jit(solution)/shard_map/ppermute | solution.py:22
  82.9 2.3 %convolution_convert_fusion = bf16[512,896]{1,0:T(8,128)(2,1)S(1)} fusion(bf16[2048,512]{1,0:T(8,128)(2,1)S(1)} %bitcast.138, bf16[2048,896]{1,0:T(8,128)(2,1)S(1)} %bitcast.161), kind=kOutput, calls=%fused_computation.24 | convolution fusion | flops 1879506944 | bytes 6684672 | tf_op jit(solution)/shard_map/dot_general | solution.py:95
  85.2 1.4 %collective-permute-start.28 = (bf16[512,896]{1,0:T(8,128)(2,1)S(1)}, bf16[512,896]{1,0:T(8,128)(2,1)S(1)}, u32[]{:S(2)}, u32[]{:S(2)}) collective-permute-start(bf16[512,896]{1,0:T(8,128)(2,1)S(1)} %convolution_convert_fusion), channel_id=1, source_target_pairs={{0,2},{2,0},{1,3},{3,1},{4,6},{6,4},{5,7},{7,5},{8,10},{10,8},{9,1... | collective-permute-start | bytes 2752520 | tf_op jit(solution)/shard_map/ppermute | solution.py:22
  86.6 11.2 %collective-permute-done.25 = bf16[512,896]{1,0:T(8,128)(2,1)S(1)} collective-permute-done((bf16[512,896]{1,0:T(8,128)(2,1)S(1)}, bf16[512,896]{1,0:T(8,128)(2,1)S(1)}, u32[]{:S(2)}, u32[]{:S(2)}) %collective-permute-start.25) | collective-permute-done | bytes 917536 | tf_op jit(solution)/shard_map/ppermute | solution.py:22
  97.9 6.0 %collective-permute-done.22 = bf16[2,256,896]{2,1,0:T(8,128)(2,1)S(1)} collective-permute-done((bf16[2,256,896]{2,1,0:T(8,128)(2,1)S(1)}, bf16[2,256,896]{2,1,0:T(8,128)(2,1)S(1)}, u32[]{:S(2)}, u32[]{:S(2)}) %collective-permute-start.22) | collective-permute-done | bytes 917536 | tf_op jit(solution)/shard_map/ppermute | solution.py:22
  103.9 0.6 collective-permute-done.24
  104.7 1.6 %collective-permute-start.27 = (bf16[256,896]{1,0:T(8,128)(2,1)S(1)}, bf16[256,896]{1,0:T(8,128)(2,1)S(1)}, u32[]{:S(2)}, u32[]{:S(2)}) collective-permute-start(bf16[256,896]{1,0:T(8,128)(2,1)S(1)} %get-tuple-element.80), channel_id=1, source_target_pairs={{0,12},{4,8},{8,4},{12,0},{1,13},{5,9},{9,5},{13,1},{2,14},{6,10},... | collective-permute-start | bytes 1376264 | tf_op jit(solution)/shard_map/ppermute | solution.py:22
  106.3 2.3 %fusion.42 = f32[512,896]{1,0:T(8,128)S(1)} fusion(bf16[2048,512]{1,0:T(8,128)(2,1)S(1)} %bitcast.134, bf16[2048,896]{1,0:T(8,128)(2,1)S(1)} %bitcast.148), kind=kOutput, calls=%fused_computation.96 | convolution fusion | flops 1879048192 | bytes 7602176 | tf_op jit(solution)/shard_map/dot_general | solution.py:95
  108.7 2.3 %fusion.43 = f32[512,896]{1,0:T(8,128)S(1)} fusion(bf16[2048,512]{1,0:T(8,128)(2,1)S(1)} %bitcast.135, bf16[2048,896]{1,0:T(8,128)(2,1)S(1)} %bitcast.162), kind=kOutput, calls=%fused_computation.97 | convolution fusion | flops 1879048192 | bytes 7602176 | tf_op jit(solution)/shard_map/dot_general | solution.py:95
  111.0 6.0 %collective-permute-done.27.far_r = bf16[256,896]{1,0:T(8,128)(2,1)S(1)} collective-permute-done((bf16[256,896]{1,0:T(8,128)(2,1)S(1)}, bf16[256,896]{1,0:T(8,128)(2,1)S(1)}, u32[]{:S(2)}, u32[]{:S(2)}) %collective-permute-start.27) | collective-permute-done | bytes 458784 | tf_op jit(solution)/shard_map/ppermute | solution.py:22
  117.3 1.3 %shard_map.52 = bf16[256,1792]{1,0:T(8,128)(2,1)} custom-call(f32[256,896]{1,0:T(8,128)S(1)} %get-tuple-element.44.slope_l, f32[256,896]{1,0:T(8,128)S(1)} %get-tuple-element.45.slope_r, f32[256,896]{1,0:T(8,128)S(1)} %get-tuple-element.83.own_l, f32[256,896]{1,0:T(8,128)S(1)} %get-tuple-element.81.own_r, ...), custom_call_target="tpu_custom_call" | custom-call | tf_op jit(solution)/shard_map/pallas_call | solution.py:91
  118.9 1.4 %pad_maximum_fusion.3 = bf16[512,1792]{1,0:T(8,128)(2,1)} fusion(bf16[512,896]{1,0:T(8,128)(2,1)S(1)} %add_convert_fusion, bf16[512,896]{1,0:T(8,128)(2,1)S(1)} %add_convert_fusion.1), kind=kLoop, calls=%fused_computation.15 | loop fusion | flops 3670016 | bytes 3670016 | tf_op jit(solution)/shard_map/concatenate | solution.py:179
  (75 shorter events, 6.0 us)
Async XLA Ops:
  0.6 1.0 copy-start.1
  1.7 9.5 %copy-start.2 = (bf16[512,1792]{1,0:T(8,128)(2,1)S(1)}, bf16[512,1792]{1,0:T(8,128)(2,1)}, u32[]{:S(2)}) copy-start(bf16[512,1792]{1,0:T(8,128)(2,1)} %param.5) | copy-start | bytes 5505028
  1.7 1.6 %collective-permute-start = (bf16[4,32,1024]{2,1,0:T(8,128)(2,1)S(1)}, bf16[4,32,1024]{2,1,0:T(8,128)(2,1)S(1)}, u32[]{:S(2)}, u32[]{:S(2)}) collective-permute-start(bf16[4,32,1024]{2,1,0:T(8,128)(2,1)S(1)} %get-tuple-element.42), channel_id=1, source_target_pairs={{0,1},{1,0},{2,3},{3,2},{4,5},{5,4},{6,7},{7,6},{8,9},{9,8},{10,11... | collective-permute-start | bytes 786440 | tf_op jit(solution)/shard_map/ppermute | solution.py:22
  3.4 7.8 %copy-start = (bf16[256,1792]{1,0:T(8,128)(2,1)S(1)}, bf16[256,1792]{1,0:T(8,128)(2,1)}, u32[]{:S(2)}) copy-start(bf16[256,1792]{1,0:T(8,128)(2,1)} %pre) | copy-start | bytes 2752516
  3.4 8.7 %collective-permute-start.1 = (bf16[2,32,1024]{2,1,0:T(8,128)(2,1)S(1)}, bf16[2,32,1024]{2,1,0:T(8,128)(2,1)S(1)}, u32[]{:S(2)}, u32[]{:S(2)}) collective-permute-start(bf16[2,32,1024]{2,1,0:T(8,128)(2,1)S(1)} %get-tuple-element.100), channel_id=1, source_target_pairs={{0,4},{4,0},{8,12},{12,8},{1,5},{5,1},{9,13},{13,9},{2,6},{6,2},{1... | collective-permute-start | bytes 393224 | tf_op jit(solution)/shard_map/ppermute | solution.py:22
  5.1 7.8 %collective-permute-start.2 = (bf16[2,32,1024]{2,1,0:T(8,128)(2,1)S(1)}, bf16[2,32,1024]{2,1,0:T(8,128)(2,1)S(1)}, u32[]{:S(2)}, u32[]{:S(2)}) collective-permute-start(bf16[2,32,1024]{2,1,0:T(8,128)(2,1)S(1)} %get-tuple-element.101), channel_id=1, source_target_pairs={{0,12},{4,8},{8,4},{12,0},{1,13},{5,9},{9,5},{13,1},{2,14},{6,10},... | collective-permute-start | bytes 393224 | tf_op jit(solution)/shard_map/ppermute | solution.py:22
  7.3 7.1 %collective-permute-start.3 = (bf16[2,32,1024]{2,1,0:T(8,128)(2,1)S(1)}, bf16[2,32,1024]{2,1,0:T(8,128)(2,1)S(1)}, u32[]{:S(2)}, u32[]{:S(2)}) collective-permute-start(bf16[2,32,1024]{2,1,0:T(8,128)(2,1)S(1)} %get-tuple-element.102), channel_id=1, source_target_pairs={{0,8},{4,12},{8,0},{12,4},{1,9},{5,13},{9,1},{13,5},{2,10},{6,14},... | collective-permute-start | bytes 393224 | tf_op jit(solution)/shard_map/ppermute | solution.py:22
  9.1 14.7 %collective-permute-start.8 = (bf16[160,1792]{1,0:T(8,128)(2,1)S(1)}, bf16[160,1792]{1,0:T(8,128)(2,1)S(1)}, u32[]{:S(2)}, u32[]{:S(2)}) collective-permute-start(bf16[160,1792]{1,0:T(8,128)(2,1)S(1)} %slice.115), channel_id=1, source_target_pairs={{0,2},{2,0},{1,3},{3,1},{4,6},{6,4},{5,7},{7,5},{8,10},{10,8},{9,1... | collective-permute-start | bytes 1720328 | tf_op jit(solution)/shard_map/ppermute | solution.py:22
  14.6 12.9 %collective-permute-start.5 = (bf16[8,32,512]{2,1,0:T(8,128)(2,1)S(1)}, bf16[8,32,512]{2,1,0:T(8,128)(2,1)S(1)}, u32[]{:S(2)}, u32[]{:S(2)}) collective-permute-start(bf16[8,32,512]{2,1,0:T(8,128)(2,1)S(1)} %get-tuple-element.97), channel_id=1, source_target_pairs={{0,96},{32,64},{64,32},{96,0},{1,97},{33,65},{65,33},{97,1},{2,98}... | collective-permute-start | bytes 786440 | tf_op jit(solution)/shard_map/ppermute | solution.py:22
  17.5 10.1 %collective-permute-start.4 = (bf16[8,32,512]{2,1,0:T(8,128)(2,1)S(1)}, bf16[8,32,512]{2,1,0:T(8,128)(2,1)S(1)}, u32[]{:S(2)}, u32[]{:S(2)}) collective-permute-start(bf16[8,32,512]{2,1,0:T(8,128)(2,1)S(1)} %get-tuple-element.98), channel_id=1, source_target_pairs={{0,32},{32,0},{64,96},{96,64},{1,33},{33,1},{65,97},{97,65},{2,34}... | collective-permute-start | bytes 786440 | tf_op jit(solution)/shard_map/ppermute | solution.py:22
  17.8 13.1 %collective-permute-start.17 = (bf16[256,896]{1,0:T(8,128)(2,1)S(1)}, bf16[256,896]{1,0:T(8,128)(2,1)S(1)}, u32[]{:S(2)}, u32[]{:S(2)}) collective-permute-start(bf16[256,896]{1,0:T(8,128)(2,1)S(1)} %get-tuple-element.57), channel_id=1, source_target_pairs={{0,12},{4,8},{8,4},{12,0},{1,13},{5,9},{9,5},{13,1},{2,14},{6,10},... | collective-permute-start | bytes 1376264 | tf_op jit(solution)/shard_map/ppermute | solution.py:22
  20.1 11.9 %collective-permute-start.14 = (bf16[256,896]{1,0:T(8,128)(2,1)S(1)}, bf16[256,896]{1,0:T(8,128)(2,1)S(1)}, u32[]{:S(2)}, u32[]{:S(2)}) collective-permute-start(bf16[256,896]{1,0:T(8,128)(2,1)S(1)} %get-tuple-element.55), channel_id=1, source_target_pairs={{0,4},{4,0},{8,12},{12,8},{1,5},{5,1},{9,13},{13,9},{2,6},{6,2},{1... | collective-permute-start | bytes 1376264 | tf_op jit(solution)/shard_map/ppermute | solution.py:22
  23.8 14.5 %collective-permute-start.9 = (bf16[8,32,1024]{2,1,0:T(8,128)(2,1)S(1)}, bf16[8,32,1024]{2,1,0:T(8,128)(2,1)S(1)}, u32[]{:S(2)}, u32[]{:S(2)}) collective-permute-start(bf16[8,32,1024]{2,1,0:T(8,128)(2,1)S(1)} %bitcast.140), channel_id=1, source_target_pairs={{0,16},{16,0},{1,17},{17,1},{2,18},{18,2},{3,19},{19,3},{4,20},{20... | collective-permute-start | bytes 1572872 | tf_op jit(solution)/shard_map/ppermute | solution.py:22
  27.6 13.5 %collective-permute-start.6 = (bf16[2,8,32,512]{3,2,1,0:T(8,128)(2,1)S(1)}, bf16[2,8,32,512]{3,2,1,0:T(8,128)(2,1)S(1)}, u32[]{:S(2)}, u32[]{:S(2)}) collective-permute-start(bf16[2,8,32,512]{3,2,1,0:T(8,128)(2,1)S(1)} %pad_maximum_fusion.8), channel_id=1, source_target_pairs={{0,96},{32,64},{64,32},{96,0},{1,97},{33,65},{65,33},{97,1},{2,98}... | collective-permute-start | bytes 1572872 | tf_op jit(solution)/shard_map/ppermute | solution.py:22
  30.5 12.0 %collective-permute-start.7 = (bf16[2,8,32,512]{3,2,1,0:T(8,128)(2,1)S(1)}, bf16[2,8,32,512]{3,2,1,0:T(8,128)(2,1)S(1)}, u32[]{:S(2)}, u32[]{:S(2)}) collective-permute-start(bf16[2,8,32,512]{3,2,1,0:T(8,128)(2,1)S(1)} %pad_maximum_fusion.9), channel_id=1, source_target_pairs={{0,32},{32,0},{64,96},{96,64},{1,33},{33,1},{65,97},{97,65},{2,34}... | collective-permute-start | bytes 1572872 | tf_op jit(solution)/shard_map/ppermute | solution.py:22
  31.0 22.3 %collective-permute-start.18 = (bf16[2,256,896]{2,1,0:T(8,128)(2,1)S(1)}, bf16[2,256,896]{2,1,0:T(8,128)(2,1)S(1)}, u32[]{:S(2)}, u32[]{:S(2)}) collective-permute-start(bf16[2,256,896]{2,1,0:T(8,128)(2,1)S(1)} %pad_maximum_fusion.5), channel_id=1, source_target_pairs={{0,4},{4,0},{8,12},{12,8},{1,5},{5,1},{9,13},{13,9},{2,6},{6,2},{1... | collective-permute-start | bytes 2752520 | tf_op jit(solution)/shard_map/ppermute | solution.py:22
  32.1 20.9 %collective-permute-start.15 = (bf16[2,256,896]{2,1,0:T(8,128)(2,1)S(1)}, bf16[2,256,896]{2,1,0:T(8,128)(2,1)S(1)}, u32[]{:S(2)}, u32[]{:S(2)}) collective-permute-start(bf16[2,256,896]{2,1,0:T(8,128)(2,1)S(1)} %pad_maximum_fusion.4), channel_id=1, source_target_pairs={{0,12},{4,8},{8,4},{12,0},{1,13},{5,9},{9,5},{13,1},{2,14},{6,10},... | collective-permute-start | bytes 2752520 | tf_op jit(solution)/shard_map/ppermute | solution.py:22
  38.4 27.7 %collective-permute-start.20 = (bf16[352,1792]{1,0:T(8,128)(2,1)S(1)}, bf16[352,1792]{1,0:T(8,128)(2,1)S(1)}, u32[]{:S(2)}, u32[]{:S(2)}) collective-permute-start(bf16[352,1792]{1,0:T(8,128)(2,1)S(1)} %slice.128), channel_id=1, source_target_pairs={{0,2},{2,0},{1,3},{3,1},{4,6},{6,4},{5,7},{7,5},{8,10},{10,8},{9,1... | collective-permute-start | bytes 3784712 | tf_op jit(solution)/shard_map/ppermute | solution.py:22
  42.6 7.7 %collective-permute-start.11 = (bf16[8,32,512]{2,1,0:T(8,128)(2,1)S(1)}, bf16[8,32,512]{2,1,0:T(8,128)(2,1)S(1)}, u32[]{:S(2)}, u32[]{:S(2)}) collective-permute-start(bf16[8,32,512]{2,1,0:T(8,128)(2,1)S(1)} %get-tuple-element.89), channel_id=1, source_target_pairs={{0,96},{32,64},{64,32},{96,0},{1,97},{33,65},{65,33},{97,1},{2,98}... | collective-permute-start | bytes 786440 | tf_op jit(solution)/shard_map/ppermute | solution.py:22
  44.1 6.4 %collective-permute-start.10 = (bf16[8,32,512]{2,1,0:T(8,128)(2,1)S(1)}, bf16[8,32,512]{2,1,0:T(8,128)(2,1)S(1)}, u32[]{:S(2)}, u32[]{:S(2)}) collective-permute-start(bf16[8,32,512]{2,1,0:T(8,128)(2,1)S(1)} %get-tuple-element.90), channel_id=1, source_target_pairs={{0,32},{32,0},{64,96},{96,64},{1,33},{33,1},{65,97},{97,65},{2,34}... | collective-permute-start | bytes 786440 | tf_op jit(solution)/shard_map/ppermute | solution.py:22
  50.5 12.1 %collective-permute-start.12 = (bf16[2,8,32,512]{3,2,1,0:T(8,128)(2,1)S(1)}, bf16[2,8,32,512]{3,2,1,0:T(8,128)(2,1)S(1)}, u32[]{:S(2)}, u32[]{:S(2)}) collective-permute-start(bf16[2,8,32,512]{3,2,1,0:T(8,128)(2,1)S(1)} %pad_maximum_fusion.10), channel_id=1, source_target_pairs={{0,96},{32,64},{64,32},{96,0},{1,97},{33,65},{65,33},{97,1},{2,98}... | collective-permute-start | bytes 1572872 | tf_op jit(solution)/shard_map/ppermute | solution.py:22
  52.5 9.7 %collective-permute-start.13 = (bf16[2,8,32,512]{3,2,1,0:T(8,128)(2,1)S(1)}, bf16[2,8,32,512]{3,2,1,0:T(8,128)(2,1)S(1)}, u32[]{:S(2)}, u32[]{:S(2)}) collective-permute-start(bf16[2,8,32,512]{3,2,1,0:T(8,128)(2,1)S(1)} %pad_maximum_fusion.11), channel_id=1, source_target_pairs={{0,32},{32,0},{64,96},{96,64},{1,33},{33,1},{65,97},{97,65},{2,34}... | collective-permute-start | bytes 1572872 | tf_op jit(solution)/shard_map/ppermute | solution.py:22
  53.2 10.1 %collective-permute-start.16 = (bf16[4,256,896]{2,1,0:T(8,128)(2,1)S(1)}, bf16[4,256,896]{2,1,0:T(8,128)(2,1)S(1)}, u32[]{:S(2)}, u32[]{:S(2)}) collective-permute-start(bf16[4,256,896]{2,1,0:T(8,128)(2,1)S(1)} %pad_maximum_fusion.1), channel_id=1, source_target_pairs={{0,1},{1,0},{2,3},{3,2},{4,5},{5,4},{6,7},{7,6},{8,9},{9,8},{10,11... | collective-permute-start | bytes 5505032 | tf_op jit(solution)/shard_map/ppermute | solution.py:22
  53.7 9.2 %collective-permute-start.19 = (bf16[4,256,896]{2,1,0:T(8,128)(2,1)S(1)}, bf16[4,256,896]{2,1,0:T(8,128)(2,1)S(1)}, u32[]{:S(2)}, u32[]{:S(2)}) collective-permute-start(bf16[4,256,896]{2,1,0:T(8,128)(2,1)S(1)} %pad_maximum_fusion.2), channel_id=1, source_target_pairs={{0,1},{1,0},{2,3},{3,2},{4,5},{5,4},{6,7},{7,6},{8,9},{9,8},{10,11... | collective-permute-start | bytes 5505032 | tf_op jit(solution)/shard_map/ppermute | solution.py:22
  69.2 6.4 %collective-permute-start.21 = (bf16[1024,896]{1,0:T(8,128)(2,1)S(1)}, bf16[1024,896]{1,0:T(8,128)(2,1)S(1)}, u32[]{:S(2)}, u32[]{:S(2)}) collective-permute-start(bf16[1024,896]{1,0:T(8,128)(2,1)S(1)} %fusion.15), channel_id=1, source_target_pairs={{0,1},{1,0},{2,3},{3,2},{4,5},{5,4},{6,7},{7,6},{8,9},{9,8},{10,11... | collective-permute-start | bytes 5505032 | tf_op jit(solution)/shard_map/ppermute | solution.py:22
  71.7 6.4 %collective-permute-start.23 = (bf16[1024,896]{1,0:T(8,128)(2,1)S(1)}, bf16[1024,896]{1,0:T(8,128)(2,1)S(1)}, u32[]{:S(2)}, u32[]{:S(2)}) collective-permute-start(bf16[1024,896]{1,0:T(8,128)(2,1)S(1)} %fusion.12), channel_id=1, source_target_pairs={{0,1},{1,0},{2,3},{3,2},{4,5},{5,4},{6,7},{7,6},{8,9},{9,8},{10,11... | collective-permute-start | bytes 5505032 | tf_op jit(solution)/shard_map/ppermute | solution.py:22
  74.6 23.3 %collective-permute-start.25 = (bf16[512,896]{1,0:T(8,128)(2,1)S(1)}, bf16[512,896]{1,0:T(8,128)(2,1)S(1)}, u32[]{:S(2)}, u32[]{:S(2)}) collective-permute-start(bf16[512,896]{1,0:T(8,128)(2,1)S(1)} %convolution_convert_fusion.1), channel_id=1, source_target_pairs={{0,2},{2,0},{1,3},{3,1},{4,6},{6,4},{5,7},{7,5},{8,10},{10,8},{9,1... | collective-permute-start | bytes 2752520 | tf_op jit(solution)/shard_map/ppermute | solution.py:22
  80.6 23.3 %collective-permute-start.22 = (bf16[2,256,896]{2,1,0:T(8,128)(2,1)S(1)}, bf16[2,256,896]{2,1,0:T(8,128)(2,1)S(1)}, u32[]{:S(2)}, u32[]{:S(2)}) collective-permute-start(bf16[2,256,896]{2,1,0:T(8,128)(2,1)S(1)} %bitcast.156), channel_id=1, source_target_pairs={{0,12},{4,8},{8,4},{12,0},{1,13},{5,9},{9,5},{13,1},{2,14},{6,10},... | collective-permute-start | bytes 2752520 | tf_op jit(solution)/shard_map/ppermute | solution.py:22
  82.7 21.7 %collective-permute-start.24 = (bf16[2,256,896]{2,1,0:T(8,128)(2,1)S(1)}, bf16[2,256,896]{2,1,0:T(8,128)(2,1)S(1)}, u32[]{:S(2)}, u32[]{:S(2)}) collective-permute-start(bf16[2,256,896]{2,1,0:T(8,128)(2,1)S(1)} %fusion.22), channel_id=1, source_target_pairs={{0,4},{4,0},{8,12},{12,8},{1,5},{5,1},{9,13},{13,9},{2,6},{6,2},{1... | collective-permute-start | bytes 2752520 | tf_op jit(solution)/shard_map/ppermute | solution.py:22
  85.2 33.3 %collective-permute-start.28 = (bf16[512,896]{1,0:T(8,128)(2,1)S(1)}, bf16[512,896]{1,0:T(8,128)(2,1)S(1)}, u32[]{:S(2)}, u32[]{:S(2)}) collective-permute-start(bf16[512,896]{1,0:T(8,128)(2,1)S(1)} %convolution_convert_fusion), channel_id=1, source_target_pairs={{0,2},{2,0},{1,3},{3,1},{4,6},{6,4},{5,7},{7,5},{8,10},{10,8},{9,1... | collective-permute-start | bytes 2752520 | tf_op jit(solution)/shard_map/ppermute | solution.py:22
  104.7 12.2 %collective-permute-start.27 = (bf16[256,896]{1,0:T(8,128)(2,1)S(1)}, bf16[256,896]{1,0:T(8,128)(2,1)S(1)}, u32[]{:S(2)}, u32[]{:S(2)}) collective-permute-start(bf16[256,896]{1,0:T(8,128)(2,1)S(1)} %get-tuple-element.80), channel_id=1, source_target_pairs={{0,12},{4,8},{8,4},{12,0},{1,13},{5,9},{9,5},{13,1},{2,14},{6,10},... | collective-permute-start | bytes 1376264 | tf_op jit(solution)/shard_map/ppermute | solution.py:22
  106.3 11.0 %collective-permute-start.26 = (bf16[256,896]{1,0:T(8,128)(2,1)S(1)}, bf16[256,896]{1,0:T(8,128)(2,1)S(1)}, u32[]{:S(2)}, u32[]{:S(2)}) collective-permute-start(bf16[256,896]{1,0:T(8,128)(2,1)S(1)} %get-tuple-element.82), channel_id=1, source_target_pairs={{0,4},{4,0},{8,12},{12,8},{1,5},{5,1},{9,13},{13,9},{2,6},{6,2},{1... | collective-permute-start | bytes 1376264 | tf_op jit(solution)/shard_map/ppermute | solution.py:22

commit v6 on v5

--- a/solution.py
+++ b/solution.py
@@ -141,42 +141,48 @@
     grad_t = [near_t[0], far_t[0], near_tb[0], far_tb[0], near_t[1], far_t[1], near_tb[1], far_tb[1]]
     grad_other = jnp.stack(grad_o, 1).reshape(8 * tokens, own_rows)
     grad_own = jnp.stack(grad_t, 1).reshape(8 * tokens, own_rows)
-    grad_other, grad_own, hidden_l, hidden_r, other_top, other_low = lax.optimization_barrier(
-        (grad_other, grad_own, hidden_l, hidden_r, other_top, other_low)
-    )
+    grad_other, grad_own, hidden_l = lax.optimization_barrier((grad_other, grad_own, hidden_l))
 
-    grad_both = jnp.concatenate([grad_own, grad_other], 1)
-    weights = jnp.concatenate([weight, other_top, other_low])
+    grad_both = jnp.concatenate([grad_own, grad_other], 1).reshape(2, 2, 2, tokens, 2 * own_rows)
+    flat, pair = (2 * tokens, 2 * own_rows), (2, tokens, half)
+    sent_l = outer(grad_other, hidden_l).astype(BF16)
+    got_l = swap(sent_l, "zl")
+    weights = jnp.concatenate([weight, other_top, after(other_low, sent_l)])
     w_l, w_r = weights[:, :half], weights[:, half:]
-    edge = 4 * tokens
-    away_l = inner(grad_both[edge:], w_l).astype(BF16)
-    away_r = inner(after(grad_both, away_l)[edge:], w_r).astype(BF16)
-    back_l, back_r = swap(away_l, "core"), swap(away_r, "core")
-    sent_l = outer(after(grad_other, away_r), hidden_l).astype(BF16)
-    got_l = swap(sent_l, "zl")
-    back_l = after(back_l, sent_l)
-    part_l = inner(grad_both[:edge], w_l) + back_l.astype(F32)
-    part_l = part_l.reshape(2, 2, tokens, half)
-    next_l = swap(part_l[1].astype(BF16), "y", "a")
-    back_r = after(back_r, part_l)
-    part_r = inner(grad_both[:edge], w_r) + back_r.astype(F32)
-    part_r = part_r.reshape(2, 2, tokens, half)
-    next_r = swap(part_r[:, 1].astype(BF16), "y", "b")
-    sent_r = outer(after(grad_other, part_r), hidden_r).astype(BF16)
+    away_l1 = inner(after(grad_both, sent_l)[1, 1].reshape(flat), w_l).astype(BF16)
+    away_r1 = inner(after(grad_both, away_l1)[1, :, 1].reshape(flat), w_r).astype(BF16)
+    back_1 = swap(jnp.stack([away_l1, away_r1]), "core")
+    back_l1, back_r1 = back_1[0], back_1[1]
+    part_l1 = inner(grad_both[0, 1].reshape(flat), w_l) + after(back_l1, away_r1).astype(F32)
+    part_l1 = part_l1.astype(BF16)
+    next_l = swap(part_l1.reshape(pair), "y", "a")
+    part_r1 = inner(grad_both[0, :, 1].reshape(flat), w_r) + after(back_r1, part_l1).astype(F32)
+    part_r1 = part_r1.astype(BF16)
+    next_r = swap(part_r1.reshape(pair), "y", "b")
+    tick_2 = swap(part_r1[:16, :128], "core")
+    away_l0 = inner(after(grad_both, tick_2)[1, 0].reshape(flat), w_l).astype(BF16)
+    away_r0 = inner(after(grad_both, away_l0)[1, :, 0].reshape(flat), w_r).astype(BF16)
+    back_0 = swap(jnp.stack([away_l0, away_r0]), "core")
+    sent_r = outer(after(grad_other, away_r0), hidden_r).astype(BF16)
     got_r = swap(sent_r, "zl")
-    next_l, next_r, got_l, sent_r = lax.optimization_barrier((next_l, next_r, got_l, sent_r))
-    give_l = (part_l[0, 1] + next_l[1].astype(F32)).astype(BF16)
-    give_r = (part_r[1, 0] + next_r[1].astype(F32)).astype(BF16)
+    back_0 = after(back_0, sent_r)
+    part_l0 = (inner(grad_both[0, 0].reshape(flat), w_l) + back_0[0].astype(F32)).reshape(pair)
+    part_r0 = (inner(after(grad_both, part_l0)[0, :, 0].reshape(flat), w_r) + back_0[1].astype(F32)).reshape(pair)
+    next_l, next_r, got_l, part_l0, part_r0 = lax.optimization_barrier((next_l, next_r, got_l, part_l0, part_r0))
+    give_l = (part_l0[1] + next_l[1].astype(F32)).astype(BF16)
+    give_r = (part_r0[1] + next_r[1].astype(F32)).astype(BF16)
     far_l, far_r = swap(give_l, "y", "b"), swap(give_r, "y", "a")
     kept_l = outer(after(grad_own, give_l, give_r), hidden_l)
     kept_r = outer(after(grad_own, kept_l), hidden_r)
-    own_l = part_l[0, 0] + next_l[0].astype(F32)
-    own_r = part_r[0, 0] + next_r[0].astype(F32)
-    kept_l, kept_r, far_l, far_r = lax.optimization_barrier((kept_l, kept_r, far_l, far_r))
+    own_l = part_l0[0] + next_l[0].astype(F32)
+    own_r = part_r0[0] + next_r[0].astype(F32)
+    kept_l, kept_r = lax.optimization_barrier((kept_l, kept_r))
+    kept_l = (kept_l + got_l.astype(F32)).astype(BF16)
+    kept_r = (kept_r + got_r.astype(F32)).astype(BF16)
+    kept = jnp.concatenate([kept_l, kept_r], 1)
+    far_l, far_r, kept = lax.optimization_barrier((far_l, far_r, kept))
     grad_pre = finish(slope_l, slope_r, own_l, own_r, far_l, far_r)
-    kept_l = (kept_l + got_l.astype(F32)).astype(BF16)
-    kept_r = (kept_r + after(got_r, grad_pre).astype(F32)).astype(BF16)
-    return (grad_pre, jnp.concatenate([kept_l, kept_r], 1))
+    return (grad_pre, kept)
 
 
 def solution(mesh):

time: 121 us -> 119 us (0.983)
  waiting for transfers between devices: 55.2 us -> 47.4 us
  local copies, waits for them, and re-layouts: 4.88 us -> 9.15 us
    ppermute x29, waiting for transfers between devices: 55.2 us -> 47.4 us  [swap(): return lax.ppermute(value, axis, [(i, move(i)) for i in range(SIZES[axis])])]
    unnamed x23 -> x24, local copies, waits for them, and re-layouts: 1.94 us -> 5.21 us
    dot_general x4 -> x8, matrix products: 9.38 us -> 10.1 us  [inner(): return jnp.dot(g, w, preferred_element_type=F32)]
  transfers between devices with their start and end apart: 29 -> 29, of which waited for: 17 -> 20; matrix products, arithmetic and copies ran while one was open for 18% -> 25% of each run, Pallas kernels for 2% -> 1%
where the time goes in v6:
time: 119 us; the launch traced here: 118 us
  waiting for transfers between devices  47.4 us (40%)
  starting transfers between devices  34.2 us (29%)
  matrix products  19.5 us (16%)
  local copies, waits for them, and re-layouts  9.15 us (8%)
  other arithmetic  4.68 us (4%)
  Pallas kernels  2.06 us (2%)
    ppermute x29, waiting for transfers between devices, swap(): return lax.ppermute(value, axis, [(i, move(i)) for i in range(SIZES[axis])])  47.4 us
    ppermute x29, starting transfers between devices, swap(): return lax.ppermute(value, axis, [(i, move(i)) for i in range(SIZES[axis])])  34.2 us
    dot_general x8, matrix products, inner(): return jnp.dot(g, w, preferred_element_type=F32)  10.1 us
    dot_general x4, matrix products, outer(): lax.dot_general(g, h, (((0,), (0,)), ((), ())), preferred_element_type=F32)  9.38 us
    unnamed x24, local copies, waits for them, and re-layouts  5.21 us
  transfers between devices with their start and end apart: 29, of which 20 were waited for; matrix products, arithmetic and copies ran while one was open for 25% of the time, Pallas kernels for 1%

profile of v6, /device:TPU:0, one launch (start us, length us, event | category | flops | bytes accessed | tf_op | source)
XLA Modules:
  0.0 118.2 jit_solution(9336704799986617522)
XLA Ops:
  1.8 1.5 %collective-permute-done = bf16[4,32,1024]{2,1,0:T(8,128)(2,1)S(1)} collective-permute-done((bf16[4,32,1024]{2,1,0:T(8,128)(2,1)S(1)}, bf16[4,32,1024]{2,1,0:T(8,128)(2,1)S(1)}, u32[]{:S(2)}, u32[]{:S(2)}) %collective-permute-start) | collective-permute-done | bytes 262176 | tf_op jit(solution)/shard_map/ppermute | solution.py:22
  3.4 1.7 %collective-permute-start.1 = (bf16[2,32,1024]{2,1,0:T(8,128)(2,1)S(1)}, bf16[2,32,1024]{2,1,0:T(8,128)(2,1)S(1)}, u32[]{:S(2)}, u32[]{:S(2)}) collective-permute-start(bf16[2,32,1024]{2,1,0:T(8,128)(2,1)S(1)} %get-tuple-element.110), channel_id=1, source_target_pairs={{0,4},{4,0},{8,12},{12,8},{1,5},{5,1},{9,13},{13,9},{2,6},{6,2},{1... | collective-permute-start | bytes 393224 | tf_op jit(solution)/shard_map/ppermute | solution.py:22
  5.1 2.2 %collective-permute-start.2 = (bf16[2,32,1024]{2,1,0:T(8,128)(2,1)S(1)}, bf16[2,32,1024]{2,1,0:T(8,128)(2,1)S(1)}, u32[]{:S(2)}, u32[]{:S(2)}) collective-permute-start(bf16[2,32,1024]{2,1,0:T(8,128)(2,1)S(1)} %get-tuple-element.111), channel_id=1, source_target_pairs={{0,12},{4,8},{8,4},{12,0},{1,13},{5,9},{9,5},{13,1},{2,14},{6,10},... | collective-permute-start | bytes 393224 | tf_op jit(solution)/shard_map/ppermute | solution.py:22
  8.0 1.1 slice.133
  9.1 2.0 %collective-permute-start.8 = (bf16[160,1792]{1,0:T(8,128)(2,1)S(1)}, bf16[160,1792]{1,0:T(8,128)(2,1)S(1)}, u32[]{:S(2)}, u32[]{:S(2)}) collective-permute-start(bf16[160,1792]{1,0:T(8,128)(2,1)S(1)} %slice.133), channel_id=1, source_target_pairs={{0,2},{2,0},{1,3},{3,1},{4,6},{6,4},{5,7},{7,5},{8,10},{10,8},{9,1... | collective-permute-start | bytes 1720328 | tf_op jit(solution)/shard_map/ppermute | solution.py:22
  11.1 1.8 %collective-permute-done.2 = bf16[2,32,1024]{2,1,0:T(8,128)(2,1)S(1)} collective-permute-done((bf16[2,32,1024]{2,1,0:T(8,128)(2,1)S(1)}, bf16[2,32,1024]{2,1,0:T(8,128)(2,1)S(1)}, u32[]{:S(2)}, u32[]{:S(2)}) %collective-permute-start.2) | collective-permute-done | bytes 131104 | tf_op jit(solution)/shard_map/ppermute | solution.py:22
  12.9 1.5 %collective-permute-done.3 = bf16[2,32,1024]{2,1,0:T(8,128)(2,1)S(1)} collective-permute-done((bf16[2,32,1024]{2,1,0:T(8,128)(2,1)S(1)}, bf16[2,32,1024]{2,1,0:T(8,128)(2,1)S(1)}, u32[]{:S(2)}, u32[]{:S(2)}) %collective-permute-start.3) | collective-permute-done | bytes 131104 | tf_op jit(solution)/shard_map/ppermute | solution.py:22
  14.6 2.8 %collective-permute-start.5 = (bf16[8,32,512]{2,1,0:T(8,128)(2,1)S(1)}, bf16[8,32,512]{2,1,0:T(8,128)(2,1)S(1)}, u32[]{:S(2)}, u32[]{:S(2)}) collective-permute-start(bf16[8,32,512]{2,1,0:T(8,128)(2,1)S(1)} %get-tuple-element.107), channel_id=1, source_target_pairs={{0,96},{32,64},{64,32},{96,0},{1,97},{33,65},{65,33},{97,1},{2,98}... | collective-permute-start | bytes 786440 | tf_op jit(solution)/shard_map/ppermute | solution.py:22
  17.9 1.1 copy-done
  19.8 2.3 %collective-permute-start.23 = (bf16[256,896]{1,0:T(8,128)(2,1)S(1)}, bf16[256,896]{1,0:T(8,128)(2,1)S(1)}, u32[]{:S(2)}, u32[]{:S(2)}) collective-permute-start(bf16[256,896]{1,0:T(8,128)(2,1)S(1)} %get-tuple-element.71), channel_id=1, source_target_pairs={{0,12},{4,8},{8,4},{12,0},{1,13},{5,9},{9,5},{13,1},{2,14},{6,10},... | collective-permute-start | bytes 1376264 | tf_op jit(solution)/shard_map/ppermute | solution.py:22
  23.8 3.7 %collective-permute-start.9 = (bf16[8,32,1024]{2,1,0:T(8,128)(2,1)S(1)}, bf16[8,32,1024]{2,1,0:T(8,128)(2,1)S(1)}, u32[]{:S(2)}, u32[]{:S(2)}) collective-permute-start(bf16[8,32,1024]{2,1,0:T(8,128)(2,1)S(1)} %bitcast.153), channel_id=1, source_target_pairs={{0,16},{16,0},{1,17},{17,1},{2,18},{18,2},{3,19},{19,3},{4,20},{20... | collective-permute-start | bytes 1572872 | tf_op jit(solution)/shard_map/ppermute | solution.py:22
  27.6 2.8 %collective-permute-start.6 = (bf16[2,8,32,512]{3,2,1,0:T(8,128)(2,1)S(1)}, bf16[2,8,32,512]{3,2,1,0:T(8,128)(2,1)S(1)}, u32[]{:S(2)}, u32[]{:S(2)}) collective-permute-start(bf16[2,8,32,512]{3,2,1,0:T(8,128)(2,1)S(1)} %pad_maximum_fusion.11), channel_id=1, source_target_pairs={{0,96},{32,64},{64,32},{96,0},{1,97},{33,65},{65,33},{97,1},{2,98}... | collective-permute-start | bytes 1572872 | tf_op jit(solution)/shard_map/ppermute | solution.py:22
  30.9 1.3 %collective-permute-done.23 = bf16[256,896]{1,0:T(8,128)(2,1)S(1)} collective-permute-done((bf16[256,896]{1,0:T(8,128)(2,1)S(1)}, bf16[256,896]{1,0:T(8,128)(2,1)S(1)}, u32[]{:S(2)}, u32[]{:S(2)}) %collective-permute-start.23) | collective-permute-done | bytes 458784 | tf_op jit(solution)/shard_map/ppermute | solution.py:22
  32.8 1.8 %collective-permute-start.15 = (bf16[2,256,896]{2,1,0:T(8,128)(2,1)S(1)}, bf16[2,256,896]{2,1,0:T(8,128)(2,1)S(1)}, u32[]{:S(2)}, u32[]{:S(2)}) collective-permute-start(bf16[2,256,896]{2,1,0:T(8,128)(2,1)S(1)} %pad_maximum_fusion.7), channel_id=1, source_target_pairs={{0,12},{4,8},{8,4},{12,0},{1,13},{5,9},{9,5},{13,1},{2,14},{6,10},... | collective-permute-start | bytes 2752520 | tf_op jit(solution)/shard_map/ppermute | solution.py:22
  34.6 3.8 %collective-permute-done.9 = bf16[8,32,1024]{2,1,0:T(8,128)(2,1)S(1)} collective-permute-done((bf16[8,32,1024]{2,1,0:T(8,128)(2,1)S(1)}, bf16[8,32,1024]{2,1,0:T(8,128)(2,1)S(1)}, u32[]{:S(2)}, u32[]{:S(2)}) %collective-permute-start.9) | collective-permute-done | bytes 524320 | tf_op jit(solution)/shard_map/ppermute | solution.py:22
  38.4 1.2 %collective-permute-start.17 = (bf16[352,1792]{1,0:T(8,128)(2,1)S(1)}, bf16[352,1792]{1,0:T(8,128)(2,1)S(1)}, u32[]{:S(2)}, u32[]{:S(2)}) collective-permute-start(bf16[352,1792]{1,0:T(8,128)(2,1)S(1)} %slice.145), channel_id=1, source_target_pairs={{0,2},{2,0},{1,3},{3,1},{4,6},{6,4},{5,7},{7,5},{8,10},{10,8},{9,1... | collective-permute-start | bytes 3784712 | tf_op jit(solution)/shard_map/ppermute | solution.py:22
  39.6 1.5 %collective-permute-done.6 = bf16[2,8,32,512]{3,2,1,0:T(8,128)(2,1)S(1)} collective-permute-done((bf16[2,8,32,512]{3,2,1,0:T(8,128)(2,1)S(1)}, bf16[2,8,32,512]{3,2,1,0:T(8,128)(2,1)S(1)}, u32[]{:S(2)}, u32[]{:S(2)}) %collective-permute-start.6) | collective-permute-done | bytes 524320 | tf_op jit(solution)/shard_map/ppermute | solution.py:22
  41.1 1.4 %collective-permute-done.7 = bf16[2,8,32,512]{3,2,1,0:T(8,128)(2,1)S(1)} collective-permute-done((bf16[2,8,32,512]{3,2,1,0:T(8,128)(2,1)S(1)}, bf16[2,8,32,512]{3,2,1,0:T(8,128)(2,1)S(1)}, u32[]{:S(2)}, u32[]{:S(2)}) %collective-permute-start.7) | collective-permute-done | bytes 524320 | tf_op jit(solution)/shard_map/ppermute | solution.py:22
  42.6 1.4 %collective-permute-start.11 = (bf16[8,32,512]{2,1,0:T(8,128)(2,1)S(1)}, bf16[8,32,512]{2,1,0:T(8,128)(2,1)S(1)}, u32[]{:S(2)}, u32[]{:S(2)}) collective-permute-start(bf16[8,32,512]{2,1,0:T(8,128)(2,1)S(1)} %get-tuple-element.99), channel_id=1, source_target_pairs={{0,96},{32,64},{64,32},{96,0},{1,97},{33,65},{65,33},{97,1},{2,98}... | collective-permute-start | bytes 786440 | tf_op jit(solution)/shard_map/ppermute | solution.py:22
  44.1 6.1 %collective-permute-done.11 = bf16[8,32,512]{2,1,0:T(8,128)(2,1)S(1)} collective-permute-done((bf16[8,32,512]{2,1,0:T(8,128)(2,1)S(1)}, bf16[8,32,512]{2,1,0:T(8,128)(2,1)S(1)}, u32[]{:S(2)}, u32[]{:S(2)}) %collective-permute-start.11) | collective-permute-done | bytes 262176 | tf_op jit(solution)/shard_map/ppermute | solution.py:22
  50.5 2.0 %collective-permute-start.12 = (bf16[2,8,32,512]{3,2,1,0:T(8,128)(2,1)S(1)}, bf16[2,8,32,512]{3,2,1,0:T(8,128)(2,1)S(1)}, u32[]{:S(2)}, u32[]{:S(2)}) collective-permute-start(bf16[2,8,32,512]{3,2,1,0:T(8,128)(2,1)S(1)} %pad_maximum_fusion.13), channel_id=1, source_target_pairs={{0,96},{32,64},{64,32},{96,0},{1,97},{33,65},{65,33},{97,1},{2,98}... | collective-permute-start | bytes 1572872 | tf_op jit(solution)/shard_map/ppermute | solution.py:22
  52.6 1.2 %collective-permute-done.15 = bf16[2,256,896]{2,1,0:T(8,128)(2,1)S(1)} collective-permute-done((bf16[2,256,896]{2,1,0:T(8,128)(2,1)S(1)}, bf16[2,256,896]{2,1,0:T(8,128)(2,1)S(1)}, u32[]{:S(2)}, u32[]{:S(2)}) %collective-permute-start.15) | collective-permute-done | bytes 917536 | tf_op jit(solution)/shard_map/ppermute | solution.py:22
  56.0 6.1 %collective-permute-done.13 = bf16[2,8,32,512]{3,2,1,0:T(8,128)(2,1)S(1)} collective-permute-done((bf16[2,8,32,512]{3,2,1,0:T(8,128)(2,1)S(1)}, bf16[2,8,32,512]{3,2,1,0:T(8,128)(2,1)S(1)}, u32[]{:S(2)}, u32[]{:S(2)}) %collective-permute-start.13) | collective-permute-done | bytes 524320 | tf_op jit(solution)/shard_map/ppermute | solution.py:22
  63.5 2.3 %convolution_convert_fusion.5 = bf16[512,896]{1,0:T(8,128)(2,1)S(1)} fusion(bf16[2048,512]{1,0:T(8,128)(2,1)S(1)} %bitcast.149, bf16[2048,896]{1,0:T(8,128)(2,1)S(1)} %bitcast.160), kind=kOutput, calls=%fused_computation.18 | convolution fusion | flops 1879506944 | bytes 6684672 | tf_op jit(solution)/shard_map/dot_general | solution.py:95
  66.9 1.3 %convolution_convert_fusion.3 = bf16[512,896]{1,0:T(8,128)(2,1)S(1)} fusion(bf16[512,1024]{1,0:T(8,128)(2,1)S(1)} %bitcast.165, bf16[1024,1792]{1,0:T(8,128)(2,1)S(1)} %constant_dynamic-update-slice_fusion), kind=kOutput, calls=%fused_computation.16 | convolution fusion | flops 939982848 | bytes 3801088 | tf_op jit(solution)/shard_map/dot_general | solution.py:99
  68.3 1.3 %convolution_convert_fusion.2 = bf16[512,896]{1,0:T(8,128)(2,1)S(1)} fusion(bf16[512,1024]{1,0:T(8,128)(2,1)S(1)} %bitcast.167, bf16[1024,1792]{1,0:T(8,128)(2,1)S(1)} %constant_dynamic-update-slice_fusion), kind=kOutput, calls=%fused_computation.15 | convolution fusion | flops 939982848 | bytes 3801088 | tf_op jit(solution)/shard_map/dot_general | solution.py:99
  69.8 1.7 %copy-done.3 = bf16[8,256,896]{2,1,0:T(8,128)(2,1)S(1)} copy-done((bf16[8,256,896]{2,1,0:T(8,128)(2,1)S(1)}, bf16[8,256,896]{2,1,0:T(8,128)(2,1)}, u32[]{:S(2)}) %copy-start.3) | copy-done | bytes 3670040
  71.7 1.0 collective-permute-start.21
  72.8 1.3 %convolution_convert_fusion.1 = bf16[512,896]{1,0:T(8,128)(2,1)S(1)} fusion(bf16[512,1024]{1,0:T(8,128)(2,1)S(1)} %bitcast.168, bf16[1024,1792]{1,0:T(8,128)(2,1)S(1)} %constant_dynamic-update-slice_fusion), kind=kOutput, calls=%fused_computation.14 | convolution fusion | flops 939982848 | bytes 3801088 | tf_op jit(solution)/shard_map/dot_general | solution.py:99
  74.1 1.3 %convolution_convert_fusion = bf16[512,896]{1,0:T(8,128)(2,1)S(1)} fusion(bf16[512,1024]{1,0:T(8,128)(2,1)S(1)} %bitcast.169, bf16[1024,1792]{1,0:T(8,128)(2,1)S(1)} %constant_dynamic-update-slice_fusion), kind=kOutput, calls=%fused_computation.13 | convolution fusion | flops 939982848 | bytes 3801088 | tf_op jit(solution)/shard_map/dot_general | solution.py:99
  76.4 1.3 %add_convert_fusion.3 = bf16[512,896]{1,0:T(8,128)(2,1)S(1)} fusion(bf16[512,896]{1,0:T(8,128)(2,1)S(1)} %get-tuple-element.66, bf16[512,1024]{1,0:T(8,128)(2,1)S(1)} %bitcast.173, bf16[1024,1792]{1,0:T(8,128)(2,1)S(1)} %constant_dynamic-update-slice_fusion), kind=kOutput, calls=%fused_computation.12 | convolution fusion | flops 940900352 | bytes 4718592 | tf_op jit(solution)/shard_map/dot_general | solution.py:99
  77.7 1.3 %add_convert_fusion.2 = bf16[512,896]{1,0:T(8,128)(2,1)S(1)} fusion(bf16[512,896]{1,0:T(8,128)(2,1)S(1)} %get-tuple-element.67, bf16[512,1024]{1,0:T(8,128)(2,1)S(1)} %bitcast.164, bf16[1024,1792]{1,0:T(8,128)(2,1)S(1)} %constant_dynamic-update-slice_fusion), kind=kOutput, calls=%fused_computation.11 | convolution fusion | flops 940900352 | bytes 4718592 | tf_op jit(solution)/shard_map/dot_general | solution.py:99
  79.7 2.2 %collective-permute-start.19 = (bf16[2,256,896]{2,1,0:T(8,128)(2,1)S(1)}, bf16[2,256,896]{2,1,0:T(8,128)(2,1)S(1)}, u32[]{:S(2)}, u32[]{:S(2)}) collective-permute-start(bf16[2,256,896]{2,1,0:T(8,128)(2,1)S(1)} %bitcast.186), channel_id=1, source_target_pairs={{0,12},{4,8},{8,4},{12,0},{1,13},{5,9},{9,5},{13,1},{2,14},{6,10},... | collective-permute-start | bytes 2752520 | tf_op jit(solution)/shard_map/ppermute | solution.py:22
  81.8 2.3 %convolution_convert_fusion.4 = bf16[512,896]{1,0:T(8,128)(2,1)S(1)} fusion(bf16[2048,512]{1,0:T(8,128)(2,1)S(1)} %bitcast.151, bf16[2048,896]{1,0:T(8,128)(2,1)S(1)} %bitcast.184), kind=kOutput, calls=%fused_computation.17 | convolution fusion | flops 1879506944 | bytes 6684672 | tf_op jit(solution)/shard_map/dot_general | solution.py:95
  84.2 1.4 %collective-permute-start.28 = (bf16[512,896]{1,0:T(8,128)(2,1)S(1)}, bf16[512,896]{1,0:T(8,128)(2,1)S(1)}, u32[]{:S(2)}, u32[]{:S(2)}) collective-permute-start(bf16[512,896]{1,0:T(8,128)(2,1)S(1)} %convolution_convert_fusion.4), channel_id=1, source_target_pairs={{0,2},{2,0},{1,3},{3,1},{4,6},{6,4},{5,7},{7,5},{8,10},{10,8},{9,1... | collective-permute-start | bytes 2752520 | tf_op jit(solution)/shard_map/ppermute | solution.py:22
  85.6 1.3 %convert_add_fusion.1 = f32[512,896]{1,0:T(8,128)S(1)} fusion(bf16[512,1024]{1,0:T(8,128)(2,1)S(1)} %bitcast.172, bf16[1024,1792]{1,0:T(8,128)(2,1)S(1)} %constant_dynamic-update-slice_fusion, bf16[2,512,896]{2,1,0:T(8,128)(2,1)S(1)} %collective-permute-done.22), kind=kOutput, calls=%fused_computation.8 | convolution fusion | flops 940441600 | bytes 5636096 | tf_op jit(solution)/shard_map/dot_general | solution.py:99
  87.0 1.3 %convert_add_fusion = f32[512,896]{1,0:T(8,128)S(1)} fusion(bf16[512,1024]{1,0:T(8,128)(2,1)S(1)} %bitcast.166, bf16[1024,1792]{1,0:T(8,128)(2,1)S(1)} %constant_dynamic-update-slice_fusion, bf16[2,512,896]{2,1,0:T(8,128)(2,1)S(1)} %collective-permute-done.22), kind=kOutput, calls=%fused_computation.7 | convolution fusion | flops 940441600 | bytes 5636096 | tf_op jit(solution)/shard_map/dot_general | solution.py:99
  88.3 6.8 %collective-permute-done.21 = bf16[512,896]{1,0:T(8,128)(2,1)S(1)} collective-permute-done((bf16[512,896]{1,0:T(8,128)(2,1)S(1)}, bf16[512,896]{1,0:T(8,128)(2,1)S(1)}, u32[]{:S(2)}, u32[]{:S(2)}) %collective-permute-start.21) | collective-permute-done | bytes 917536 | tf_op jit(solution)/shard_map/ppermute | solution.py:22
  95.1 6.7 %collective-permute-done.20 = bf16[2,256,896]{2,1,0:T(8,128)(2,1)S(1)} collective-permute-done((bf16[2,256,896]{2,1,0:T(8,128)(2,1)S(1)}, bf16[2,256,896]{2,1,0:T(8,128)(2,1)S(1)}, u32[]{:S(2)}, u32[]{:S(2)}) %collective-permute-start.20) | collective-permute-done | bytes 917536 | tf_op jit(solution)/shard_map/ppermute | solution.py:22
  101.8 1.5 %collective-permute-done.19 = bf16[2,256,896]{2,1,0:T(8,128)(2,1)S(1)} collective-permute-done((bf16[2,256,896]{2,1,0:T(8,128)(2,1)S(1)}, bf16[2,256,896]{2,1,0:T(8,128)(2,1)S(1)}, u32[]{:S(2)}, u32[]{:S(2)}) %collective-permute-start.19) | collective-permute-done | bytes 917536 | tf_op jit(solution)/shard_map/ppermute | solution.py:22
  104.0 2.1 %collective-permute-start.27 = (bf16[256,896]{1,0:T(8,128)(2,1)S(1)}, bf16[256,896]{1,0:T(8,128)(2,1)S(1)}, u32[]{:S(2)}, u32[]{:S(2)}) collective-permute-start(bf16[256,896]{1,0:T(8,128)(2,1)S(1)} %get-tuple-element.88), channel_id=1, source_target_pairs={{0,12},{4,8},{8,4},{12,0},{1,13},{5,9},{9,5},{13,1},{2,14},{6,10},... | collective-permute-start | bytes 1376264 | tf_op jit(solution)/shard_map/ppermute | solution.py:22
  106.2 2.3 %fusion.24 = f32[512,896]{1,0:T(8,128)S(1)} fusion(bf16[2048,512]{1,0:T(8,128)(2,1)S(1)} %bitcast.147, bf16[2048,896]{1,0:T(8,128)(2,1)S(1)} %bitcast.161), kind=kOutput, calls=%fused_computation.93 | convolution fusion | flops 1879048192 | bytes 7602176 | tf_op jit(solution)/shard_map/dot_general | solution.py:95
  108.5 2.3 %fusion.25 = f32[512,896]{1,0:T(8,128)S(1)} fusion(bf16[2048,512]{1,0:T(8,128)(2,1)S(1)} %bitcast.148, bf16[2048,896]{1,0:T(8,128)(2,1)S(1)} %bitcast.185), kind=kOutput, calls=%fused_computation.94 | convolution fusion | flops 1879048192 | bytes 7602176 | tf_op jit(solution)/shard_map/dot_general | solution.py:95
  111.0 1.4 %collective-permute-done.28 = bf16[512,896]{1,0:T(8,128)(2,1)S(1)} collective-permute-done((bf16[512,896]{1,0:T(8,128)(2,1)S(1)}, bf16[512,896]{1,0:T(8,128)(2,1)S(1)}, u32[]{:S(2)}, u32[]{:S(2)}) %collective-permute-start.28) | collective-permute-done | bytes 917536 | tf_op jit(solution)/shard_map/ppermute | solution.py:22
  112.7 1.4 %pad_maximum_fusion.6 = bf16[512,1792]{1,0:T(8,128)(2,1)} fusion(bf16[512,896]{1,0:T(8,128)(2,1)S(1)} %add_convert_fusion, bf16[512,896]{1,0:T(8,128)(2,1)S(1)} %add_convert_fusion.1), kind=kLoop, calls=%fused_computation.6 | loop fusion | flops 3670016 | bytes 3670016 | tf_op jit(solution)/shard_map/concatenate | solution.py:182
  114.0 1.4 %collective-permute-done.26.far_l = bf16[256,896]{1,0:T(8,128)(2,1)S(1)} collective-permute-done((bf16[256,896]{1,0:T(8,128)(2,1)S(1)}, bf16[256,896]{1,0:T(8,128)(2,1)S(1)}, u32[]{:S(2)}, u32[]{:S(2)}) %collective-permute-start.26) | collective-permute-done | bytes 458784 | tf_op jit(solution)/shard_map/ppermute | solution.py:22
  115.5 1.5 %collective-permute-done.27.far_r = bf16[256,896]{1,0:T(8,128)(2,1)S(1)} collective-permute-done((bf16[256,896]{1,0:T(8,128)(2,1)S(1)}, bf16[256,896]{1,0:T(8,128)(2,1)S(1)}, u32[]{:S(2)}, u32[]{:S(2)}) %collective-permute-start.27) | collective-permute-done | bytes 458784 | tf_op jit(solution)/shard_map/ppermute | solution.py:22
  117.0 1.2 %shard_map.52 = bf16[256,1792]{1,0:T(8,128)(2,1)} custom-call(f32[256,896]{1,0:T(8,128)S(1)} %get-tuple-element.47.slope_l, f32[256,896]{1,0:T(8,128)S(1)} %get-tuple-element.48.slope_r, f32[256,896]{1,0:T(8,128)S(1)} %get-tuple-element.91.own_l, f32[256,896]{1,0:T(8,128)S(1)} %get-tuple-element.89.own_r, ...), custom_call_target="tpu_custom_call" | custom-call | tf_op jit(solution)/shard_map/pallas_call | solution.py:91
  (88 shorter events, 14.7 us)
Async XLA Ops:
  0.6 1.0 copy-start.1
  1.7 1.6 %collective-permute-start = (bf16[4,32,1024]{2,1,0:T(8,128)(2,1)S(1)}, bf16[4,32,1024]{2,1,0:T(8,128)(2,1)S(1)}, u32[]{:S(2)}, u32[]{:S(2)}) collective-permute-start(bf16[4,32,1024]{2,1,0:T(8,128)(2,1)S(1)} %get-tuple-element.45), channel_id=1, source_target_pairs={{0,1},{1,0},{2,3},{3,2},{4,5},{5,4},{6,7},{7,6},{8,9},{9,8},{10,11... | collective-permute-start | bytes 786440 | tf_op jit(solution)/shard_map/ppermute | solution.py:22
  3.4 7.8 %collective-permute-start.1 = (bf16[2,32,1024]{2,1,0:T(8,128)(2,1)S(1)}, bf16[2,32,1024]{2,1,0:T(8,128)(2,1)S(1)}, u32[]{:S(2)}, u32[]{:S(2)}) collective-permute-start(bf16[2,32,1024]{2,1,0:T(8,128)(2,1)S(1)} %get-tuple-element.110), channel_id=1, source_target_pairs={{0,4},{4,0},{8,12},{12,8},{1,5},{5,1},{9,13},{13,9},{2,6},{6,2},{1... | collective-permute-start | bytes 393224 | tf_op jit(solution)/shard_map/ppermute | solution.py:22
  5.1 7.8 %collective-permute-start.2 = (bf16[2,32,1024]{2,1,0:T(8,128)(2,1)S(1)}, bf16[2,32,1024]{2,1,0:T(8,128)(2,1)S(1)}, u32[]{:S(2)}, u32[]{:S(2)}) collective-permute-start(bf16[2,32,1024]{2,1,0:T(8,128)(2,1)S(1)} %get-tuple-element.111), channel_id=1, source_target_pairs={{0,12},{4,8},{8,4},{12,0},{1,13},{5,9},{9,5},{13,1},{2,14},{6,10},... | collective-permute-start | bytes 393224 | tf_op jit(solution)/shard_map/ppermute | solution.py:22
  7.3 7.1 %collective-permute-start.3 = (bf16[2,32,1024]{2,1,0:T(8,128)(2,1)S(1)}, bf16[2,32,1024]{2,1,0:T(8,128)(2,1)S(1)}, u32[]{:S(2)}, u32[]{:S(2)}) collective-permute-start(bf16[2,32,1024]{2,1,0:T(8,128)(2,1)S(1)} %get-tuple-element.112), channel_id=1, source_target_pairs={{0,8},{4,12},{8,0},{12,4},{1,9},{5,13},{9,1},{13,5},{2,10},{6,14},... | collective-permute-start | bytes 393224 | tf_op jit(solution)/shard_map/ppermute | solution.py:22
  9.1 8.6 %copy-start.2 = (bf16[512,1792]{1,0:T(8,128)(2,1)S(1)}, bf16[512,1792]{1,0:T(8,128)(2,1)}, u32[]{:S(2)}) copy-start(bf16[512,1792]{1,0:T(8,128)(2,1)} %param.5) | copy-start | bytes 5505028
  9.1 14.7 %collective-permute-start.8 = (bf16[160,1792]{1,0:T(8,128)(2,1)S(1)}, bf16[160,1792]{1,0:T(8,128)(2,1)S(1)}, u32[]{:S(2)}, u32[]{:S(2)}) collective-permute-start(bf16[160,1792]{1,0:T(8,128)(2,1)S(1)} %slice.133), channel_id=1, source_target_pairs={{0,2},{2,0},{1,3},{3,1},{4,6},{6,4},{5,7},{7,5},{8,10},{10,8},{9,1... | collective-permute-start | bytes 1720328 | tf_op jit(solution)/shard_map/ppermute | solution.py:22
  14.6 12.9 %collective-permute-start.5 = (bf16[8,32,512]{2,1,0:T(8,128)(2,1)S(1)}, bf16[8,32,512]{2,1,0:T(8,128)(2,1)S(1)}, u32[]{:S(2)}, u32[]{:S(2)}) collective-permute-start(bf16[8,32,512]{2,1,0:T(8,128)(2,1)S(1)} %get-tuple-element.107), channel_id=1, source_target_pairs={{0,96},{32,64},{64,32},{96,0},{1,97},{33,65},{65,33},{97,1},{2,98}... | collective-permute-start | bytes 786440 | tf_op jit(solution)/shard_map/ppermute | solution.py:22
  17.5 10.1 %collective-permute-start.4 = (bf16[8,32,512]{2,1,0:T(8,128)(2,1)S(1)}, bf16[8,32,512]{2,1,0:T(8,128)(2,1)S(1)}, u32[]{:S(2)}, u32[]{:S(2)}) collective-permute-start(bf16[8,32,512]{2,1,0:T(8,128)(2,1)S(1)} %get-tuple-element.108), channel_id=1, source_target_pairs={{0,32},{32,0},{64,96},{96,64},{1,33},{33,1},{65,97},{97,65},{2,34}... | collective-permute-start | bytes 786440 | tf_op jit(solution)/shard_map/ppermute | solution.py:22
  17.8 1.2 %copy-start = (bf16[256,1792]{1,0:T(8,128)(2,1)S(1)}, bf16[256,1792]{1,0:T(8,128)(2,1)}, u32[]{:S(2)}) copy-start(bf16[256,1792]{1,0:T(8,128)(2,1)} %pre) | copy-start | bytes 2752516
  19.8 12.4 %collective-permute-start.23 = (bf16[256,896]{1,0:T(8,128)(2,1)S(1)}, bf16[256,896]{1,0:T(8,128)(2,1)S(1)}, u32[]{:S(2)}, u32[]{:S(2)}) collective-permute-start(bf16[256,896]{1,0:T(8,128)(2,1)S(1)} %get-tuple-element.71), channel_id=1, source_target_pairs={{0,12},{4,8},{8,4},{12,0},{1,13},{5,9},{9,5},{13,1},{2,14},{6,10},... | collective-permute-start | bytes 1376264 | tf_op jit(solution)/shard_map/ppermute | solution.py:22
  22.1 10.6 %collective-permute-start.14 = (bf16[256,896]{1,0:T(8,128)(2,1)S(1)}, bf16[256,896]{1,0:T(8,128)(2,1)S(1)}, u32[]{:S(2)}, u32[]{:S(2)}) collective-permute-start(bf16[256,896]{1,0:T(8,128)(2,1)S(1)} %get-tuple-element.58), channel_id=1, source_target_pairs={{0,4},{4,0},{8,12},{12,8},{1,5},{5,1},{9,13},{13,9},{2,6},{6,2},{1... | collective-permute-start | bytes 1376264 | tf_op jit(solution)/shard_map/ppermute | solution.py:22
  23.8 14.5 %collective-permute-start.9 = (bf16[8,32,1024]{2,1,0:T(8,128)(2,1)S(1)}, bf16[8,32,1024]{2,1,0:T(8,128)(2,1)S(1)}, u32[]{:S(2)}, u32[]{:S(2)}) collective-permute-start(bf16[8,32,1024]{2,1,0:T(8,128)(2,1)S(1)} %bitcast.153), channel_id=1, source_target_pairs={{0,16},{16,0},{1,17},{17,1},{2,18},{18,2},{3,19},{19,3},{4,20},{20... | collective-permute-start | bytes 1572872 | tf_op jit(solution)/shard_map/ppermute | solution.py:22
  27.6 13.5 %collective-permute-start.6 = (bf16[2,8,32,512]{3,2,1,0:T(8,128)(2,1)S(1)}, bf16[2,8,32,512]{3,2,1,0:T(8,128)(2,1)S(1)}, u32[]{:S(2)}, u32[]{:S(2)}) collective-permute-start(bf16[2,8,32,512]{3,2,1,0:T(8,128)(2,1)S(1)} %pad_maximum_fusion.11), channel_id=1, source_target_pairs={{0,96},{32,64},{64,32},{96,0},{1,97},{33,65},{65,33},{97,1},{2,98}... | collective-permute-start | bytes 1572872 | tf_op jit(solution)/shard_map/ppermute | solution.py:22
  30.5 12.0 %collective-permute-start.7 = (bf16[2,8,32,512]{3,2,1,0:T(8,128)(2,1)S(1)}, bf16[2,8,32,512]{3,2,1,0:T(8,128)(2,1)S(1)}, u32[]{:S(2)}, u32[]{:S(2)}) collective-permute-start(bf16[2,8,32,512]{3,2,1,0:T(8,128)(2,1)S(1)} %pad_maximum_fusion.12), channel_id=1, source_target_pairs={{0,32},{32,0},{64,96},{96,64},{1,33},{33,1},{65,97},{97,65},{2,34}... | collective-permute-start | bytes 1572872 | tf_op jit(solution)/shard_map/ppermute | solution.py:22
  32.3 21.8 %collective-permute-start.24 = (bf16[2,256,896]{2,1,0:T(8,128)(2,1)S(1)}, bf16[2,256,896]{2,1,0:T(8,128)(2,1)S(1)}, u32[]{:S(2)}, u32[]{:S(2)}) collective-permute-start(bf16[2,256,896]{2,1,0:T(8,128)(2,1)S(1)} %pad_maximum_fusion.8), channel_id=1, source_target_pairs={{0,4},{4,0},{8,12},{12,8},{1,5},{5,1},{9,13},{13,9},{2,6},{6,2},{1... | collective-permute-start | bytes 2752520 | tf_op jit(solution)/shard_map/ppermute | solution.py:22
  32.8 21.0 %collective-permute-start.15 = (bf16[2,256,896]{2,1,0:T(8,128)(2,1)S(1)}, bf16[2,256,896]{2,1,0:T(8,128)(2,1)S(1)}, u32[]{:S(2)}, u32[]{:S(2)}) collective-permute-start(bf16[2,256,896]{2,1,0:T(8,128)(2,1)S(1)} %pad_maximum_fusion.7), channel_id=1, source_target_pairs={{0,12},{4,8},{8,4},{12,0},{1,13},{5,9},{9,5},{13,1},{2,14},{6,10},... | collective-permute-start | bytes 2752520 | tf_op jit(solution)/shard_map/ppermute | solution.py:22
  38.4 27.7 %collective-permute-start.17 = (bf16[352,1792]{1,0:T(8,128)(2,1)S(1)}, bf16[352,1792]{1,0:T(8,128)(2,1)S(1)}, u32[]{:S(2)}, u32[]{:S(2)}) collective-permute-start(bf16[352,1792]{1,0:T(8,128)(2,1)S(1)} %slice.145), channel_id=1, source_target_pairs={{0,2},{2,0},{1,3},{3,1},{4,6},{6,4},{5,7},{7,5},{8,10},{10,8},{9,1... | collective-permute-start | bytes 3784712 | tf_op jit(solution)/shard_map/ppermute | solution.py:22
  42.6 7.7 %collective-permute-start.11 = (bf16[8,32,512]{2,1,0:T(8,128)(2,1)S(1)}, bf16[8,32,512]{2,1,0:T(8,128)(2,1)S(1)}, u32[]{:S(2)}, u32[]{:S(2)}) collective-permute-start(bf16[8,32,512]{2,1,0:T(8,128)(2,1)S(1)} %get-tuple-element.99), channel_id=1, source_target_pairs={{0,96},{32,64},{64,32},{96,0},{1,97},{33,65},{65,33},{97,1},{2,98}... | collective-permute-start | bytes 786440 | tf_op jit(solution)/shard_map/ppermute | solution.py:22
  44.1 6.4 %collective-permute-start.10 = (bf16[8,32,512]{2,1,0:T(8,128)(2,1)S(1)}, bf16[8,32,512]{2,1,0:T(8,128)(2,1)S(1)}, u32[]{:S(2)}, u32[]{:S(2)}) collective-permute-start(bf16[8,32,512]{2,1,0:T(8,128)(2,1)S(1)} %get-tuple-element.100), channel_id=1, source_target_pairs={{0,32},{32,0},{64,96},{96,64},{1,33},{33,1},{65,97},{97,65},{2,34}... | collective-permute-start | bytes 786440 | tf_op jit(solution)/shard_map/ppermute | solution.py:22
  50.5 11.9 %collective-permute-start.12 = (bf16[2,8,32,512]{3,2,1,0:T(8,128)(2,1)S(1)}, bf16[2,8,32,512]{3,2,1,0:T(8,128)(2,1)S(1)}, u32[]{:S(2)}, u32[]{:S(2)}) collective-permute-start(bf16[2,8,32,512]{3,2,1,0:T(8,128)(2,1)S(1)} %pad_maximum_fusion.13), channel_id=1, source_target_pairs={{0,96},{32,64},{64,32},{96,0},{1,97},{33,65},{65,33},{97,1},{2,98}... | collective-permute-start | bytes 1572872 | tf_op jit(solution)/shard_map/ppermute | solution.py:22
  52.5 9.7 %collective-permute-start.13 = (bf16[2,8,32,512]{3,2,1,0:T(8,128)(2,1)S(1)}, bf16[2,8,32,512]{3,2,1,0:T(8,128)(2,1)S(1)}, u32[]{:S(2)}, u32[]{:S(2)}) collective-permute-start(bf16[2,8,32,512]{3,2,1,0:T(8,128)(2,1)S(1)} %pad_maximum_fusion.14), channel_id=1, source_target_pairs={{0,32},{32,0},{64,96},{96,64},{1,33},{33,1},{65,97},{97,65},{2,34}... | collective-permute-start | bytes 1572872 | tf_op jit(solution)/shard_map/ppermute | solution.py:22
  54.0 9.0 %collective-permute-start.16 = (bf16[4,256,896]{2,1,0:T(8,128)(2,1)S(1)}, bf16[4,256,896]{2,1,0:T(8,128)(2,1)S(1)}, u32[]{:S(2)}, u32[]{:S(2)}) collective-permute-start(bf16[4,256,896]{2,1,0:T(8,128)(2,1)S(1)} %pad_maximum_fusion.2), channel_id=1, source_target_pairs={{0,1},{1,0},{2,3},{3,2},{4,5},{5,4},{6,7},{7,6},{8,9},{9,8},{10,11... | collective-permute-start | bytes 5505032 | tf_op jit(solution)/shard_map/ppermute | solution.py:22
  55.3 20.7 %collective-permute-start.25 = (bf16[4,256,896]{2,1,0:T(8,128)(2,1)S(1)}, bf16[4,256,896]{2,1,0:T(8,128)(2,1)S(1)}, u32[]{:S(2)}, u32[]{:S(2)}) collective-permute-start(bf16[4,256,896]{2,1,0:T(8,128)(2,1)S(1)} %pad_maximum_fusion.5), channel_id=1, source_target_pairs={{0,1},{1,0},{2,3},{3,2},{4,5},{5,4},{6,7},{7,6},{8,9},{9,8},{10,11... | collective-permute-start | bytes 5505032 | tf_op jit(solution)/shard_map/ppermute | solution.py:22
  69.5 2.0 %copy-start.3 = (bf16[8,256,896]{2,1,0:T(8,128)(2,1)S(1)}, bf16[8,256,896]{2,1,0:T(8,128)(2,1)}, u32[]{:S(2)}) copy-start(bf16[8,256,896]{2,1,0:T(8,128)(2,1)} %get-tuple-element.95) | copy-start | bytes 11010052
  69.7 6.5 %collective-permute-start.18 = (bf16[2,512,896]{2,1,0:T(8,128)(2,1)S(1)}, bf16[2,512,896]{2,1,0:T(8,128)(2,1)S(1)}, u32[]{:S(2)}, u32[]{:S(2)}) collective-permute-start(bf16[2,512,896]{2,1,0:T(8,128)(2,1)S(1)} %pad_maximum_fusion.3), channel_id=1, source_target_pairs={{0,1},{1,0},{2,3},{3,2},{4,5},{5,4},{6,7},{7,6},{8,9},{9,8},{10,11... | collective-permute-start | bytes 5505032 | tf_op jit(solution)/shard_map/ppermute | solution.py:22
  71.7 23.4 %collective-permute-start.21 = (bf16[512,896]{1,0:T(8,128)(2,1)S(1)}, bf16[512,896]{1,0:T(8,128)(2,1)S(1)}, u32[]{:S(2)}, u32[]{:S(2)}) collective-permute-start(bf16[512,896]{1,0:T(8,128)(2,1)S(1)} %convolution_convert_fusion.5), channel_id=1, source_target_pairs={{0,2},{2,0},{1,3},{3,1},{4,6},{6,4},{5,7},{7,5},{8,10},{10,8},{9,1... | collective-permute-start | bytes 2752520 | tf_op jit(solution)/shard_map/ppermute | solution.py:22
  75.6 10.0 %collective-permute-start.22 = (bf16[2,512,896]{2,1,0:T(8,128)(2,1)S(1)}, bf16[2,512,896]{2,1,0:T(8,128)(2,1)S(1)}, u32[]{:S(2)}, u32[]{:S(2)}) collective-permute-start(bf16[2,512,896]{2,1,0:T(8,128)(2,1)S(1)} %pad_maximum_fusion.4), channel_id=1, source_target_pairs={{0,1},{1,0},{2,3},{3,2},{4,5},{5,4},{6,7},{7,6},{8,9},{9,8},{10,11... | collective-permute-start | bytes 5505032 | tf_op jit(solution)/shard_map/ppermute | solution.py:22
  79.0 22.8 %collective-permute-start.20 = (bf16[2,256,896]{2,1,0:T(8,128)(2,1)S(1)}, bf16[2,256,896]{2,1,0:T(8,128)(2,1)S(1)}, u32[]{:S(2)}, u32[]{:S(2)}) collective-permute-start(bf16[2,256,896]{2,1,0:T(8,128)(2,1)S(1)} %bitcast.187), channel_id=1, source_target_pairs={{0,4},{4,0},{8,12},{12,8},{1,5},{5,1},{9,13},{13,9},{2,6},{6,2},{1... | collective-permute-start | bytes 2752520 | tf_op jit(solution)/shard_map/ppermute | solution.py:22
  79.7 23.7 %collective-permute-start.19 = (bf16[2,256,896]{2,1,0:T(8,128)(2,1)S(1)}, bf16[2,256,896]{2,1,0:T(8,128)(2,1)S(1)}, u32[]{:S(2)}, u32[]{:S(2)}) collective-permute-start(bf16[2,256,896]{2,1,0:T(8,128)(2,1)S(1)} %bitcast.186), channel_id=1, source_target_pairs={{0,12},{4,8},{8,4},{12,0},{1,13},{5,9},{9,5},{13,1},{2,14},{6,10},... | collective-permute-start | bytes 2752520 | tf_op jit(solution)/shard_map/ppermute | solution.py:22
  84.2 28.2 %collective-permute-start.28 = (bf16[512,896]{1,0:T(8,128)(2,1)S(1)}, bf16[512,896]{1,0:T(8,128)(2,1)S(1)}, u32[]{:S(2)}, u32[]{:S(2)}) collective-permute-start(bf16[512,896]{1,0:T(8,128)(2,1)S(1)} %convolution_convert_fusion.4), channel_id=1, source_target_pairs={{0,2},{2,0},{1,3},{3,1},{4,6},{6,4},{5,7},{7,5},{8,10},{10,8},{9,1... | collective-permute-start | bytes 2752520 | tf_op jit(solution)/shard_map/ppermute | solution.py:22
  103.6 11.9 %collective-permute-start.26 = (bf16[256,896]{1,0:T(8,128)(2,1)S(1)}, bf16[256,896]{1,0:T(8,128)(2,1)S(1)}, u32[]{:S(2)}, u32[]{:S(2)}) collective-permute-start(bf16[256,896]{1,0:T(8,128)(2,1)S(1)} %get-tuple-element.90), channel_id=1, source_target_pairs={{0,4},{4,0},{8,12},{12,8},{1,5},{5,1},{9,13},{13,9},{2,6},{6,2},{1... | collective-permute-start | bytes 1376264 | tf_op jit(solution)/shard_map/ppermute | solution.py:22
  104.0 12.9 %collective-permute-start.27 = (bf16[256,896]{1,0:T(8,128)(2,1)S(1)}, bf16[256,896]{1,0:T(8,128)(2,1)S(1)}, u32[]{:S(2)}, u32[]{:S(2)}) collective-permute-start(bf16[256,896]{1,0:T(8,128)(2,1)S(1)} %get-tuple-element.88), channel_id=1, source_target_pairs={{0,12},{4,8},{8,4},{12,0},{1,13},{5,9},{9,5},{13,1},{2,14},{6,10},... | collective-permute-start | bytes 1376264 | tf_op jit(solution)/shard_map/ppermute | solution.py:22

commit v7 on v6

--- a/solution.py
+++ b/solution.py
@@ -12,7 +12,7 @@
 SIZES = {"x": 4, "zh": 2, "y": 4, "zl": 2, "core": 2}
 BF16, F32 = jnp.bfloat16, jnp.float32
 VMEM = pl.BlockSpec(memory_space=pltpu.VMEM)
-SMALL = pltpu.CompilerParams(vmem_limit_bytes=16 * 1024 * 1024)
+SMALL = pltpu.CompilerParams(vmem_limit_bytes=24 * 1024 * 1024)
 
 STEP = {"b": lambda i: i ^ 1, "a": lambda i: 3 - i, "ab": lambda i: i ^ 2}
 

time: 119 us -> 118 us (level)
  no operation moved by 1% of the time
where the time goes in v7:
time: 118 us
  waiting for transfers between devices  47.4 us (40%)
  starting transfers between devices  34.2 us (29%)
  matrix products  19.5 us (17%)
  local copies, waits for them, and re-layouts  9.18 us (8%)
  other arithmetic  4.61 us (4%)
  Pallas kernels  1.98 us (2%)
  between operations  1.18 us (1%)
    ppermute x29, waiting for transfers between devices, swap(): return lax.ppermute(value, axis, [(i, move(i)) for i in range(SIZES[axis])])  47.4 us
    ppermute x29, starting transfers between devices, swap(): return lax.ppermute(value, axis, [(i, move(i)) for i in range(SIZES[axis])])  34.2 us
    dot_general x8, matrix products, inner(): return jnp.dot(g, w, preferred_element_type=F32)  10.1 us
    dot_general x4, matrix products, outer(): lax.dot_general(g, h, (((0,), (0,)), ((), ())), preferred_element_type=F32)  9.37 us
    unnamed x24, local copies, waits for them, and re-layouts  5.21 us
  transfers between devices with their start and end apart: 29, of which 20 were waited for; matrix products, arithmetic and copies ran while one was open for 25% of the time, Pallas kernels for 1%

profile of v7, /device:TPU:0, one launch (start us, length us, event | category | flops | bytes accessed | tf_op | source)
XLA Modules:
  0.0 118.0 jit_solution(9082759397559776907)
XLA Ops:
  1.8 1.5 %collective-permute-done = bf16[4,32,1024]{2,1,0:T(8,128)(2,1)S(1)} collective-permute-done((bf16[4,32,1024]{2,1,0:T(8,128)(2,1)S(1)}, bf16[4,32,1024]{2,1,0:T(8,128)(2,1)S(1)}, u32[]{:S(2)}, u32[]{:S(2)}) %collective-permute-start) | collective-permute-done | bytes 262176 | tf_op jit(solution)/shard_map/ppermute | solution.py:22
  3.4 1.7 %collective-permute-start.1 = (bf16[2,32,1024]{2,1,0:T(8,128)(2,1)S(1)}, bf16[2,32,1024]{2,1,0:T(8,128)(2,1)S(1)}, u32[]{:S(2)}, u32[]{:S(2)}) collective-permute-start(bf16[2,32,1024]{2,1,0:T(8,128)(2,1)S(1)} %get-tuple-element.110), channel_id=1, source_target_pairs={{0,4},{4,0},{8,12},{12,8},{1,5},{5,1},{9,13},{13,9},{2,6},{6,2},{1... | collective-permute-start | bytes 393224 | tf_op jit(solution)/shard_map/ppermute | solution.py:22
  5.1 2.2 %collective-permute-start.2 = (bf16[2,32,1024]{2,1,0:T(8,128)(2,1)S(1)}, bf16[2,32,1024]{2,1,0:T(8,128)(2,1)S(1)}, u32[]{:S(2)}, u32[]{:S(2)}) collective-permute-start(bf16[2,32,1024]{2,1,0:T(8,128)(2,1)S(1)} %get-tuple-element.111), channel_id=1, source_target_pairs={{0,12},{4,8},{8,4},{12,0},{1,13},{5,9},{9,5},{13,1},{2,14},{6,10},... | collective-permute-start | bytes 393224 | tf_op jit(solution)/shard_map/ppermute | solution.py:22
  8.0 1.1 slice.133
  9.1 2.0 %collective-permute-start.8 = (bf16[160,1792]{1,0:T(8,128)(2,1)S(1)}, bf16[160,1792]{1,0:T(8,128)(2,1)S(1)}, u32[]{:S(2)}, u32[]{:S(2)}) collective-permute-start(bf16[160,1792]{1,0:T(8,128)(2,1)S(1)} %slice.133), channel_id=1, source_target_pairs={{0,2},{2,0},{1,3},{3,1},{4,6},{6,4},{5,7},{7,5},{8,10},{10,8},{9,1... | collective-permute-start | bytes 1720328 | tf_op jit(solution)/shard_map/ppermute | solution.py:22
  11.1 1.8 %collective-permute-done.2 = bf16[2,32,1024]{2,1,0:T(8,128)(2,1)S(1)} collective-permute-done((bf16[2,32,1024]{2,1,0:T(8,128)(2,1)S(1)}, bf16[2,32,1024]{2,1,0:T(8,128)(2,1)S(1)}, u32[]{:S(2)}, u32[]{:S(2)}) %collective-permute-start.2) | collective-permute-done | bytes 131104 | tf_op jit(solution)/shard_map/ppermute | solution.py:22
  12.9 1.5 %collective-permute-done.3 = bf16[2,32,1024]{2,1,0:T(8,128)(2,1)S(1)} collective-permute-done((bf16[2,32,1024]{2,1,0:T(8,128)(2,1)S(1)}, bf16[2,32,1024]{2,1,0:T(8,128)(2,1)S(1)}, u32[]{:S(2)}, u32[]{:S(2)}) %collective-permute-start.3) | collective-permute-done | bytes 131104 | tf_op jit(solution)/shard_map/ppermute | solution.py:22
  14.6 2.8 %collective-permute-start.5 = (bf16[8,32,512]{2,1,0:T(8,128)(2,1)S(1)}, bf16[8,32,512]{2,1,0:T(8,128)(2,1)S(1)}, u32[]{:S(2)}, u32[]{:S(2)}) collective-permute-start(bf16[8,32,512]{2,1,0:T(8,128)(2,1)S(1)} %get-tuple-element.107), channel_id=1, source_target_pairs={{0,96},{32,64},{64,32},{96,0},{1,97},{33,65},{65,33},{97,1},{2,98}... | collective-permute-start | bytes 786440 | tf_op jit(solution)/shard_map/ppermute | solution.py:22
  17.9 1.1 copy-done
  19.8 2.3 %collective-permute-start.23 = (bf16[256,896]{1,0:T(8,128)(2,1)S(1)}, bf16[256,896]{1,0:T(8,128)(2,1)S(1)}, u32[]{:S(2)}, u32[]{:S(2)}) collective-permute-start(bf16[256,896]{1,0:T(8,128)(2,1)S(1)} %get-tuple-element.71), channel_id=1, source_target_pairs={{0,12},{4,8},{8,4},{12,0},{1,13},{5,9},{9,5},{13,1},{2,14},{6,10},... | collective-permute-start | bytes 1376264 | tf_op jit(solution)/shard_map/ppermute | solution.py:22
  23.8 3.7 %collective-permute-start.9 = (bf16[8,32,1024]{2,1,0:T(8,128)(2,1)S(1)}, bf16[8,32,1024]{2,1,0:T(8,128)(2,1)S(1)}, u32[]{:S(2)}, u32[]{:S(2)}) collective-permute-start(bf16[8,32,1024]{2,1,0:T(8,128)(2,1)S(1)} %bitcast.153), channel_id=1, source_target_pairs={{0,16},{16,0},{1,17},{17,1},{2,18},{18,2},{3,19},{19,3},{4,20},{20... | collective-permute-start | bytes 1572872 | tf_op jit(solution)/shard_map/ppermute | solution.py:22
  27.6 2.8 %collective-permute-start.6 = (bf16[2,8,32,512]{3,2,1,0:T(8,128)(2,1)S(1)}, bf16[2,8,32,512]{3,2,1,0:T(8,128)(2,1)S(1)}, u32[]{:S(2)}, u32[]{:S(2)}) collective-permute-start(bf16[2,8,32,512]{3,2,1,0:T(8,128)(2,1)S(1)} %pad_maximum_fusion.11), channel_id=1, source_target_pairs={{0,96},{32,64},{64,32},{96,0},{1,97},{33,65},{65,33},{97,1},{2,98}... | collective-permute-start | bytes 1572872 | tf_op jit(solution)/shard_map/ppermute | solution.py:22
  30.9 1.3 %collective-permute-done.23 = bf16[256,896]{1,0:T(8,128)(2,1)S(1)} collective-permute-done((bf16[256,896]{1,0:T(8,128)(2,1)S(1)}, bf16[256,896]{1,0:T(8,128)(2,1)S(1)}, u32[]{:S(2)}, u32[]{:S(2)}) %collective-permute-start.23) | collective-permute-done | bytes 458784 | tf_op jit(solution)/shard_map/ppermute | solution.py:22
  32.8 1.8 %collective-permute-start.15 = (bf16[2,256,896]{2,1,0:T(8,128)(2,1)S(1)}, bf16[2,256,896]{2,1,0:T(8,128)(2,1)S(1)}, u32[]{:S(2)}, u32[]{:S(2)}) collective-permute-start(bf16[2,256,896]{2,1,0:T(8,128)(2,1)S(1)} %pad_maximum_fusion.7), channel_id=1, source_target_pairs={{0,12},{4,8},{8,4},{12,0},{1,13},{5,9},{9,5},{13,1},{2,14},{6,10},... | collective-permute-start | bytes 2752520 | tf_op jit(solution)/shard_map/ppermute | solution.py:22
  34.6 3.8 %collective-permute-done.9 = bf16[8,32,1024]{2,1,0:T(8,128)(2,1)S(1)} collective-permute-done((bf16[8,32,1024]{2,1,0:T(8,128)(2,1)S(1)}, bf16[8,32,1024]{2,1,0:T(8,128)(2,1)S(1)}, u32[]{:S(2)}, u32[]{:S(2)}) %collective-permute-start.9) | collective-permute-done | bytes 524320 | tf_op jit(solution)/shard_map/ppermute | solution.py:22
  38.4 1.2 %collective-permute-start.17 = (bf16[352,1792]{1,0:T(8,128)(2,1)S(1)}, bf16[352,1792]{1,0:T(8,128)(2,1)S(1)}, u32[]{:S(2)}, u32[]{:S(2)}) collective-permute-start(bf16[352,1792]{1,0:T(8,128)(2,1)S(1)} %slice.145), channel_id=1, source_target_pairs={{0,2},{2,0},{1,3},{3,1},{4,6},{6,4},{5,7},{7,5},{8,10},{10,8},{9,1... | collective-permute-start | bytes 3784712 | tf_op jit(solution)/shard_map/ppermute | solution.py:22
  39.6 1.5 %collective-permute-done.6 = bf16[2,8,32,512]{3,2,1,0:T(8,128)(2,1)S(1)} collective-permute-done((bf16[2,8,32,512]{3,2,1,0:T(8,128)(2,1)S(1)}, bf16[2,8,32,512]{3,2,1,0:T(8,128)(2,1)S(1)}, u32[]{:S(2)}, u32[]{:S(2)}) %collective-permute-start.6) | collective-permute-done | bytes 524320 | tf_op jit(solution)/shard_map/ppermute | solution.py:22
  41.1 1.4 %collective-permute-done.7 = bf16[2,8,32,512]{3,2,1,0:T(8,128)(2,1)S(1)} collective-permute-done((bf16[2,8,32,512]{3,2,1,0:T(8,128)(2,1)S(1)}, bf16[2,8,32,512]{3,2,1,0:T(8,128)(2,1)S(1)}, u32[]{:S(2)}, u32[]{:S(2)}) %collective-permute-start.7) | collective-permute-done | bytes 524320 | tf_op jit(solution)/shard_map/ppermute | solution.py:22
  42.6 1.4 %collective-permute-start.11 = (bf16[8,32,512]{2,1,0:T(8,128)(2,1)S(1)}, bf16[8,32,512]{2,1,0:T(8,128)(2,1)S(1)}, u32[]{:S(2)}, u32[]{:S(2)}) collective-permute-start(bf16[8,32,512]{2,1,0:T(8,128)(2,1)S(1)} %get-tuple-element.99), channel_id=1, source_target_pairs={{0,96},{32,64},{64,32},{96,0},{1,97},{33,65},{65,33},{97,1},{2,98}... | collective-permute-start | bytes 786440 | tf_op jit(solution)/shard_map/ppermute | solution.py:22
  44.2 6.1 %collective-permute-done.11 = bf16[8,32,512]{2,1,0:T(8,128)(2,1)S(1)} collective-permute-done((bf16[8,32,512]{2,1,0:T(8,128)(2,1)S(1)}, bf16[8,32,512]{2,1,0:T(8,128)(2,1)S(1)}, u32[]{:S(2)}, u32[]{:S(2)}) %collective-permute-start.11) | collective-permute-done | bytes 262176 | tf_op jit(solution)/shard_map/ppermute | solution.py:22
  50.5 2.0 %collective-permute-start.12 = (bf16[2,8,32,512]{3,2,1,0:T(8,128)(2,1)S(1)}, bf16[2,8,32,512]{3,2,1,0:T(8,128)(2,1)S(1)}, u32[]{:S(2)}, u32[]{:S(2)}) collective-permute-start(bf16[2,8,32,512]{3,2,1,0:T(8,128)(2,1)S(1)} %pad_maximum_fusion.13), channel_id=1, source_target_pairs={{0,96},{32,64},{64,32},{96,0},{1,97},{33,65},{65,33},{97,1},{2,98}... | collective-permute-start | bytes 1572872 | tf_op jit(solution)/shard_map/ppermute | solution.py:22
  52.6 1.2 %collective-permute-done.15 = bf16[2,256,896]{2,1,0:T(8,128)(2,1)S(1)} collective-permute-done((bf16[2,256,896]{2,1,0:T(8,128)(2,1)S(1)}, bf16[2,256,896]{2,1,0:T(8,128)(2,1)S(1)}, u32[]{:S(2)}, u32[]{:S(2)}) %collective-permute-start.15) | collective-permute-done | bytes 917536 | tf_op jit(solution)/shard_map/ppermute | solution.py:22
  56.0 6.1 %collective-permute-done.13 = bf16[2,8,32,512]{3,2,1,0:T(8,128)(2,1)S(1)} collective-permute-done((bf16[2,8,32,512]{3,2,1,0:T(8,128)(2,1)S(1)}, bf16[2,8,32,512]{3,2,1,0:T(8,128)(2,1)S(1)}, u32[]{:S(2)}, u32[]{:S(2)}) %collective-permute-start.13) | collective-permute-done | bytes 524320 | tf_op jit(solution)/shard_map/ppermute | solution.py:22
  63.5 2.3 %convolution_convert_fusion.5 = bf16[512,896]{1,0:T(8,128)(2,1)S(1)} fusion(bf16[2048,512]{1,0:T(8,128)(2,1)S(1)} %bitcast.149, bf16[2048,896]{1,0:T(8,128)(2,1)S(1)} %bitcast.160), kind=kOutput, calls=%fused_computation.18 | convolution fusion | flops 1879506944 | bytes 6684672 | tf_op jit(solution)/shard_map/dot_general | solution.py:95
  66.9 1.3 %convolution_convert_fusion.3 = bf16[512,896]{1,0:T(8,128)(2,1)S(1)} fusion(bf16[512,1024]{1,0:T(8,128)(2,1)S(1)} %bitcast.165, bf16[1024,1792]{1,0:T(8,128)(2,1)S(1)} %constant_dynamic-update-slice_fusion), kind=kOutput, calls=%fused_computation.16 | convolution fusion | flops 939982848 | bytes 3801088 | tf_op jit(solution)/shard_map/dot_general | solution.py:99
  68.3 1.3 %convolution_convert_fusion.2 = bf16[512,896]{1,0:T(8,128)(2,1)S(1)} fusion(bf16[512,1024]{1,0:T(8,128)(2,1)S(1)} %bitcast.167, bf16[1024,1792]{1,0:T(8,128)(2,1)S(1)} %constant_dynamic-update-slice_fusion), kind=kOutput, calls=%fused_computation.15 | convolution fusion | flops 939982848 | bytes 3801088 | tf_op jit(solution)/shard_map/dot_general | solution.py:99
  69.8 1.7 %copy-done.3 = bf16[8,256,896]{2,1,0:T(8,128)(2,1)S(1)} copy-done((bf16[8,256,896]{2,1,0:T(8,128)(2,1)S(1)}, bf16[8,256,896]{2,1,0:T(8,128)(2,1)}, u32[]{:S(2)}) %copy-start.3) | copy-done | bytes 3670040
  71.7 1.0 collective-permute-start.21
  72.8 1.3 %convolution_convert_fusion.1 = bf16[512,896]{1,0:T(8,128)(2,1)S(1)} fusion(bf16[512,1024]{1,0:T(8,128)(2,1)S(1)} %bitcast.168, bf16[1024,1792]{1,0:T(8,128)(2,1)S(1)} %constant_dynamic-update-slice_fusion), kind=kOutput, calls=%fused_computation.14 | convolution fusion | flops 939982848 | bytes 3801088 | tf_op jit(solution)/shard_map/dot_general | solution.py:99
  74.1 1.3 %convolution_convert_fusion = bf16[512,896]{1,0:T(8,128)(2,1)S(1)} fusion(bf16[512,1024]{1,0:T(8,128)(2,1)S(1)} %bitcast.169, bf16[1024,1792]{1,0:T(8,128)(2,1)S(1)} %constant_dynamic-update-slice_fusion), kind=kOutput, calls=%fused_computation.13 | convolution fusion | flops 939982848 | bytes 3801088 | tf_op jit(solution)/shard_map/dot_general | solution.py:99
  76.4 1.3 %add_convert_fusion.3 = bf16[512,896]{1,0:T(8,128)(2,1)S(1)} fusion(bf16[512,896]{1,0:T(8,128)(2,1)S(1)} %get-tuple-element.66, bf16[512,1024]{1,0:T(8,128)(2,1)S(1)} %bitcast.173, bf16[1024,1792]{1,0:T(8,128)(2,1)S(1)} %constant_dynamic-update-slice_fusion), kind=kOutput, calls=%fused_computation.12 | convolution fusion | flops 940900352 | bytes 4718592 | tf_op jit(solution)/shard_map/dot_general | solution.py:99
  77.7 1.3 %add_convert_fusion.2 = bf16[512,896]{1,0:T(8,128)(2,1)S(1)} fusion(bf16[512,896]{1,0:T(8,128)(2,1)S(1)} %get-tuple-element.67, bf16[512,1024]{1,0:T(8,128)(2,1)S(1)} %bitcast.164, bf16[1024,1792]{1,0:T(8,128)(2,1)S(1)} %constant_dynamic-update-slice_fusion), kind=kOutput, calls=%fused_computation.11 | convolution fusion | flops 940900352 | bytes 4718592 | tf_op jit(solution)/shard_map/dot_general | solution.py:99
  79.7 2.2 %collective-permute-start.19 = (bf16[2,256,896]{2,1,0:T(8,128)(2,1)S(1)}, bf16[2,256,896]{2,1,0:T(8,128)(2,1)S(1)}, u32[]{:S(2)}, u32[]{:S(2)}) collective-permute-start(bf16[2,256,896]{2,1,0:T(8,128)(2,1)S(1)} %bitcast.186), channel_id=1, source_target_pairs={{0,12},{4,8},{8,4},{12,0},{1,13},{5,9},{9,5},{13,1},{2,14},{6,10},... | collective-permute-start | bytes 2752520 | tf_op jit(solution)/shard_map/ppermute | solution.py:22
  81.8 2.3 %convolution_convert_fusion.4 = bf16[512,896]{1,0:T(8,128)(2,1)S(1)} fusion(bf16[2048,512]{1,0:T(8,128)(2,1)S(1)} %bitcast.151, bf16[2048,896]{1,0:T(8,128)(2,1)S(1)} %bitcast.184), kind=kOutput, calls=%fused_computation.17 | convolution fusion | flops 1879506944 | bytes 6684672 | tf_op jit(solution)/shard_map/dot_general | solution.py:95
  84.2 1.4 %collective-permute-start.28 = (bf16[512,896]{1,0:T(8,128)(2,1)S(1)}, bf16[512,896]{1,0:T(8,128)(2,1)S(1)}, u32[]{:S(2)}, u32[]{:S(2)}) collective-permute-start(bf16[512,896]{1,0:T(8,128)(2,1)S(1)} %convolution_convert_fusion.4), channel_id=1, source_target_pairs={{0,2},{2,0},{1,3},{3,1},{4,6},{6,4},{5,7},{7,5},{8,10},{10,8},{9,1... | collective-permute-start | bytes 2752520 | tf_op jit(solution)/shard_map/ppermute | solution.py:22
  85.6 1.3 %convert_add_fusion.1 = f32[512,896]{1,0:T(8,128)S(1)} fusion(bf16[512,1024]{1,0:T(8,128)(2,1)S(1)} %bitcast.172, bf16[1024,1792]{1,0:T(8,128)(2,1)S(1)} %constant_dynamic-update-slice_fusion, bf16[2,512,896]{2,1,0:T(8,128)(2,1)S(1)} %collective-permute-done.22), kind=kOutput, calls=%fused_computation.8 | convolution fusion | flops 940441600 | bytes 5636096 | tf_op jit(solution)/shard_map/dot_general | solution.py:99
  87.0 1.3 %convert_add_fusion = f32[512,896]{1,0:T(8,128)S(1)} fusion(bf16[512,1024]{1,0:T(8,128)(2,1)S(1)} %bitcast.166, bf16[1024,1792]{1,0:T(8,128)(2,1)S(1)} %constant_dynamic-update-slice_fusion, bf16[2,512,896]{2,1,0:T(8,128)(2,1)S(1)} %collective-permute-done.22), kind=kOutput, calls=%fused_computation.7 | convolution fusion | flops 940441600 | bytes 5636096 | tf_op jit(solution)/shard_map/dot_general | solution.py:99
  88.3 6.8 %collective-permute-done.21 = bf16[512,896]{1,0:T(8,128)(2,1)S(1)} collective-permute-done((bf16[512,896]{1,0:T(8,128)(2,1)S(1)}, bf16[512,896]{1,0:T(8,128)(2,1)S(1)}, u32[]{:S(2)}, u32[]{:S(2)}) %collective-permute-start.21) | collective-permute-done | bytes 917536 | tf_op jit(solution)/shard_map/ppermute | solution.py:22
  95.1 6.7 %collective-permute-done.20 = bf16[2,256,896]{2,1,0:T(8,128)(2,1)S(1)} collective-permute-done((bf16[2,256,896]{2,1,0:T(8,128)(2,1)S(1)}, bf16[2,256,896]{2,1,0:T(8,128)(2,1)S(1)}, u32[]{:S(2)}, u32[]{:S(2)}) %collective-permute-start.20) | collective-permute-done | bytes 917536 | tf_op jit(solution)/shard_map/ppermute | solution.py:22
  101.8 1.5 %collective-permute-done.19 = bf16[2,256,896]{2,1,0:T(8,128)(2,1)S(1)} collective-permute-done((bf16[2,256,896]{2,1,0:T(8,128)(2,1)S(1)}, bf16[2,256,896]{2,1,0:T(8,128)(2,1)S(1)}, u32[]{:S(2)}, u32[]{:S(2)}) %collective-permute-start.19) | collective-permute-done | bytes 917536 | tf_op jit(solution)/shard_map/ppermute | solution.py:22
  104.0 2.1 %collective-permute-start.27 = (bf16[256,896]{1,0:T(8,128)(2,1)S(1)}, bf16[256,896]{1,0:T(8,128)(2,1)S(1)}, u32[]{:S(2)}, u32[]{:S(2)}) collective-permute-start(bf16[256,896]{1,0:T(8,128)(2,1)S(1)} %get-tuple-element.88), channel_id=1, source_target_pairs={{0,12},{4,8},{8,4},{12,0},{1,13},{5,9},{9,5},{13,1},{2,14},{6,10},... | collective-permute-start | bytes 1376264 | tf_op jit(solution)/shard_map/ppermute | solution.py:22
  106.1 2.3 %fusion.24 = f32[512,896]{1,0:T(8,128)S(1)} fusion(bf16[2048,512]{1,0:T(8,128)(2,1)S(1)} %bitcast.147, bf16[2048,896]{1,0:T(8,128)(2,1)S(1)} %bitcast.161), kind=kOutput, calls=%fused_computation.93 | convolution fusion | flops 1879048192 | bytes 7602176 | tf_op jit(solution)/shard_map/dot_general | solution.py:95
  108.5 2.3 %fusion.25 = f32[512,896]{1,0:T(8,128)S(1)} fusion(bf16[2048,512]{1,0:T(8,128)(2,1)S(1)} %bitcast.148, bf16[2048,896]{1,0:T(8,128)(2,1)S(1)} %bitcast.185), kind=kOutput, calls=%fused_computation.94 | convolution fusion | flops 1879048192 | bytes 7602176 | tf_op jit(solution)/shard_map/dot_general | solution.py:95
  111.0 1.5 %collective-permute-done.28 = bf16[512,896]{1,0:T(8,128)(2,1)S(1)} collective-permute-done((bf16[512,896]{1,0:T(8,128)(2,1)S(1)}, bf16[512,896]{1,0:T(8,128)(2,1)S(1)}, u32[]{:S(2)}, u32[]{:S(2)}) %collective-permute-start.28) | collective-permute-done | bytes 917536 | tf_op jit(solution)/shard_map/ppermute | solution.py:22
  112.7 1.4 %pad_maximum_fusion.6 = bf16[512,1792]{1,0:T(8,128)(2,1)} fusion(bf16[512,896]{1,0:T(8,128)(2,1)S(1)} %add_convert_fusion, bf16[512,896]{1,0:T(8,128)(2,1)S(1)} %add_convert_fusion.1), kind=kLoop, calls=%fused_computation.6 | loop fusion | flops 3670016 | bytes 3670016 | tf_op jit(solution)/shard_map/concatenate | solution.py:182
  114.0 1.4 %collective-permute-done.26.far_l = bf16[256,896]{1,0:T(8,128)(2,1)S(1)} collective-permute-done((bf16[256,896]{1,0:T(8,128)(2,1)S(1)}, bf16[256,896]{1,0:T(8,128)(2,1)S(1)}, u32[]{:S(2)}, u32[]{:S(2)}) %collective-permute-start.26) | collective-permute-done | bytes 458784 | tf_op jit(solution)/shard_map/ppermute | solution.py:22
  115.4 1.5 %collective-permute-done.27.far_r = bf16[256,896]{1,0:T(8,128)(2,1)S(1)} collective-permute-done((bf16[256,896]{1,0:T(8,128)(2,1)S(1)}, bf16[256,896]{1,0:T(8,128)(2,1)S(1)}, u32[]{:S(2)}, u32[]{:S(2)}) %collective-permute-start.27) | collective-permute-done | bytes 458784 | tf_op jit(solution)/shard_map/ppermute | solution.py:22
  116.9 1.1 shard_map.52
  (88 shorter events, 14.6 us)
Async XLA Ops:
  0.6 1.0 copy-start.1
  1.7 1.6 %collective-permute-start = (bf16[4,32,1024]{2,1,0:T(8,128)(2,1)S(1)}, bf16[4,32,1024]{2,1,0:T(8,128)(2,1)S(1)}, u32[]{:S(2)}, u32[]{:S(2)}) collective-permute-start(bf16[4,32,1024]{2,1,0:T(8,128)(2,1)S(1)} %get-tuple-element.45), channel_id=1, source_target_pairs={{0,1},{1,0},{2,3},{3,2},{4,5},{5,4},{6,7},{7,6},{8,9},{9,8},{10,11... | collective-permute-start | bytes 786440 | tf_op jit(solution)/shard_map/ppermute | solution.py:22
  3.4 7.8 %collective-permute-start.1 = (bf16[2,32,1024]{2,1,0:T(8,128)(2,1)S(1)}, bf16[2,32,1024]{2,1,0:T(8,128)(2,1)S(1)}, u32[]{:S(2)}, u32[]{:S(2)}) collective-permute-start(bf16[2,32,1024]{2,1,0:T(8,128)(2,1)S(1)} %get-tuple-element.110), channel_id=1, source_target_pairs={{0,4},{4,0},{8,12},{12,8},{1,5},{5,1},{9,13},{13,9},{2,6},{6,2},{1... | collective-permute-start | bytes 393224 | tf_op jit(solution)/shard_map/ppermute | solution.py:22
  5.1 7.8 %collective-permute-start.2 = (bf16[2,32,1024]{2,1,0:T(8,128)(2,1)S(1)}, bf16[2,32,1024]{2,1,0:T(8,128)(2,1)S(1)}, u32[]{:S(2)}, u32[]{:S(2)}) collective-permute-start(bf16[2,32,1024]{2,1,0:T(8,128)(2,1)S(1)} %get-tuple-element.111), channel_id=1, source_target_pairs={{0,12},{4,8},{8,4},{12,0},{1,13},{5,9},{9,5},{13,1},{2,14},{6,10},... | collective-permute-start | bytes 393224 | tf_op jit(solution)/shard_map/ppermute | solution.py:22
  7.3 7.1 %collective-permute-start.3 = (bf16[2,32,1024]{2,1,0:T(8,128)(2,1)S(1)}, bf16[2,32,1024]{2,1,0:T(8,128)(2,1)S(1)}, u32[]{:S(2)}, u32[]{:S(2)}) collective-permute-start(bf16[2,32,1024]{2,1,0:T(8,128)(2,1)S(1)} %get-tuple-element.112), channel_id=1, source_target_pairs={{0,8},{4,12},{8,0},{12,4},{1,9},{5,13},{9,1},{13,5},{2,10},{6,14},... | collective-permute-start | bytes 393224 | tf_op jit(solution)/shard_map/ppermute | solution.py:22
  9.1 8.6 %copy-start.2 = (bf16[512,1792]{1,0:T(8,128)(2,1)S(1)}, bf16[512,1792]{1,0:T(8,128)(2,1)}, u32[]{:S(2)}) copy-start(bf16[512,1792]{1,0:T(8,128)(2,1)} %param.5) | copy-start | bytes 5505028
  9.1 14.7 %collective-permute-start.8 = (bf16[160,1792]{1,0:T(8,128)(2,1)S(1)}, bf16[160,1792]{1,0:T(8,128)(2,1)S(1)}, u32[]{:S(2)}, u32[]{:S(2)}) collective-permute-start(bf16[160,1792]{1,0:T(8,128)(2,1)S(1)} %slice.133), channel_id=1, source_target_pairs={{0,2},{2,0},{1,3},{3,1},{4,6},{6,4},{5,7},{7,5},{8,10},{10,8},{9,1... | collective-permute-start | bytes 1720328 | tf_op jit(solution)/shard_map/ppermute | solution.py:22
  14.6 12.9 %collective-permute-start.5 = (bf16[8,32,512]{2,1,0:T(8,128)(2,1)S(1)}, bf16[8,32,512]{2,1,0:T(8,128)(2,1)S(1)}, u32[]{:S(2)}, u32[]{:S(2)}) collective-permute-start(bf16[8,32,512]{2,1,0:T(8,128)(2,1)S(1)} %get-tuple-element.107), channel_id=1, source_target_pairs={{0,96},{32,64},{64,32},{96,0},{1,97},{33,65},{65,33},{97,1},{2,98}... | collective-permute-start | bytes 786440 | tf_op jit(solution)/shard_map/ppermute | solution.py:22
  17.5 10.1 %collective-permute-start.4 = (bf16[8,32,512]{2,1,0:T(8,128)(2,1)S(1)}, bf16[8,32,512]{2,1,0:T(8,128)(2,1)S(1)}, u32[]{:S(2)}, u32[]{:S(2)}) collective-permute-start(bf16[8,32,512]{2,1,0:T(8,128)(2,1)S(1)} %get-tuple-element.108), channel_id=1, source_target_pairs={{0,32},{32,0},{64,96},{96,64},{1,33},{33,1},{65,97},{97,65},{2,34}... | collective-permute-start | bytes 786440 | tf_op jit(solution)/shard_map/ppermute | solution.py:22
  17.8 1.2 %copy-start = (bf16[256,1792]{1,0:T(8,128)(2,1)S(1)}, bf16[256,1792]{1,0:T(8,128)(2,1)}, u32[]{:S(2)}) copy-start(bf16[256,1792]{1,0:T(8,128)(2,1)} %pre) | copy-start | bytes 2752516
  19.8 12.4 %collective-permute-start.23 = (bf16[256,896]{1,0:T(8,128)(2,1)S(1)}, bf16[256,896]{1,0:T(8,128)(2,1)S(1)}, u32[]{:S(2)}, u32[]{:S(2)}) collective-permute-start(bf16[256,896]{1,0:T(8,128)(2,1)S(1)} %get-tuple-element.71), channel_id=1, source_target_pairs={{0,12},{4,8},{8,4},{12,0},{1,13},{5,9},{9,5},{13,1},{2,14},{6,10},... | collective-permute-start | bytes 1376264 | tf_op jit(solution)/shard_map/ppermute | solution.py:22
  22.1 10.6 %collective-permute-start.14 = (bf16[256,896]{1,0:T(8,128)(2,1)S(1)}, bf16[256,896]{1,0:T(8,128)(2,1)S(1)}, u32[]{:S(2)}, u32[]{:S(2)}) collective-permute-start(bf16[256,896]{1,0:T(8,128)(2,1)S(1)} %get-tuple-element.58), channel_id=1, source_target_pairs={{0,4},{4,0},{8,12},{12,8},{1,5},{5,1},{9,13},{13,9},{2,6},{6,2},{1... | collective-permute-start | bytes 1376264 | tf_op jit(solution)/shard_map/ppermute | solution.py:22
  23.8 14.5 %collective-permute-start.9 = (bf16[8,32,1024]{2,1,0:T(8,128)(2,1)S(1)}, bf16[8,32,1024]{2,1,0:T(8,128)(2,1)S(1)}, u32[]{:S(2)}, u32[]{:S(2)}) collective-permute-start(bf16[8,32,1024]{2,1,0:T(8,128)(2,1)S(1)} %bitcast.153), channel_id=1, source_target_pairs={{0,16},{16,0},{1,17},{17,1},{2,18},{18,2},{3,19},{19,3},{4,20},{20... | collective-permute-start | bytes 1572872 | tf_op jit(solution)/shard_map/ppermute | solution.py:22
  27.6 13.5 %collective-permute-start.6 = (bf16[2,8,32,512]{3,2,1,0:T(8,128)(2,1)S(1)}, bf16[2,8,32,512]{3,2,1,0:T(8,128)(2,1)S(1)}, u32[]{:S(2)}, u32[]{:S(2)}) collective-permute-start(bf16[2,8,32,512]{3,2,1,0:T(8,128)(2,1)S(1)} %pad_maximum_fusion.11), channel_id=1, source_target_pairs={{0,96},{32,64},{64,32},{96,0},{1,97},{33,65},{65,33},{97,1},{2,98}... | collective-permute-start | bytes 1572872 | tf_op jit(solution)/shard_map/ppermute | solution.py:22
  30.5 12.0 %collective-permute-start.7 = (bf16[2,8,32,512]{3,2,1,0:T(8,128)(2,1)S(1)}, bf16[2,8,32,512]{3,2,1,0:T(8,128)(2,1)S(1)}, u32[]{:S(2)}, u32[]{:S(2)}) collective-permute-start(bf16[2,8,32,512]{3,2,1,0:T(8,128)(2,1)S(1)} %pad_maximum_fusion.12), channel_id=1, source_target_pairs={{0,32},{32,0},{64,96},{96,64},{1,33},{33,1},{65,97},{97,65},{2,34}... | collective-permute-start | bytes 1572872 | tf_op jit(solution)/shard_map/ppermute | solution.py:22
  32.3 21.8 %collective-permute-start.24 = (bf16[2,256,896]{2,1,0:T(8,128)(2,1)S(1)}, bf16[2,256,896]{2,1,0:T(8,128)(2,1)S(1)}, u32[]{:S(2)}, u32[]{:S(2)}) collective-permute-start(bf16[2,256,896]{2,1,0:T(8,128)(2,1)S(1)} %pad_maximum_fusion.8), channel_id=1, source_target_pairs={{0,4},{4,0},{8,12},{12,8},{1,5},{5,1},{9,13},{13,9},{2,6},{6,2},{1... | collective-permute-start | bytes 2752520 | tf_op jit(solution)/shard_map/ppermute | solution.py:22
  32.8 21.0 %collective-permute-start.15 = (bf16[2,256,896]{2,1,0:T(8,128)(2,1)S(1)}, bf16[2,256,896]{2,1,0:T(8,128)(2,1)S(1)}, u32[]{:S(2)}, u32[]{:S(2)}) collective-permute-start(bf16[2,256,896]{2,1,0:T(8,128)(2,1)S(1)} %pad_maximum_fusion.7), channel_id=1, source_target_pairs={{0,12},{4,8},{8,4},{12,0},{1,13},{5,9},{9,5},{13,1},{2,14},{6,10},... | collective-permute-start | bytes 2752520 | tf_op jit(solution)/shard_map/ppermute | solution.py:22
  38.4 27.7 %collective-permute-start.17 = (bf16[352,1792]{1,0:T(8,128)(2,1)S(1)}, bf16[352,1792]{1,0:T(8,128)(2,1)S(1)}, u32[]{:S(2)}, u32[]{:S(2)}) collective-permute-start(bf16[352,1792]{1,0:T(8,128)(2,1)S(1)} %slice.145), channel_id=1, source_target_pairs={{0,2},{2,0},{1,3},{3,1},{4,6},{6,4},{5,7},{7,5},{8,10},{10,8},{9,1... | collective-permute-start | bytes 3784712 | tf_op jit(solution)/shard_map/ppermute | solution.py:22
  42.6 7.7 %collective-permute-start.11 = (bf16[8,32,512]{2,1,0:T(8,128)(2,1)S(1)}, bf16[8,32,512]{2,1,0:T(8,128)(2,1)S(1)}, u32[]{:S(2)}, u32[]{:S(2)}) collective-permute-start(bf16[8,32,512]{2,1,0:T(8,128)(2,1)S(1)} %get-tuple-element.99), channel_id=1, source_target_pairs={{0,96},{32,64},{64,32},{96,0},{1,97},{33,65},{65,33},{97,1},{2,98}... | collective-permute-start | bytes 786440 | tf_op jit(solution)/shard_map/ppermute | solution.py:22
  44.1 6.4 %collective-permute-start.10 = (bf16[8,32,512]{2,1,0:T(8,128)(2,1)S(1)}, bf16[8,32,512]{2,1,0:T(8,128)(2,1)S(1)}, u32[]{:S(2)}, u32[]{:S(2)}) collective-permute-start(bf16[8,32,512]{2,1,0:T(8,128)(2,1)S(1)} %get-tuple-element.100), channel_id=1, source_target_pairs={{0,32},{32,0},{64,96},{96,64},{1,33},{33,1},{65,97},{97,65},{2,34}... | collective-permute-start | bytes 786440 | tf_op jit(solution)/shard_map/ppermute | solution.py:22
  50.5 11.9 %collective-permute-start.12 = (bf16[2,8,32,512]{3,2,1,0:T(8,128)(2,1)S(1)}, bf16[2,8,32,512]{3,2,1,0:T(8,128)(2,1)S(1)}, u32[]{:S(2)}, u32[]{:S(2)}) collective-permute-start(bf16[2,8,32,512]{3,2,1,0:T(8,128)(2,1)S(1)} %pad_maximum_fusion.13), channel_id=1, source_target_pairs={{0,96},{32,64},{64,32},{96,0},{1,97},{33,65},{65,33},{97,1},{2,98}... | collective-permute-start | bytes 1572872 | tf_op jit(solution)/shard_map/ppermute | solution.py:22
  52.5 9.7 %collective-permute-start.13 = (bf16[2,8,32,512]{3,2,1,0:T(8,128)(2,1)S(1)}, bf16[2,8,32,512]{3,2,1,0:T(8,128)(2,1)S(1)}, u32[]{:S(2)}, u32[]{:S(2)}) collective-permute-start(bf16[2,8,32,512]{3,2,1,0:T(8,128)(2,1)S(1)} %pad_maximum_fusion.14), channel_id=1, source_target_pairs={{0,32},{32,0},{64,96},{96,64},{1,33},{33,1},{65,97},{97,65},{2,34}... | collective-permute-start | bytes 1572872 | tf_op jit(solution)/shard_map/ppermute | solution.py:22
  54.0 9.0 %collective-permute-start.16 = (bf16[4,256,896]{2,1,0:T(8,128)(2,1)S(1)}, bf16[4,256,896]{2,1,0:T(8,128)(2,1)S(1)}, u32[]{:S(2)}, u32[]{:S(2)}) collective-permute-start(bf16[4,256,896]{2,1,0:T(8,128)(2,1)S(1)} %pad_maximum_fusion.2), channel_id=1, source_target_pairs={{0,1},{1,0},{2,3},{3,2},{4,5},{5,4},{6,7},{7,6},{8,9},{9,8},{10,11... | collective-permute-start | bytes 5505032 | tf_op jit(solution)/shard_map/ppermute | solution.py:22
  55.3 20.7 %collective-permute-start.25 = (bf16[4,256,896]{2,1,0:T(8,128)(2,1)S(1)}, bf16[4,256,896]{2,1,0:T(8,128)(2,1)S(1)}, u32[]{:S(2)}, u32[]{:S(2)}) collective-permute-start(bf16[4,256,896]{2,1,0:T(8,128)(2,1)S(1)} %pad_maximum_fusion.5), channel_id=1, source_target_pairs={{0,1},{1,0},{2,3},{3,2},{4,5},{5,4},{6,7},{7,6},{8,9},{9,8},{10,11... | collective-permute-start | bytes 5505032 | tf_op jit(solution)/shard_map/ppermute | solution.py:22
  69.5 2.0 %copy-start.3 = (bf16[8,256,896]{2,1,0:T(8,128)(2,1)S(1)}, bf16[8,256,896]{2,1,0:T(8,128)(2,1)}, u32[]{:S(2)}) copy-start(bf16[8,256,896]{2,1,0:T(8,128)(2,1)} %get-tuple-element.95) | copy-start | bytes 11010052
  69.7 6.5 %collective-permute-start.18 = (bf16[2,512,896]{2,1,0:T(8,128)(2,1)S(1)}, bf16[2,512,896]{2,1,0:T(8,128)(2,1)S(1)}, u32[]{:S(2)}, u32[]{:S(2)}) collective-permute-start(bf16[2,512,896]{2,1,0:T(8,128)(2,1)S(1)} %pad_maximum_fusion.3), channel_id=1, source_target_pairs={{0,1},{1,0},{2,3},{3,2},{4,5},{5,4},{6,7},{7,6},{8,9},{9,8},{10,11... | collective-permute-start | bytes 5505032 | tf_op jit(solution)/shard_map/ppermute | solution.py:22
  71.7 23.4 %collective-permute-start.21 = (bf16[512,896]{1,0:T(8,128)(2,1)S(1)}, bf16[512,896]{1,0:T(8,128)(2,1)S(1)}, u32[]{:S(2)}, u32[]{:S(2)}) collective-permute-start(bf16[512,896]{1,0:T(8,128)(2,1)S(1)} %convolution_convert_fusion.5), channel_id=1, source_target_pairs={{0,2},{2,0},{1,3},{3,1},{4,6},{6,4},{5,7},{7,5},{8,10},{10,8},{9,1... | collective-permute-start | bytes 2752520 | tf_op jit(solution)/shard_map/ppermute | solution.py:22
  75.6 10.0 %collective-permute-start.22 = (bf16[2,512,896]{2,1,0:T(8,128)(2,1)S(1)}, bf16[2,512,896]{2,1,0:T(8,128)(2,1)S(1)}, u32[]{:S(2)}, u32[]{:S(2)}) collective-permute-start(bf16[2,512,896]{2,1,0:T(8,128)(2,1)S(1)} %pad_maximum_fusion.4), channel_id=1, source_target_pairs={{0,1},{1,0},{2,3},{3,2},{4,5},{5,4},{6,7},{7,6},{8,9},{9,8},{10,11... | collective-permute-start | bytes 5505032 | tf_op jit(solution)/shard_map/ppermute | solution.py:22
  79.0 22.8 %collective-permute-start.20 = (bf16[2,256,896]{2,1,0:T(8,128)(2,1)S(1)}, bf16[2,256,896]{2,1,0:T(8,128)(2,1)S(1)}, u32[]{:S(2)}, u32[]{:S(2)}) collective-permute-start(bf16[2,256,896]{2,1,0:T(8,128)(2,1)S(1)} %bitcast.187), channel_id=1, source_target_pairs={{0,4},{4,0},{8,12},{12,8},{1,5},{5,1},{9,13},{13,9},{2,6},{6,2},{1... | collective-permute-start | bytes 2752520 | tf_op jit(solution)/shard_map/ppermute | solution.py:22
  79.7 23.7 %collective-permute-start.19 = (bf16[2,256,896]{2,1,0:T(8,128)(2,1)S(1)}, bf16[2,256,896]{2,1,0:T(8,128)(2,1)S(1)}, u32[]{:S(2)}, u32[]{:S(2)}) collective-permute-start(bf16[2,256,896]{2,1,0:T(8,128)(2,1)S(1)} %bitcast.186), channel_id=1, source_target_pairs={{0,12},{4,8},{8,4},{12,0},{1,13},{5,9},{9,5},{13,1},{2,14},{6,10},... | collective-permute-start | bytes 2752520 | tf_op jit(solution)/shard_map/ppermute | solution.py:22
  84.2 28.2 %collective-permute-start.28 = (bf16[512,896]{1,0:T(8,128)(2,1)S(1)}, bf16[512,896]{1,0:T(8,128)(2,1)S(1)}, u32[]{:S(2)}, u32[]{:S(2)}) collective-permute-start(bf16[512,896]{1,0:T(8,128)(2,1)S(1)} %convolution_convert_fusion.4), channel_id=1, source_target_pairs={{0,2},{2,0},{1,3},{3,1},{4,6},{6,4},{5,7},{7,5},{8,10},{10,8},{9,1... | collective-permute-start | bytes 2752520 | tf_op jit(solution)/shard_map/ppermute | solution.py:22
  103.5 11.9 %collective-permute-start.26 = (bf16[256,896]{1,0:T(8,128)(2,1)S(1)}, bf16[256,896]{1,0:T(8,128)(2,1)S(1)}, u32[]{:S(2)}, u32[]{:S(2)}) collective-permute-start(bf16[256,896]{1,0:T(8,128)(2,1)S(1)} %get-tuple-element.90), channel_id=1, source_target_pairs={{0,4},{4,0},{8,12},{12,8},{1,5},{5,1},{9,13},{13,9},{2,6},{6,2},{1... | collective-permute-start | bytes 1376264 | tf_op jit(solution)/shard_map/ppermute | solution.py:22
  104.0 12.9 %collective-permute-start.27 = (bf16[256,896]{1,0:T(8,128)(2,1)S(1)}, bf16[256,896]{1,0:T(8,128)(2,1)S(1)}, u32[]{:S(2)}, u32[]{:S(2)}) collective-permute-start(bf16[256,896]{1,0:T(8,128)(2,1)S(1)} %get-tuple-element.88), channel_id=1, source_target_pairs={{0,12},{4,8},{8,4},{12,0},{1,13},{5,9},{9,5},{13,1},{2,14},{6,10},... | collective-permute-start | bytes 1376264 | tf_op jit(solution)/shard_map/ppermute | solution.py:22
